TPU v7x, 32 devices: a whole 2x2x4 slice. The times are simulated.
32 devices in a mesh: page: 16 (over z, y, x), seq: 2 (over core).
Axes of the slice: x: 2, y: 2, z: 4, core: 2. Of those that a mesh axis runs over, the one named last changes fastest.
Arguments:
- hidden: bfloat16 [32, 512, 768], P('page', 'seq'), may hold values from -6 to 6
- lengths: int32 [32], P('page'), may hold values from 64 to 512, as said below
- w_query: bfloat16 [768, 768], P(('page', 'seq')), may hold values from -0.21875 to 0.21875
- w_key: bfloat16 [768, 768], P(('page', 'seq')), may hold values from -0.21875 to 0.21875
- w_value: bfloat16 [768, 768], P(('page', 'seq')), may hold values from -0.21875 to 0.21875
- w_output: bfloat16 [768, 768], P(('page', 'seq')), may hold values from -0.625 to 0.625
- b_query: bfloat16 [768], P(('page', 'seq')), may hold values from -3 to 3
- b_value: bfloat16 [768], P(('page', 'seq')), may hold values from -3 to 3
- b_output: bfloat16 [768], P(('page', 'seq')), may hold values from -3 to 3
- attn_gain: bfloat16 [768], P(('page', 'seq')), may hold values from 0.5 to 1.5
- attn_shift: bfloat16 [768], P(('page', 'seq')), may hold values from -3 to 3
- w_inner: bfloat16 [768, 3072], P(('page', 'seq')), may hold values from -0.21875 to 0.21875
- b_inner: bfloat16 [3072], P(('page', 'seq')), may hold values from -3 to 3
- w_outer: bfloat16 [3072, 768], P(('page', 'seq')), may hold values from -0.109375 to 0.109375
- b_outer: bfloat16 [768], P(('page', 'seq')), may hold values from -3 to 3
- ffn_gain: bfloat16 [768], P(('page', 'seq')), may hold values from 0.5 to 1.5
- ffn_shift: bfloat16 [768], P(('page', 'seq')), may hold values from -3 to 3
- cotangent: bfloat16 [32, 512, 768], P('page', 'seq'), may hold values from -6 to 6
Outputs:
- layer_out: bfloat16 [32, 512, 768], P('page', 'seq')
- hidden_grad: bfloat16 [32, 512, 768], P('page', 'seq')
- query_w_grad: float32 [768, 768], P(('page', 'seq'))
- key_w_grad: float32 [768, 768], P(('page', 'seq'))
- value_w_grad: float32 [768, 768], P(('page', 'seq'))
- output_w_grad: float32 [768, 768], P(('page', 'seq'))
- query_b_grad: float32 [768], P(('page', 'seq'))
- value_b_grad: float32 [768], P(('page', 'seq'))
- output_b_grad: float32 [768], P(('page', 'seq'))
- attn_gain_grad: float32 [768], P(('page', 'seq'))
- attn_shift_grad: float32 [768], P(('page', 'seq'))
- inner_w_grad: float32 [768, 3072], P(('page', 'seq'))
- inner_b_grad: float32 [3072], P(('page', 'seq'))
- outer_w_grad: float32 [3072, 768], P(('page', 'seq'))
- outer_b_grad: float32 [768], P(('page', 'seq'))
- ffn_gain_grad: float32 [768], P(('page', 'seq'))
- ffn_shift_grad: float32 [768], P(('page', 'seq'))
Inputs may be any that keep to these rules, and one draw needn't show every extreme that they name: `lengths`: positions below a page's count hold real tokens and the rest are padding; some page is full and some has 64 real tokens.
All inputs are finite; a program needn't handle non-finite values.
Results may differ from a plain program's by a relative error of at most 0.018.
Values may be sent and summed in bfloat16 or wider, within the bound.
A program may use at most 192 MiB of HBM per device.

v0:
```python
import jax
import jax.numpy as jnp
from jax import lax
from jax.sharding import PartitionSpec as P

HEADS = 12


masked_value = -1e30
norm_eps = 1e-06


def layer_norm(values, norm_gain, norm_shift):
    centre = jnp.mean(values, axis=-1, keepdims=True)
    centered = values - centre
    spread = jnp.mean(centered * centered, axis=-1, keepdims=True)
    return centered * lax.rsqrt(spread + norm_eps) * norm_gain + norm_shift


def gelu_exact(values):
    return jax.nn.gelu(values, approximate=False)


def matmul(left_side, right_side):
    return jnp.dot(left_side, right_side, preferred_element_type=jnp.float32)


def column_sum(values):
    return jnp.sum(values.astype(jnp.float32), axis=0)


def usable_keys(page_lengths, seg_len):
    places = lax.broadcasted_iota(jnp.int32, (page_lengths.shape[0], seg_len), 1)
    return places < page_lengths[:, None]


def head_split(values, head_count):
    return values.reshape(
        values.shape[0], values.shape[1], head_count, values.shape[2] // head_count
    )


def page_scores(query_heads, key_piece, usable, score_scale):
    key_heads = head_split(key_piece, query_heads.shape[2])
    scores = (
        jnp.einsum("pqhd,pkhd->phqk", query_heads, key_heads, preferred_element_type=jnp.float32)
        * score_scale
    )
    return jnp.where(usable[:, None, None, :], scores, masked_value)


def per_device(
    hidden,
    lengths,
    w_query,
    w_key,
    w_value,
    w_output,
    b_query,
    b_value,
    b_output,
    attn_gain,
    attn_shift,
    w_inner,
    b_inner,
    w_outer,
    b_outer,
    ffn_gain,
    ffn_shift,
    cotangent,
):
    model_width = hidden.shape[2]
    head_count = HEADS
    score_scale = (model_width // head_count) ** (-0.5)
    f32 = jnp.float32
    bf16 = jnp.bfloat16
    work_hidden, work_cot = (hidden, cotangent)
    local_pages, local_tokens = (work_hidden.shape[0], work_hidden.shape[1])
    row_count = local_pages * local_tokens
    (
        query_full,
        key_full,
        value_full,
        output_full,
        query_bias,
        value_bias,
        output_bias,
        gain_one,
        shift_one,
    ) = (
        lax.all_gather(w_query, ("page", "seq"), axis=0, tiled=True),
        lax.all_gather(w_key, ("page", "seq"), axis=0, tiled=True),
        lax.all_gather(w_value, ("page", "seq"), axis=0, tiled=True),
        lax.all_gather(w_output, ("page", "seq"), axis=0, tiled=True),
        lax.all_gather(b_query, ("page", "seq"), axis=0, tiled=True),
        lax.all_gather(b_value, ("page", "seq"), axis=0, tiled=True),
        lax.all_gather(b_output, ("page", "seq"), axis=0, tiled=True),
        lax.all_gather(attn_gain, ("page", "seq"), axis=0, tiled=True),
        lax.all_gather(attn_shift, ("page", "seq"), axis=0, tiled=True),
    )
    flat_rows = work_hidden.reshape(row_count, model_width)
    queries = (matmul(flat_rows, query_full) + query_bias.astype(f32)).astype(bf16)
    key_rows = matmul(flat_rows, key_full).astype(bf16)
    value_rows = (matmul(flat_rows, value_full) + value_bias.astype(f32)).astype(bf16)
    query_heads = head_split(queries.reshape(local_pages, local_tokens, model_width), head_count)
    key_pages = key_rows.reshape(local_pages, local_tokens, model_width)
    value_pages = value_rows.reshape(local_pages, local_tokens, model_width)
    stat_shape = (local_pages, head_count, local_tokens)
    stat_start = (jnp.full(stat_shape, masked_value, f32), jnp.zeros(stat_shape, f32))
    key_piece = lax.all_gather(key_pages, "seq", axis=1, tiled=True)
    usable = usable_keys(lengths, key_piece.shape[1])

    def merged():
        run_peak, run_total = stat_start
        scores = page_scores(query_heads, key_piece, usable, score_scale)
        new_peak = jnp.maximum(run_peak, jnp.max(scores, axis=-1))
        summed = jnp.sum(jnp.exp(scores - new_peak[..., None]), axis=-1)
        return (new_peak, summed)

    run_peak, run_total = merged()
    log_norm = run_peak + jnp.log(run_total)
    add_key_piece = lax.all_gather(key_pages, "seq", axis=1, tiled=True)
    value_piece = lax.all_gather(value_pages, "seq", axis=1, tiled=True)
    add_usable = usable_keys(lengths, add_key_piece.shape[1])

    def merged():
        scores = page_scores(query_heads, add_key_piece, add_usable, score_scale)
        attn_probs = jnp.exp(scores - log_norm[..., None]).astype(bf16)
        addend = jnp.einsum(
            "phqk,pkhd->pqhd",
            attn_probs,
            head_split(value_piece, head_count),
            preferred_element_type=f32,
        )
        return addend.reshape(local_pages, local_tokens, model_width)

    context = merged()
    context_low = context.astype(bf16).reshape(row_count, model_width)
    residual_one = (
        flat_rows.astype(f32) + matmul(context_low, output_full) + output_bias.astype(f32)
    )
    normed_one, pull_one = jax.vjp(
        layer_norm, residual_one, gain_one.astype(f32), shift_one.astype(f32)
    )
    inner_full, outer_full, inner_bias, outer_bias, gain_two, shift_two = (
        lax.all_gather(w_inner, ("page", "seq"), axis=0, tiled=True),
        lax.all_gather(w_outer, ("page", "seq"), axis=0, tiled=True),
        lax.all_gather(b_inner, ("page", "seq"), axis=0, tiled=True),
        lax.all_gather(b_outer, ("page", "seq"), axis=0, tiled=True),
        lax.all_gather(ffn_gain, ("page", "seq"), axis=0, tiled=True),
        lax.all_gather(ffn_shift, ("page", "seq"), axis=0, tiled=True),
    )
    normed_low = normed_one.astype(bf16)
    pre_gelu = matmul(normed_low, inner_full) + inner_bias.astype(f32)
    post_gelu, pull_gelu = jax.vjp(gelu_exact, pre_gelu)
    post_low = post_gelu.astype(bf16)
    residual_two = normed_one + matmul(post_low, outer_full) + outer_bias.astype(f32)
    layer_out, pull_two = jax.vjp(
        layer_norm, residual_two, gain_two.astype(f32), shift_two.astype(f32)
    )
    cot_rows = work_cot.reshape(row_count, model_width).astype(f32)
    d_res_two, gain_two_grad, shift_two_grad = pull_two(cot_rows)
    d_outer = d_res_two.astype(bf16)
    outer_w_grad = matmul(post_low.T, d_outer)
    outer_b_grad = column_sum(d_outer)
    (d_pre_full,) = pull_gelu(matmul(d_outer, outer_full.T))
    d_pre = d_pre_full.astype(bf16)
    inner_w_grad = matmul(normed_low.T, d_pre)
    inner_b_grad = column_sum(d_pre)
    d_normed = d_res_two + matmul(d_pre, inner_full.T)
    d_res_one, gain_one_grad, shift_one_grad = pull_one(d_normed)
    ffn_owned = (
        lax.psum_scatter(inner_w_grad, ("page", "seq"), scatter_dimension=0, tiled=True),
        lax.psum_scatter(outer_w_grad, ("page", "seq"), scatter_dimension=0, tiled=True),
        lax.psum_scatter(inner_b_grad, ("page", "seq"), scatter_dimension=0, tiled=True),
        lax.psum_scatter(outer_b_grad, ("page", "seq"), scatter_dimension=0, tiled=True),
        lax.psum_scatter(gain_two_grad, ("page", "seq"), scatter_dimension=0, tiled=True),
        lax.psum_scatter(shift_two_grad, ("page", "seq"), scatter_dimension=0, tiled=True),
    )
    d_attn = d_res_one.astype(bf16)
    output_w_grad = matmul(context_low.T, d_attn)
    output_b_grad = column_sum(d_attn)
    d_context = matmul(d_attn, output_full.T).astype(bf16)
    d_context_heads = head_split(
        d_context.reshape(local_pages, local_tokens, model_width), head_count
    )
    context_heads = head_split(context, head_count)
    row_delta = jnp.transpose(
        jnp.sum(d_context_heads.astype(f32) * context_heads, axis=-1), (0, 2, 1)
    )

    def add_grads(segment):
        key_piece, value_piece = segment
        seg_len = key_piece.shape[1]
        usable = usable_keys(lengths, seg_len)

        def merged():
            scores = page_scores(query_heads, key_piece, usable, score_scale)
            attn_probs = jnp.exp(scores - log_norm[..., None])
            key_heads = head_split(key_piece, head_count)
            value_heads = head_split(value_piece, head_count)
            d_probs = jnp.einsum(
                "pqhd,pkhd->phqk", d_context_heads, value_heads, preferred_element_type=f32
            )
            d_scores = (attn_probs * (d_probs - row_delta[..., None])).astype(bf16)
            query_part = jnp.einsum(
                "phqk,pkhd->pqhd", d_scores, key_heads, preferred_element_type=f32
            )
            key_part = jnp.einsum(
                "phqk,pqhd->pkhd", d_scores, query_heads, preferred_element_type=f32
            )
            value_part = jnp.einsum(
                "phqk,pqhd->pkhd",
                attn_probs.astype(bf16),
                d_context_heads,
                preferred_element_type=f32,
            )
            query_grad = query_part.reshape(local_pages, local_tokens, model_width) * score_scale
            key_grads = key_part.reshape(local_pages, seg_len, model_width) * score_scale
            value_grads = value_part.reshape(local_pages, seg_len, model_width)
            return (query_grad, key_grads, value_grads)

        return merged()

    query_grad, key_grads, value_grads = add_grads(
        (
            lax.all_gather(key_pages, "seq", axis=1, tiled=True),
            lax.all_gather(value_pages, "seq", axis=1, tiled=True),
        )
    )
    key_owned, value_owned = (
        lax.psum_scatter(
            key_grads.astype(jnp.bfloat16), "seq", scatter_dimension=1, tiled=True
        ).astype(jnp.float32),
        lax.psum_scatter(
            value_grads.astype(jnp.bfloat16), "seq", scatter_dimension=1, tiled=True
        ).astype(jnp.float32),
    )
    d_queries = query_grad.astype(bf16).reshape(row_count, model_width)
    d_keys = key_owned.astype(bf16).reshape(row_count, model_width)
    d_values = value_owned.astype(bf16).reshape(row_count, model_width)
    query_w_grad = matmul(flat_rows.T, d_queries)
    key_w_grad = matmul(flat_rows.T, d_keys)
    value_w_grad = matmul(flat_rows.T, d_values)
    query_b_grad = column_sum(d_queries)
    value_b_grad = column_sum(d_values)
    hidden_grad = (
        d_res_one
        + matmul(d_queries, query_full.T)
        + matmul(d_keys, key_full.T)
        + matmul(d_values, value_full.T)
    ).astype(bf16)
    attn_owned = (
        lax.psum_scatter(query_w_grad, ("page", "seq"), scatter_dimension=0, tiled=True),
        lax.psum_scatter(key_w_grad, ("page", "seq"), scatter_dimension=0, tiled=True),
        lax.psum_scatter(value_w_grad, ("page", "seq"), scatter_dimension=0, tiled=True),
        lax.psum_scatter(output_w_grad, ("page", "seq"), scatter_dimension=0, tiled=True),
        lax.psum_scatter(query_b_grad, ("page", "seq"), scatter_dimension=0, tiled=True),
        lax.psum_scatter(value_b_grad, ("page", "seq"), scatter_dimension=0, tiled=True),
        lax.psum_scatter(output_b_grad, ("page", "seq"), scatter_dimension=0, tiled=True),
        lax.psum_scatter(gain_one_grad, ("page", "seq"), scatter_dimension=0, tiled=True),
        lax.psum_scatter(shift_one_grad, ("page", "seq"), scatter_dimension=0, tiled=True),
    )
    out_pages = layer_out.astype(bf16).reshape(local_pages, local_tokens, model_width)
    grad_pages = hidden_grad.reshape(local_pages, local_tokens, model_width)
    return (
        out_pages,
        grad_pages,
        attn_owned[0],
        attn_owned[1],
        attn_owned[2],
        attn_owned[3],
        attn_owned[4],
        attn_owned[5],
        attn_owned[6],
        attn_owned[7],
        attn_owned[8],
        ffn_owned[0],
        ffn_owned[2],
        ffn_owned[1],
        ffn_owned[3],
        ffn_owned[4],
        ffn_owned[5],
    )


def solution(mesh):
    in_specs = (
        P("page", "seq", None),
        P("page"),
        P(("page", "seq"), None),
        P(("page", "seq"), None),
        P(("page", "seq"), None),
        P(("page", "seq"), None),
        P(("page", "seq")),
        P(("page", "seq")),
        P(("page", "seq")),
        P(("page", "seq")),
        P(("page", "seq")),
        P(("page", "seq"), None),
        P(("page", "seq")),
        P(("page", "seq"), None),
        P(("page", "seq")),
        P(("page", "seq")),
        P(("page", "seq")),
        P("page", "seq", None),
    )
    out_specs = (
        P("page", "seq", None),
        P("page", "seq", None),
        P(("page", "seq"), None),
        P(("page", "seq"), None),
        P(("page", "seq"), None),
        P(("page", "seq"), None),
        P(("page", "seq")),
        P(("page", "seq")),
        P(("page", "seq")),
        P(("page", "seq")),
        P(("page", "seq")),
        P(("page", "seq"), None),
        P(("page", "seq")),
        P(("page", "seq"), None),
        P(("page", "seq")),
        P(("page", "seq")),
        P(("page", "seq")),
    )
    return jax.shard_map(
        per_device, mesh=mesh, in_specs=in_specs, out_specs=out_specs, check_vma=False
    )
```

profile of v0, /device:TPU:0, one launch (start us, length us, event | category | flops | bytes accessed | tf_op | source)
XLA Modules:
  0.0 1169.5 jit_solution(16663596713661625190)
XLA Ops:
  17.0 42.4 %all-reduce.19 = (bf16[768]{0:T(1024)(128)(2,1)S(1)}, bf16[768]{0:T(1024)(128)(2,1)S(1)}, bf16[768]{0:T(1024)(128)(2,1)S(1)}, bf16[768]{0:T(1024)(128)(2,1)S(1)}...) all-reduce(bf16[768]{0:T(1024)(128)(2,1)S(1)} %dynamic-update-slice, ...), channel_id=1, replica_groups=mesh['page'=16,'seq'=2] {'page','seq'}, use_global_device_ids=true, to_apply=%add | all-reduce | flops 9216 | bytes 36864
  59.4 8.6 all-gather.9.cloned.1.call-done
  68.1 3.2 add_convert_fusion.4
  71.3 52.5 %all-gather.15.cloned.1.call-done = bf16[768,768]{1,0:T(8,128)(2,1)} async-done(((bf16[24,768]{1,0:T(8,128)(2,1)}), bf16[768,768]{1,0:T(8,128)(2,1)}) %all-gather.15.cloned.1.call-update) | async-done | bytes 1179664 | tf_op jit(solution)/shard_map/all_gather | solution.py:92
  123.8 2.9 convolution_convert_fusion.2
  129.0 50.7 %all-gather.13.cloned.1.call-done = bf16[768,768]{1,0:T(8,128)(2,1)} async-done(((bf16[24,768]{1,0:T(8,128)(2,1)}), bf16[768,768]{1,0:T(8,128)(2,1)}) %all-gather.13.cloned.1.call-update) | async-done | bytes 1179664 | tf_op jit(solution)/shard_map/all_gather | solution.py:91
  182.2 8.2 all-gather.11.cloned.1.call-done
  190.4 3.1 copy.60
  193.5 9.9 all-gather.17.cloned.1.call-done
  205.1 2.3 fusion.1
  207.5 3.2 exponential_reduce_fusion
  212.2 4.3 bitcast_convert_fusion
  218.3 43.1 %all-gather.19.cloned.1.call-done = bf16[768,768]{1,0:T(8,128)(2,1)} async-done(((bf16[24,768]{1,0:T(8,128)(2,1)}), bf16[768,768]{1,0:T(8,128)(2,1)}) %all-gather.19.cloned.1.call-update) | async-done | bytes 1179664 | tf_op jit(solution)/shard_map/all_gather | solution.py:94
  261.4 2.6 fusion.35
  264.4 62.5 %all-gather.21.cloned.1.call-done = bf16[768,3072]{1,0:T(8,128)(2,1)} async-done(((bf16[24,3072]{1,0:T(8,128)(2,1)}), bf16[768,3072]{1,0:T(8,128)(2,1)}) %all-gather.21.cloned.1.call-update) | async-done | bytes 4718608 | tf_op jit(solution)/shard_map/all_gather | solution.py:146
  326.9 19.8 %multiply_convert_fusion.1 = (bf16[512,3072]{1,0:T(8,128)(2,1)}, f32[512,3072]{1,0:T(8,128)}, f32[512,3072]{1,0:T(8,128)}) fusion(f32[3072]{0:T(1024)S(1)} %convert_element_type.158, bf16[768,3072]{1,0:T(8,128)(2,1)} %all-gather.21.cloned.1.call-done, f32[512,768]{1,0:T(8,128)S(1)} %get-tuple-element.109, f32[768]{0:T(1024)S(1)} %convert_element_type.156, ...), kind=kOutput, calls=%fused_computation.10 | convolution fusion | flops 2521694208 | bytes 22042624 | tf_op jit(solution)/shard_map/dot_general | solution.py:25
  346.7 45.6 %all-gather.23.cloned.1.call-done = bf16[3072,768]{1,0:T(8,128)(2,1)} async-done(((bf16[96,768]{1,0:T(8,128)(2,1)}), bf16[3072,768]{1,0:T(8,128)(2,1)}) %all-gather.23.cloned.1.call-update) | async-done | bytes 4718608 | tf_op jit(solution)/shard_map/all_gather | solution.py:147
  392.3 6.1 fusion.36
  402.1 8.2 convert_reduce_fusion
  410.4 3.2 multiply_reduce_fusion
  413.6 2.1 fusion.32
  418.6 2.3 copy.65
  420.9 2.9 reshape_reshape.7
  425.7 8.1 multiply_convert_fusion
  433.8 2.7 multiply_convert_fusion.2
  436.8 2.6 copy.70
  439.5 8.7 convolution_convert_fusion
  448.1 2.6 copy.72
  450.8 4.9 convert_reduce_fusion.5
  456.7 2.2 convolution_bitcast_fusion.2
  458.9 3.3 copy.80
  462.3 2.2 fusion.39
  464.6 3.6 convolution_bitcast_fusion.1
  468.2 3.2 copy.82
  471.5 3.4 convolution_bitcast_fusion
  474.9 3.2 copy.84
  478.2 7.5 fusion.28
  486.8 8.2 fusion.40
  497.5 3.3 fusion.37
  501.0 40.6 %all-reduce.18 = (f32[768]{0:T(1024)S(1)}, f32[768]{0:T(1024)S(1)}, f32[768]{0:T(1024)S(1)}, f32[768]{0:T(1024)S(1)}, f32[768]{0:T(1024)S(1)}, /*index=5*/f32[30...) all-reduce(f32[768]{0:T(1024)S(1)} %reduce_sum.216, ...), channel_id=8, replica_groups=mesh['page'=16,'seq'=2] {'page','seq'}, use_global_device_ids=true, to_apply=%region_18.19.clone | all-reduce | flops 9216 | bytes 73728
  546.9 2.3 fusion.38
  549.2 3.1 add_convert_fusion.1
  552.3 14.1 %reduce-scatter.25.cloned.1.call-done = f32[24,768]{1,0:T(8,128)} async-done(((f32[768,768]{1,0:T(8,128)}), f32[24,768]{1,0:T(8,128)}) %reduce-scatter.25.cloned.1.call-update) | async-done | bytes 73744
  566.4 104.7 %reduce-scatter.19.cloned.1.call-done = f32[24,768]{1,0:T(8,128)} async-done(((f32[768,768]{1,0:T(8,128)}), f32[24,768]{1,0:T(8,128)}) %reduce-scatter.19.cloned.1.call-update) | async-done | bytes 73744 | tf_op jit(solution)/shard_map/reduce_scatter | solution.py:257
  671.0 103.9 %reduce-scatter.27.cloned.1.call-done = f32[24,768]{1,0:T(8,128)} async-done(((f32[768,768]{1,0:T(8,128)}), f32[24,768]{1,0:T(8,128)}) %reduce-scatter.27.cloned.1.call-update) | async-done | bytes 73744
  775.0 104.6 %reduce-scatter.29.cloned.1.call-done = f32[24,768]{1,0:T(8,128)} async-done(((f32[768,768]{1,0:T(8,128)}), f32[24,768]{1,0:T(8,128)}) %reduce-scatter.29.cloned.1.call-update) | async-done | bytes 73744
  879.6 141.0 %reduce-scatter.21.cloned.1.call-done = f32[24,3072]{1,0:T(8,128)} async-done(((f32[768,3072]{1,0:T(8,128)}), f32[24,3072]{1,0:T(8,128)}) %reduce-scatter.21.cloned.1.call-update) | async-done | bytes 294928 | tf_op jit(solution)/shard_map/reduce_scatter | solution.py:173
  1020.6 142.0 %reduce-scatter.23.cloned.1.call-done = f32[96,768]{1,0:T(8,128)} async-done(((f32[3072,768]{1,0:T(8,128)}), f32[96,768]{1,0:T(8,128)}) %reduce-scatter.23.cloned.1.call-update) | async-done | bytes 294928 | tf_op jit(solution)/shard_map/reduce_scatter | solution.py:174
  (155 shorter events, 38.9 us)
Async XLA Ops:
  7.2 116.6 %copy-start.18 = (bf16[2,256,768]{2,1,0:T(8,128)(2,1)S(1)}, bf16[2,256,768]{2,1,0:T(8,128)(2,1)}, u32[]{:S(2)}) copy-start(bf16[2,256,768]{2,1,0:T(8,128)(2,1)} %param.18) | copy-start | bytes 2359300
  7.2 60.9 %all-gather.9.cloned.1.call-start = ((), (), s32[]{:S(2)}) async-start(), calls=%async_computation.8 | async-start | bytes 1216512 | tf_op jit(solution)/shard_map/all_gather | solution.py:93
  7.9 115.9 %all-gather.15.cloned.1.call-start = ((), (), s32[]{:S(2)}) async-start(), calls=%async_computation.11 | async-start | bytes 1216512 | tf_op jit(solution)/shard_map/all_gather | solution.py:92
  8.7 171.0 %all-gather.13.cloned.1.call-start = ((), (), s32[]{:S(2)}) async-start(), calls=%async_computation.10 | async-start | bytes 1216512 | tf_op jit(solution)/shard_map/all_gather | solution.py:91
  9.4 181.0 %all-gather.11.cloned.1.call-start = ((), (), s32[]{:S(2)}) async-start(), calls=%async_computation.9 | async-start | bytes 2359296 | tf_op jit(solution)/shard_map/all_gather | solution.py:123
  71.2 57.7 %copy-start.21 = (s32[2]{0:T(128)S(1)}, s32[2]{0:T(128)}, u32[]{:S(2)}) copy-start(s32[2]{0:T(128)} %param.19) | copy-start | bytes 28
  71.3 132.1 %all-gather.17.cloned.1.call-start = ((), (), s32[]{:S(2)}) async-start(), calls=%async_computation.12 | async-start | bytes 2359296 | tf_op jit(solution)/shard_map/all_gather | solution.py:122
  126.7 134.7 %all-gather.19.cloned.1.call-start = ((), (), s32[]{:S(2)}) async-start(), calls=%async_computation.13 | async-start | bytes 1216512 | tf_op jit(solution)/shard_map/all_gather | solution.py:94
  127.3 199.6 %all-gather.21.cloned.1.call-start = ((), (), s32[]{:S(2)}) async-start(), calls=%async_computation.14 | async-start | bytes 4866048 | tf_op jit(solution)/shard_map/all_gather | solution.py:146
  128.1 264.2 %all-gather.23.cloned.1.call-start = ((), (), s32[]{:S(2)}) async-start(), calls=%async_computation.15 | async-start | bytes 4866048 | tf_op jit(solution)/shard_map/all_gather | solution.py:147
  128.8 335.8 %reduce-scatter.15.cloned.1.call-start = ((), (), s32[]{:S(2)}) async-start(), calls=%async_computation.16 | async-start | bytes 2359296 | tf_op jit(solution)/shard_map/reduce_scatter | solution.py:232
  182.2 22.9 %copy-start.2 = (bf16[2,256,12,64]{1,0,3,2:T(2,128)(2,1)}, bf16[2,256,12,64]{1,0,3,2:T(2,128)(2,1)S(1)}, u32[]{:S(2)}) copy-start(bf16[2,256,12,64]{1,0,3,2:T(2,128)(2,1)S(1)} %reshape_reshape.6) | copy-start | bytes 2359300
  207.4 4.7 copy-start
  207.4 4.7 copy-start.14
  264.0 146.4 %copy-start.8 = (f32[512,768]{1,0:T(8,128)}, f32[512,768]{1,0:T(8,128)S(1)}, u32[]{:S(2)}) copy-start(f32[512,768]{1,0:T(8,128)S(1)} %get-tuple-element.109) | copy-start | bytes 4718596
  392.3 6.4 copy-start.4
  399.5 2.6 copy-start.22
  401.1 9.3 slice-start
  401.3 9.0 copy-start.16
  402.1 8.3 slice-start.1
  410.4 3.2 copy-start.24
  413.6 3.2 copy-start.23
  416.0 0.9 copy-start.12
  425.7 8.1 copy-start.3
  433.8 3.1 copy-start.1
  439.4 32.1 %reduce-scatter.17.cloned.1.call-start = ((), (), s32[]{:S(2)}) async-start(), calls=%async_computation.17 | async-start | bytes 2359296 | tf_op jit(solution)/shard_map/reduce_scatter | solution.py:235
  450.8 115.6 %reduce-scatter.25.cloned.1.call-start = ((), (), s32[]{:S(2)}) async-start(), calls=%async_computation.21 | async-start | bytes 2433024
  450.8 5.9 copy-start.19
  455.8 0.9 copy-start.6
  458.9 3.3 copy-start.11
  458.9 3.3 copy-start.13
  462.2 208.8 %reduce-scatter.19.cloned.1.call-start = ((), (), s32[]{:S(2)}) async-start(), calls=%async_computation.18 | async-start | bytes 2433024 | tf_op jit(solution)/shard_map/reduce_scatter | solution.py:257
  464.5 310.4 %reduce-scatter.27.cloned.1.call-start = ((), (), s32[]{:S(2)}) async-start(), calls=%async_computation.22 | async-start | bytes 2433024
  468.2 3.3 copy-start.20
  471.4 408.1 %reduce-scatter.29.cloned.1.call-start = ((), (), s32[]{:S(2)}) async-start(), calls=%async_computation.23 | async-start | bytes 2433024
  474.9 3.3 copy-start.9
  478.1 542.4 %reduce-scatter.21.cloned.1.call-start = ((), (), s32[]{:S(2)}) async-start(), calls=%async_computation.19 | async-start | bytes 9732096 | tf_op jit(solution)/shard_map/reduce_scatter | solution.py:173
  485.7 1.1 copy-start.17
  485.7 676.8 %reduce-scatter.23.cloned.1.call-start = ((), (), s32[]{:S(2)}) async-start(), calls=%async_computation.20 | async-start | bytes 9732096 | tf_op jit(solution)/shard_map/reduce_scatter | solution.py:174
  495.1 1.1 copy-start.5
  495.1 1.4 copy-start.7
  496.5 4.4 copy-start.10
  541.6 7.6 copy-start.15
Sparse Core Ops, SparseCore 0:
  10.9 57.0 all-gather.8
  71.0 52.7 all-gather.14
  126.7 52.9 all-gather.12
  181.7 8.7 all-gather.10
  192.4 10.9 all-gather.16
  206.2 55.1 all-gather.18
  264.3 62.5 all-gather.20
  329.8 62.4 all-gather.22
  439.6 7.8 reduce-scatter.14
  450.9 9.0 reduce-scatter.16
  465.8 100.5 reduce-scatter.24
  573.0 98.0 reduce-scatter.18
  676.9 97.9 reduce-scatter.26
  781.5 98.0 reduce-scatter.28
  885.9 134.5 reduce-scatter.20
  1027.9 134.5 reduce-scatter.22
where the time goes:
time: 1170 us
  waiting for transfers between devices  895 us (76%)
  matrix products  117 us (10%)
  blocking collectives  83 us (7%)
  local copies, waits for them, and re-layouts  47.7 us (4%)
  between operations  14.9 us (1%)
    unnamed x19, waiting for transfers between devices  227 us
    reduce_scatter x1, waiting for transfers between devices, per_device(): lax.psum_scatter(outer_w_grad, ('page', 'seq'), scatter_dimension=0, tile...  142 us
    reduce_scatter x1, waiting for transfers between devices, per_device(): lax.psum_scatter(inner_w_grad, ('page', 'seq'), scatter_dimension=0, tile...  141 us
    reduce_scatter x1, waiting for transfers between devices, per_device(): lax.psum_scatter(output_w_grad, ('page', 'seq'), scatter_dimension=0, til...  105 us
    dot_general x18, matrix products, matmul(): return jnp.dot(left_side, right_side, preferred_element_type=jnp.float32)  85.7 us
    unnamed x2, blocking collectives  83 us
    all_gather x1, waiting for transfers between devices, per_device(): lax.all_gather(w_inner, ('page', 'seq'), axis=0, tiled=True)  62.5 us
    all_gather x1, waiting for transfers between devices, per_device(): lax.all_gather(w_key, ('page', 'seq'), axis=0, tiled=True)  52.5 us
  transfers between devices with their start and end apart: 16, of which 14 were waited for; matrix products, arithmetic and copies ran while one was open for 11% of the time, Pallas kernels for 0%

commit v1 on v0

--- a/solution.py
+++ b/solution.py
@@ -1,7 +1,539 @@
+import functools
 import jax
 import jax.numpy as jnp
 from jax import lax
+from jax.experimental import pallas as pl
+from jax.experimental.pallas import tpu as pltpu
+
 from jax.sharding import PartitionSpec as P
+
+MESH = pl.DeviceIdType.MESH
+VMEM = pltpu.VMEM
+DMA = pltpu.SemaphoreType.DMA
+BF = jnp.bfloat16
+F32 = jnp.float32
+
+
+def page_grid(pages):
+    bits = pages.bit_length() - 1
+    nx = 2 ** (bits // 3)
+    ny = 2 ** ((bits - bits // 3) // 2)
+    return pages // (nx * ny), ny, nx
+
+
+class Place:
+    def __init__(self, pages):
+        self.nz, self.ny, self.nx = page_grid(pages)
+        self.p = lax.axis_index("page")
+        self.c = lax.axis_index("seq")
+        self.x = lax.rem(self.p, self.nx)
+        self.y = lax.rem(self.p // self.nx, self.ny)
+        self.z = self.p // (self.nx * self.ny)
+
+    def page(self, dz=0, dy=0, dx=0):
+        z = lax.rem(self.z + dz + self.nz, self.nz)
+        y = lax.rem(self.y + dy + self.ny, self.ny)
+        x = lax.rem(self.x + dx + self.nx, self.nx)
+        return (z * self.ny + y) * self.nx + x
+
+    def partners(self):
+        out = [(self.page(dz=d), self.c) for d in range(1, self.nz)]
+        out += [(self.page(dy=d), self.c) for d in range(1, self.ny)]
+        out += [(self.page(dx=d), self.c) for d in range(1, self.nx)]
+        return out + [(self.p, 1 - self.c)]
+
+    def greet(self):
+        barrier = pltpu.get_barrier_semaphore()
+        partners = self.partners()
+        for partner in partners:
+            pl.semaphore_signal(barrier, inc=1, device_id=partner, device_id_type=MESH)
+        pl.semaphore_wait(barrier, len(partners))
+
+
+def gather_slots(pages):
+    nz, ny, nx = page_grid(pages)
+    fx, fy = nx - 1, ny - 1
+    base, at = {}, 0
+    for name, size in (
+        ("z", nz - 1), ("x", nz * fx), ("y", nz * fy), ("xa", nz * fx * fy),
+        ("yb", nz * fx * fy), ("core", nz * ny * nx),
+    ):
+        base[name] = at
+        at += size
+    return base, at
+
+
+class Gather:
+    def __init__(self, place, ref, send, recv, kind):
+        self.pl, self.ref, self.send, self.recv, self.kind = place, ref, send, recv, kind
+        self.base, _ = gather_slots(place.nz * place.ny * place.nx)
+
+    def view(self, block, part):
+        ref = self.ref
+        if part == "all" or self.kind == "small":
+            return ref.at[:, block]
+        half = 0 if part == "a" else 1
+        if self.kind == "panels":
+            n = ref.shape[0] // 2
+            return ref.at[half * n:(half + 1) * n, block]
+        n = ref.shape[2] // 2
+        return ref.at[:, block, half * n:(half + 1) * n]
+
+    def copy(self, name, slot, block, part, target):
+        where = self.base[name] + slot
+        view = self.view(block, part)
+        return pltpu.make_async_remote_copy(
+            src_ref=view, dst_ref=view, send_sem=self.send.at[where], recv_sem=self.recv.at[where],
+            device_id=target, device_id_type=MESH)
+
+    def block(self, dz=0, dy=0, dx=0):
+        return 2 * self.pl.page(dz, dy, dx) + self.pl.c
+
+    def z_copy(self, dz, mine):
+        p = self.pl
+        return self.copy("z", dz - 1, self.block(0 if mine else -dz), "all", (p.page(dz=dz), p.c))
+
+    def x_copy(self, dx, dz, mine):
+        p = self.pl
+        return self.copy("x", dz * (p.nx - 1) + dx - 1, self.block(-dz, 0, 0 if mine else -dx), "all", (p.page(dx=dx), p.c))
+
+    def y_copy(self, dy, dz, mine):
+        p = self.pl
+        return self.copy("y", dz * (p.ny - 1) + dy - 1, self.block(-dz, 0 if mine else -dy, 0), "all", (p.page(dy=dy), p.c))
+
+    def diag_slot(self, dx, dy, dz):
+        p = self.pl
+        return (dz * (p.ny - 1) + dy - 1) * (p.nx - 1) + dx - 1
+
+    def xa_copy(self, dx, dy, dz, mine):
+        p = self.pl
+        return self.copy("xa", self.diag_slot(dx, dy, dz), self.block(-dz, -dy, 0 if mine else -dx), "a", (p.page(dx=dx), p.c))
+
+    def yb_copy(self, dx, dy, dz, mine):
+        p = self.pl
+        return self.copy("yb", self.diag_slot(dx, dy, dz), self.block(-dz, 0 if mine else -dy, -dx), "b", (p.page(dy=dy), p.c))
+
+    def core_copy(self, dz, dy, dx, mine):
+        p = self.pl
+        slot = (dz * p.ny + dy) * p.nx + dx
+        block = 2 * p.page(-dz, -dy, -dx) + (p.c if mine else 1 - p.c)
+        return self.copy("core", slot, block, "all", (p.p, 1 - p.c))
+
+    def spread(self, dz):
+        p = self.pl
+        for d in range(1, p.nx):
+            self.x_copy(d, dz, True).start()
+        for d in range(1, p.ny):
+            self.y_copy(d, dz, True).start()
+        self.core_copy(dz, 0, 0, True).start()
+
+    def begin(self):
+        for d in range(1, self.pl.nz):
+            self.z_copy(d, True).start()
+        self.spread(0)
+
+    def column(self, dz):
+        self.z_copy(dz, False).wait_recv()
+        self.spread(dz)
+
+    def plane(self, dz):
+        p = self.pl
+        for dy in range(1, p.ny):
+            self.y_copy(dy, dz, False).wait_recv()
+            for dx in range(1, p.nx):
+                self.xa_copy(dx, dy, dz, True).start()
+            self.core_copy(dz, dy, 0, True).start()
+        for dx in range(1, p.nx):
+            self.x_copy(dx, dz, False).wait_recv()
+            if self.kind != "small":
+                for dy in range(1, p.ny):
+                    self.yb_copy(dx, dy, dz, True).start()
+            self.core_copy(dz, 0, dx, True).start()
+
+    def corner(self, dz):
+        p = self.pl
+        for dy in range(1, p.ny):
+            for dx in range(1, p.nx):
+                self.xa_copy(dx, dy, dz, False).wait_recv()
+                if self.kind != "small":
+                    self.yb_copy(dx, dy, dz, False).wait_recv()
+                self.core_copy(dz, dy, dx, True).start()
+
+    def finish_core(self):
+        p = self.pl
+        for dz in range(p.nz):
+            for dy in range(p.ny):
+                for dx in range(p.nx):
+                    self.core_copy(dz, dy, dx, False).wait_recv()
+
+    def drain(self):
+        p = self.pl
+        for d in range(1, p.nz):
+            self.z_copy(d, True).wait_send()
+        for dz in range(p.nz):
+            for dx in range(1, p.nx):
+                self.x_copy(dx, dz, True).wait_send()
+            for dy in range(1, p.ny):
+                self.y_copy(dy, dz, True).wait_send()
+                for dx in range(1, p.nx):
+                    self.xa_copy(dx, dy, dz, True).wait_send()
+                    if self.kind != "small":
+                        self.yb_copy(dx, dy, dz, True).wait_send()
+            for dy in range(p.ny):
+                for dx in range(p.nx):
+                    self.core_copy(dz, dy, dx, True).wait_send()
+
+
+def gather_kernel(pages, wq, wk, wv, wo, wi, wout, small, g_attn, g_inner, g_outer, g_small, *sems):
+    place = Place(pages)
+    mine = 2 * place.p + place.c
+    for j, ref in enumerate((wq, wk, wv, wo)):
+        g_attn[j, mine] = ref[...]
+    width = g_inner.shape[3]
+    for j in range(g_inner.shape[0]):
+        g_inner[j, mine] = wi[:, j * width:(j + 1) * width]
+    g_outer[0, mine] = wout[...]
+    g_small[0, mine] = small[...]
+    place.greet()
+    segs = [
+        Gather(place, ref, sems[2 * i], sems[2 * i + 1], kind)
+        for i, (ref, kind) in enumerate(
+            ((g_small, "small"), (g_attn, "panels"), (g_inner, "panels"), (g_outer, "rows")))
+    ]
+    groups = [segs[:2], segs[2:3], segs[3:]]
+    for group in groups:
+        for seg in group:
+            seg.begin()
+        for dz in range(1, place.nz):
+            for seg in group:
+                seg.column(dz)
+        for dz in range(place.nz):
+            for seg in group:
+                seg.plane(dz)
+        for dz in range(place.nz):
+            for seg in group:
+                seg.corner(dz)
+    for seg in segs:
+        seg.finish_core()
+    for seg in segs:
+        seg.drain()
+
+
+def gather_weights(pages, wq, wk, wv, wo, wi, wout, small):
+    rows, width = wq.shape
+    devices = 2 * pages
+    panels = wi.shape[1] // width
+    _, slots = gather_slots(pages)
+    v = pl.BlockSpec(memory_space=VMEM)
+    return pl.pallas_call(
+        functools.partial(gather_kernel, pages),
+        name="gather_weights",
+        out_shape=(
+            jax.ShapeDtypeStruct((4, devices, rows, width), BF),
+            jax.ShapeDtypeStruct((panels, devices, rows, width), BF),
+            jax.ShapeDtypeStruct((1, devices, wout.shape[0], width), BF),
+            jax.ShapeDtypeStruct((1, devices) + small.shape, BF),
+        ),
+        in_specs=[v] * 7,
+        out_specs=(v,) * 4,
+        scratch_shapes=[DMA((slots,))] * 8,
+        compiler_params=pltpu.CompilerParams(collective_id=0, has_side_effects=True, vmem_limit_bytes=40 << 20),
+    )(wq, wk, wv, wo, wi, wout, small)
+
+
+def reduce_slots(pages):
+    nz, ny, nx = page_grid(pages)
+    fx, fy = nx - 1, ny - 1
+    base, at = {}, 0
+    for name, size in (
+        ("core", nz * ny * nx), ("xa", nz * fx * fy), ("yb", nz * fx * fy), ("x", nz * fx), ("y", nz * fy), ("z", nz - 1),
+    ):
+        base[name] = at
+        at += size
+    return base, at
+
+
+def reduce_scratch(pages, panels, rows, width, kind):
+    nz, ny, nx = page_grid(pages)
+    fx, fy = nx - 1, ny - 1
+    half = (panels // 2, rows) if kind == "panels" else (panels, rows // 2)
+    _, slots = reduce_slots(pages)
+    return [
+        VMEM((panels, nz * ny * nx, rows, width), BF),
+        VMEM((nz * fx * fy,) + half + (width,), BF),
+        VMEM((nz * fx * fy,) + half + (width,), BF),
+        VMEM((nz * fx, panels, rows, width), BF),
+        VMEM((nz * fy, panels, rows, width), BF),
+        VMEM((nz - 1, panels, rows, width), BF),
+        DMA((slots,)),
+        DMA((slots,)),
+    ]
+
+
+class Reduce:
+    def __init__(self, place, part, scratch, kind):
+        self.pl, self.part, self.kind = place, part, kind
+        self.total, self.da, self.db, self.rx, self.ry, self.rz, self.send, self.recv = scratch
+        self.base, _ = reduce_slots(place.nz * place.ny * place.nx)
+
+    def remote(self, name, slot, src, dst, target):
+        where = self.base[name] + slot
+        return pltpu.make_async_remote_copy(
+            src_ref=src, dst_ref=dst, send_sem=self.send.at[where], recv_sem=self.recv.at[where],
+            device_id=target, device_id_type=MESH)
+
+    def half(self, page, which):
+        if self.kind == "panels":
+            n = self.total.shape[0] // 2
+            return self.total.at[which * n:(which + 1) * n, page]
+        n = self.total.shape[2] // 2
+        return self.total.at[:, page, which * n:(which + 1) * n]
+
+    def core_copy(self, dz, dy, dx):
+        p = self.pl
+        page = p.page(dz, dy, dx)
+        return self.remote("core", (dz * p.ny + dy) * p.nx + dx, self.part.at[:, page, 1 - p.c], self.total.at[:, page], (p.p, 1 - p.c))
+
+    def diag(self, dz, dy, dx):
+        p = self.pl
+        return (dz * (p.ny - 1) + dy - 1) * (p.nx - 1) + dx - 1
+
+    def xa_copy(self, dz, dy, dx):
+        p, slot = self.pl, self.diag(dz, dy, dx)
+        return self.remote("xa", slot, self.half(p.page(dz, dy, dx), 0), self.da.at[slot], (p.page(dx=dx), p.c))
+
+    def yb_copy(self, dz, dy, dx):
+        p, slot = self.pl, self.diag(dz, dy, dx)
+        return self.remote("yb", slot, self.half(p.page(dz, dy, dx), 1), self.db.at[slot], (p.page(dy=dy), p.c))
+
+    def x_copy(self, dz, dx):
+        p = self.pl
+        slot = dz * (p.nx - 1) + dx - 1
+        return self.remote("x", slot, self.total.at[:, p.page(dz, 0, dx)], self.rx.at[slot], (p.page(dx=dx), p.c))
+
+    def y_copy(self, dz, dy):
+        p = self.pl
+        slot = dz * (p.ny - 1) + dy - 1
+        return self.remote("y", slot, self.total.at[:, p.page(dz, dy, 0)], self.ry.at[slot], (p.page(dy=dy), p.c))
+
+    def z_copy(self, dz):
+        p = self.pl
+        return self.remote("z", dz - 1, self.total.at[:, p.page(dz, 0, 0)], self.rz.at[dz - 1], (p.page(dz=dz), p.c))
+
+    def begin(self):
+        p = self.pl
+        order = [(dy, dx) for dy in range(1, p.ny) for dx in range(1, p.nx)]
+        order += [(0, dx) for dx in range(1, p.nx)] + [(dy, 0) for dy in range(1, p.ny)] + [(0, 0)]
+        for dy, dx in order:
+            for dz in range(p.nz):
+                self.core_copy(dz, dy, dx).start()
+
+    def pair(self, dz, dy, dx):
+        p = self.pl
+        self.core_copy(dz, dy, dx).wait_recv()
+        page = p.page(dz, dy, dx)
+        return self.part[:, page, p.c].astype(F32) + self.total[:, page].astype(F32)
+
+    def corner(self, dz):
+        p = self.pl
+        for dy in range(1, p.ny):
+            for dx in range(1, p.nx):
+                self.total[:, p.page(dz, dy, dx)] = self.pair(dz, dy, dx).astype(BF)
+                self.xa_copy(dz, dy, dx).start()
+                self.yb_copy(dz, dy, dx).start()
+
+    def plane(self, dz):
+        p = self.pl
+        panels, rows = self.total.shape[0], self.total.shape[2]
+        for dx in range(1, p.nx):
+            total = self.pair(dz, 0, dx)
+            page = p.page(dz, 0, dx)
+            for dy in range(1, p.ny):
+                self.yb_copy(dz, dy, dx).wait_recv()
+                add = self.db[self.diag(dz, dy, dx)].astype(F32)
+                if self.kind == "panels":
+                    n = panels // 2
+                    total = jnp.concatenate([total[:n], total[n:] + add], axis=0)
+                else:
+                    n = rows // 2
+                    total = jnp.concatenate([total[:, :n], total[:, n:] + add], axis=1)
+            self.total[:, page] = total.astype(BF)
+            self.x_copy(dz, dx).start()
+        for dy in range(1, p.ny):
+            total = self.pair(dz, dy, 0)
+            page = p.page(dz, dy, 0)
+            for dx in range(1, p.nx):
+                self.xa_copy(dz, dy, dx).wait_recv()
+                add = self.da[self.diag(dz, dy, dx)].astype(F32)
+                if self.kind == "panels":
+                    n = panels // 2
+                    total = jnp.concatenate([total[:n] + add, total[n:]], axis=0)
+                else:
+                    n = rows // 2
+                    total = jnp.concatenate([total[:, :n] + add, total[:, n:]], axis=1)
+            self.total[:, page] = total.astype(BF)
+            self.y_copy(dz, dy).start()
+
+    def column_sum(self, dz):
+        p = self.pl
+        total = self.pair(dz, 0, 0)
+        for dx in range(1, p.nx):
+            self.x_copy(dz, dx).wait_recv()
+            total += self.rx[dz * (p.nx - 1) + dx - 1].astype(F32)
+        for dy in range(1, p.ny):
+            self.y_copy(dz, dy).wait_recv()
+            total += self.ry[dz * (p.ny - 1) + dy - 1].astype(F32)
+        return total
+
+    def column(self, dz):
+        self.total[:, self.pl.page(dz, 0, 0)] = self.column_sum(dz).astype(BF)
+        self.z_copy(dz).start()
+
+    def finish(self):
+        total = self.column_sum(0)
+        for dz in range(1, self.pl.nz):
+            self.z_copy(dz).wait_recv()
+            total += self.rz[dz - 1].astype(F32)
+        return total
+
+    def drain(self):
+        p = self.pl
+
+        def one(dz, _):
+            for dy in range(p.ny):
+                for dx in range(p.nx):
+                    self.core_copy(dz, dy, dx).wait_send()
+            for dy in range(1, p.ny):
+                for dx in range(1, p.nx):
+                    self.xa_copy(dz, dy, dx).wait_send()
+                    self.yb_copy(dz, dy, dx).wait_send()
+            for dx in range(1, p.nx):
+                self.x_copy(dz, dx).wait_send()
+            for dy in range(1, p.ny):
+                self.y_copy(dz, dy).wait_send()
+            return 0
+
+        lax.fori_loop(0, p.nz, one, 0)
+        for dz in range(1, p.nz):
+            self.z_copy(dz).wait_send()
+
+
+def vector_scratch(pages, rows, width):
+    nz, ny, nx = page_grid(pages)
+    n = 1 + nx - 1 + ny - 1 + nz - 1
+    return [VMEM((4, rows, width), F32), VMEM((n, rows, width), F32), DMA((n,)), DMA((n,))]
+
+
+class VectorSum:
+    def __init__(self, place, scratch):
+        self.pl = place
+        self.held, self.got, self.send, self.recv = scratch
+
+    def legs(self):
+        p = self.pl
+        return [
+            [(p.p, 1 - p.c)],
+            [(p.page(dx=d), p.c) for d in range(1, p.nx)],
+            [(p.page(dy=d), p.c) for d in range(1, p.ny)],
+            [(p.page(dz=d), p.c) for d in range(1, p.nz)],
+        ]
+
+    def copies(self, leg):
+        legs = self.legs()
+        at = sum(len(one) for one in legs[:leg])
+        return [
+            pltpu.make_async_remote_copy(
+                src_ref=self.held.at[leg], dst_ref=self.got.at[at + i], send_sem=self.send.at[at + i],
+                recv_sem=self.recv.at[at + i], device_id=target, device_id_type=MESH)
+            for i, target in enumerate(legs[leg])
+        ], at
+
+    def put(self, leg, value):
+        self.held[leg] = value
+        for copy in self.copies(leg)[0]:
+            copy.start()
+
+    def take(self, leg):
+        copies, at = self.copies(leg)
+        value = self.held[leg]
+        for i, copy in enumerate(copies):
+            copy.wait_recv()
+            value += self.got[at + i]
+        return value
+
+    def drain(self):
+        for leg in range(4):
+            for copy in self.copies(leg)[0]:
+                copy.wait_send()
+
+
+def reduce_kernel(pages, p_attn, p_inner, p_outer, vec, o_q, o_k, o_v, o_o, o_inner, o_outer, o_vec, *scratch):
+    place = Place(pages)
+    outer = Reduce(place, p_outer, scratch[0:8], "rows")
+    inner = Reduce(place, p_inner, scratch[8:16], "panels")
+    attn = Reduce(place, p_attn, scratch[16:24], "panels")
+    vectors = VectorSum(place, scratch[24:28])
+    place.greet()
+    nz = place.nz
+    segs = (outer, inner, attn)
+    vectors.put(0, vec[...])
+    for seg in segs:
+        seg.begin()
+
+    def loop(start, body):
+        def one(dz, _):
+            body(dz)
+            return 0
+        lax.fori_loop(start, nz, one, 0)
+
+    loop(0, outer.corner)
+    vectors.put(1, vectors.take(0))
+    loop(0, inner.corner)
+    loop(0, outer.plane)
+    vectors.put(2, vectors.take(1))
+    loop(0, attn.corner)
+    loop(0, inner.plane)
+    vectors.put(3, vectors.take(2))
+    loop(1, outer.column)
+    loop(0, attn.plane)
+    loop(1, inner.column)
+    o_outer[...] = outer.finish()[0]
+    o_vec[...] = vectors.take(3)
+    loop(1, attn.column)
+    total = inner.finish()
+    width = total.shape[2]
+    for j in range(total.shape[0]):
+        o_inner[:, j * width:(j + 1) * width] = total[j]
+    total = attn.finish()
+    for j, ref in enumerate((o_q, o_k, o_v, o_o)):
+        ref[...] = total[j]
+    for seg in segs:
+        seg.drain()
+    vectors.drain()
+
+
+def reduce_grads(pages, p_attn, p_inner, p_outer, vec):
+    panels, width = p_inner.shape[0], p_inner.shape[4]
+    rows, rows_outer = p_inner.shape[3], p_outer.shape[3]
+    v = pl.BlockSpec(memory_space=VMEM)
+    square = jax.ShapeDtypeStruct((rows, width), F32)
+    return pl.pallas_call(
+        functools.partial(reduce_kernel, pages),
+        name="reduce_grads",
+        out_shape=(square,) * 4 + (
+            jax.ShapeDtypeStruct((rows, panels * width), F32),
+            jax.ShapeDtypeStruct((rows_outer, width), F32),
+            jax.ShapeDtypeStruct(vec.shape, F32),
+        ),
+        in_specs=[v] * 4,
+        out_specs=(v,) * 7,
+        scratch_shapes=reduce_scratch(pages, 1, rows_outer, width, "rows")
+        + reduce_scratch(pages, panels, rows, width, "panels")
+        + reduce_scratch(pages, 4, rows, width, "panels")
+        + vector_scratch(pages, *vec.shape),
+        compiler_params=pltpu.CompilerParams(collective_id=1, has_side_effects=True, vmem_limit_bytes=56 << 20),
+    )(p_attn, p_inner, p_outer, vec)
+
 
 HEADS = 12
 
@@ -49,7 +581,56 @@
     return jnp.where(usable[:, None, None, :], scores, masked_value)
 
 
+AXES = ("page", "seq")
+VECTORS = 8
+
+
+def pack_vectors(vectors, inner):
+    lanes = 128
+    rows = [jnp.pad(v, (0, lanes - v.shape[0])) for v in (*vectors, inner)]
+    rows += [jnp.zeros((lanes,), BF)] * (16 - len(rows))
+    return jnp.stack(rows)
+
+
+def unpack_vectors(small, rows):
+    vectors = [small[:, j, :rows].reshape(-1) for j in range(VECTORS)]
+    return vectors + [small[:, VECTORS, : 4 * rows].reshape(-1)]
+
+
+def gather_all(pages, wq, wk, wv, wo, wi, wout, vectors, b_inner):
+    rows, width = wq.shape
+    panels = wi.shape[1] // width
+    if rows % 8 == 0:
+        small = pack_vectors(vectors, b_inner)
+        ga, gi, go, gs = gather_weights(pages, wq, wk, wv, wo, wi, wout, small)
+        full = width, width
+        return ga.reshape(4, *full), gi.reshape(panels, *full), go.reshape(-1, width), unpack_vectors(gs[0], rows)
+    spread = lambda w: lax.all_gather(w, AXES, axis=0, tiled=True)
+    ga = lax.all_gather(jnp.stack((wq, wk, wv, wo)), AXES, axis=1, tiled=True)
+    gi = lax.all_gather(wi.reshape(rows, panels, width).transpose(1, 0, 2), AXES, axis=1, tiled=True)
+    return ga, gi, spread(wout), [spread(v) for v in (*vectors, b_inner)]
+
+
+def reduce_all(pages, pa, pi, po, vec):
+    panels, width = pi.shape[0], pi.shape[2]
+    rows = width // (2 * pages)
+    at = lax.axis_index("page") * 2 + lax.axis_index("seq")
+    if rows % 8 == 0:
+        split = lambda p: p.reshape(p.shape[0], pages, 2, -1, width)
+        *squares, o_inner, o_outer, total = reduce_grads(pages, split(pa), split(pi), split(po[None]), vec)
+    else:
+        scatter = lambda g, d: lax.psum_scatter(g.astype(F32), AXES, scatter_dimension=d, tiled=True)
+        squares = list(scatter(pa, 1))
+        o_inner = scatter(pi, 1).transpose(1, 0, 2).reshape(rows, -1)
+        o_outer = scatter(po, 0)
+        total = lax.psum(vec, AXES)
+    vectors = [lax.dynamic_slice(total, (j, rows * at), (1, rows))[0] for j in range(VECTORS)]
+    flat = total[VECTORS : VECTORS + panels].reshape(-1)
+    return squares, o_inner, o_outer, vectors, lax.dynamic_slice(flat, (panels * rows * at,), (panels * rows,))
+
+
 def per_device(
+    page_count,
     hidden,
     lengths,
     w_query,
@@ -77,27 +658,14 @@
     work_hidden, work_cot = (hidden, cotangent)
     local_pages, local_tokens = (work_hidden.shape[0], work_hidden.shape[1])
     row_count = local_pages * local_tokens
-    (
-        query_full,
-        key_full,
-        value_full,
-        output_full,
-        query_bias,
-        value_bias,
-        output_bias,
-        gain_one,
-        shift_one,
-    ) = (
-        lax.all_gather(w_query, ("page", "seq"), axis=0, tiled=True),
-        lax.all_gather(w_key, ("page", "seq"), axis=0, tiled=True),
-        lax.all_gather(w_value, ("page", "seq"), axis=0, tiled=True),
-        lax.all_gather(w_output, ("page", "seq"), axis=0, tiled=True),
-        lax.all_gather(b_query, ("page", "seq"), axis=0, tiled=True),
-        lax.all_gather(b_value, ("page", "seq"), axis=0, tiled=True),
-        lax.all_gather(b_output, ("page", "seq"), axis=0, tiled=True),
-        lax.all_gather(attn_gain, ("page", "seq"), axis=0, tiled=True),
-        lax.all_gather(attn_shift, ("page", "seq"), axis=0, tiled=True),
-    )
+    pages = page_count
+    ga, gi, go, vectors = gather_all(
+        pages, w_query, w_key, w_value, w_output, w_inner, w_outer,
+        (b_query, b_value, b_output, attn_gain, attn_shift, b_outer, ffn_gain, ffn_shift), b_inner)
+    query_full, key_full, value_full, output_full = ga[0], ga[1], ga[2], ga[3]
+    query_bias, value_bias, output_bias, gain_one, shift_one, outer_bias, gain_two, shift_two, inner_bias = vectors
+    outer_full = go
+    panels = gi.shape[0]
     flat_rows = work_hidden.reshape(row_count, model_width)
     queries = (matmul(flat_rows, query_full) + query_bias.astype(f32)).astype(bf16)
     key_rows = matmul(flat_rows, key_full).astype(bf16)
@@ -142,15 +710,8 @@
     normed_one, pull_one = jax.vjp(
         layer_norm, residual_one, gain_one.astype(f32), shift_one.astype(f32)
     )
-    inner_full, outer_full, inner_bias, outer_bias, gain_two, shift_two = (
-        lax.all_gather(w_inner, ("page", "seq"), axis=0, tiled=True),
-        lax.all_gather(w_outer, ("page", "seq"), axis=0, tiled=True),
-        lax.all_gather(b_inner, ("page", "seq"), axis=0, tiled=True),
-        lax.all_gather(b_outer, ("page", "seq"), axis=0, tiled=True),
-        lax.all_gather(ffn_gain, ("page", "seq"), axis=0, tiled=True),
-        lax.all_gather(ffn_shift, ("page", "seq"), axis=0, tiled=True),
-    )
     normed_low = normed_one.astype(bf16)
+    inner_full = gi.transpose(1, 0, 2).reshape(model_width, -1)
     pre_gelu = matmul(normed_low, inner_full) + inner_bias.astype(f32)
     post_gelu, pull_gelu = jax.vjp(gelu_exact, pre_gelu)
     post_low = post_gelu.astype(bf16)
@@ -169,14 +730,6 @@
     inner_b_grad = column_sum(d_pre)
     d_normed = d_res_two + matmul(d_pre, inner_full.T)
     d_res_one, gain_one_grad, shift_one_grad = pull_one(d_normed)
-    ffn_owned = (
-        lax.psum_scatter(inner_w_grad, ("page", "seq"), scatter_dimension=0, tiled=True),
-        lax.psum_scatter(outer_w_grad, ("page", "seq"), scatter_dimension=0, tiled=True),
-        lax.psum_scatter(inner_b_grad, ("page", "seq"), scatter_dimension=0, tiled=True),
-        lax.psum_scatter(outer_b_grad, ("page", "seq"), scatter_dimension=0, tiled=True),
-        lax.psum_scatter(gain_two_grad, ("page", "seq"), scatter_dimension=0, tiled=True),
-        lax.psum_scatter(shift_two_grad, ("page", "seq"), scatter_dimension=0, tiled=True),
-    )
     d_attn = d_res_one.astype(bf16)
     output_w_grad = matmul(context_low.T, d_attn)
     output_b_grad = column_sum(d_attn)
@@ -250,38 +803,18 @@
         + matmul(d_keys, key_full.T)
         + matmul(d_values, value_full.T)
     ).astype(bf16)
-    attn_owned = (
-        lax.psum_scatter(query_w_grad, ("page", "seq"), scatter_dimension=0, tiled=True),
-        lax.psum_scatter(key_w_grad, ("page", "seq"), scatter_dimension=0, tiled=True),
-        lax.psum_scatter(value_w_grad, ("page", "seq"), scatter_dimension=0, tiled=True),
-        lax.psum_scatter(output_w_grad, ("page", "seq"), scatter_dimension=0, tiled=True),
-        lax.psum_scatter(query_b_grad, ("page", "seq"), scatter_dimension=0, tiled=True),
-        lax.psum_scatter(value_b_grad, ("page", "seq"), scatter_dimension=0, tiled=True),
-        lax.psum_scatter(output_b_grad, ("page", "seq"), scatter_dimension=0, tiled=True),
-        lax.psum_scatter(gain_one_grad, ("page", "seq"), scatter_dimension=0, tiled=True),
-        lax.psum_scatter(shift_one_grad, ("page", "seq"), scatter_dimension=0, tiled=True),
-    )
+    pa = jnp.stack([g.astype(bf16) for g in (query_w_grad, key_w_grad, value_w_grad, output_w_grad)])
+    pi = inner_w_grad.astype(bf16).reshape(model_width, panels, model_width).transpose(1, 0, 2)
+    po = outer_w_grad.astype(bf16)
+    singles = (query_b_grad, value_b_grad, output_b_grad, gain_one_grad, shift_one_grad, outer_b_grad, gain_two_grad, shift_two_grad)
+    vec = jnp.concatenate([jnp.stack(singles), inner_b_grad.reshape(panels, model_width)])
+    vec = jnp.pad(vec, ((0, 16 - vec.shape[0]), (0, 0)))
+    squares, o_inner, o_outer, owned, o_inner_bias = reduce_all(pages, pa, pi, po, vec)
     out_pages = layer_out.astype(bf16).reshape(local_pages, local_tokens, model_width)
     grad_pages = hidden_grad.reshape(local_pages, local_tokens, model_width)
     return (
-        out_pages,
-        grad_pages,
-        attn_owned[0],
-        attn_owned[1],
-        attn_owned[2],
-        attn_owned[3],
-        attn_owned[4],
-        attn_owned[5],
-        attn_owned[6],
-        attn_owned[7],
-        attn_owned[8],
-        ffn_owned[0],
-        ffn_owned[2],
-        ffn_owned[1],
-        ffn_owned[3],
-        ffn_owned[4],
-        ffn_owned[5],
-    )
+        out_pages, grad_pages, *squares, owned[0], owned[1], owned[2], owned[3], owned[4],
+        o_inner, o_inner_bias, o_outer, owned[5], owned[6], owned[7])
 
 
 def solution(mesh):
@@ -325,5 +858,5 @@
         P(("page", "seq")),
     )
     return jax.shard_map(
-        per_device, mesh=mesh, in_specs=in_specs, out_specs=out_specs, check_vma=False
-    )
+        functools.partial(per_device, mesh.shape["page"]), mesh=mesh, in_specs=in_specs, out_specs=out_specs, check_vma=False
+    )

time: 1170 us -> 360 us (0.31)
  waiting for transfers between devices: 895 us -> 1.28 us
  Pallas kernels: 0 us -> 166 us
  blocking collectives: 83 us -> 0 us
    reduce_scatter x3 -> x0, waiting for transfers between devices: 388 us -> none  [the longest x1 142 us: per_device(): lax.psum_scatter(outer_w_grad, ('page', 'seq'), scatter_dimension=0, tile...]
    all_gather x6 -> x0, waiting for transfers between devices: 263 us -> none  [the longest x1 62.5 us: per_device(): lax.all_gather(w_inner, ('page', 'seq'), axis=0, tiled=True)]
    unnamed x19 -> x4, waiting for transfers between devices: 227 us -> 0.07 us
    pallas_call x0 -> x2, Pallas kernels: none -> 166 us  [the longest x1 83.4 us: reduce_grads(): pl.pallas_call(functools.partial(reduce_kernel, pages), name='reduce_grad...]
    unnamed x2 -> x0, blocking collectives: 83 us -> none
    unnamed x86 -> x108, local copies, waits for them, and re-layouts: 30.4 us -> 15.7 us
    dot_general x18, matrix products: 85.7 us -> 72.1 us  [matmul(): return jnp.dot(left_side, right_side, preferred_element_type=jnp.float32)]
  transfers between devices with their start and end apart: 16 -> 4, of which waited for: 14 -> 1; matrix products, arithmetic and copies ran while one was open for 11% -> 17% of each run, Pallas kernels for 0% -> 0%
where the time goes in v1:
time: 360 us; the launch traced here: 356 us
  Pallas kernels  166 us (46%)
  matrix products  106 us (29%)
  local copies, waits for them, and re-layouts  52.3 us (15%)
  other arithmetic  14.9 us (4%)
  between operations  14.6 us (4%)
    pallas_call x1, Pallas kernels, reduce_grads(): pl.pallas_call(functools.partial(reduce_kernel, pages), name='reduce_grad...  83.4 us
    pallas_call x1, Pallas kernels, gather_weights(): pl.pallas_call(functools.partial(gather_kernel, pages), name='gather_weig...  82.3 us
    dot_general x18, matrix products, matmul(): return jnp.dot(left_side, right_side, preferred_element_type=jnp.float32)  72.1 us
    unnamed x108, local copies, waits for them, and re-layouts  15.7 us
    dot_general x1, matrix products, merged(): jnp.einsum('phqk,pqhd->pkhd', attn_probs.astype(bf16), d_context_heads, p...  8.64 us
    dot_general x1, matrix products, merged(): jnp.einsum('pqhd,pkhd->phqk', d_context_heads, value_heads, preferred_ele...  7.93 us
    dot_general x1, matrix products, merged(): jnp.einsum('phqk,pkhd->pqhd', attn_probs, head_split(value_piece, head_co...  7.76 us
  transfers between devices with their start and end apart: 4, of which 1 were waited for; matrix products, arithmetic and copies ran while one was open for 17% of the time, Pallas kernels for 0%

profile of v1, /device:TPU:0, one launch (start us, length us, event | category | flops | bytes accessed | tf_op | source)
XLA Modules:
  0.0 355.6 jit_solution(4534362627174074924)
XLA Ops:
  10.7 0.9 copy-done.1
  15.6 82.3 %gather_weights.1 = (bf16[4,32,24,768]{3,2,1,0:T(8,128)(2,1)S(1)}, bf16[4,32,24,768]{3,2,1,0:T(8,128)(2,1)S(1)}, bf16[1,32,96,768]{3,2,1,0:T(8,128)(2,1)}, bf16[1,32,16,128]{3,2,1,0:T(8,128)(2,1)S(1)}) custom-call(bf16[24,768]{1,0:T(8,128)(2,1)S(1)} %copy-done.3, bf16[24,768]{1,0:T(8,128)(2,1)S(1)} %copy-done.4, bf16[24,768]{1,0:T(8,128)(2,1)S(1)} %copy-done.5, ...), custom_call_target="tpu_custom_call" | custom-call | tf_op jit(solution)/shard_map/gather_weights/pallas_call | solution.py:228
  97.9 1.3 fusion.44
  99.2 1.1 copy-done
  100.4 1.0 copy-done.19
  101.4 1.7 convolution_convert_fusion.4
  103.6 2.8 add_convert_fusion.4
  106.9 6.8 %copy.50 = bf16[4,768,768]{1,2,0:T(8,128)(2,1)} copy(bf16[4,768,768]{2,1,0:T(8,128)(2,1)} %bitcast.167) | data formatting | bytes 9437184 | tf_op jit(solution)/shard_map/reshape | solution.py:607
  115.4 1.7 copy.47
  117.1 2.3 fusion.1
  119.4 3.3 exponential_reduce_fusion
  122.7 1.7 copy-done.7
  124.4 1.2 all-gather.3.cloned.1.call-done
  125.6 2.7 copy.46
  128.2 7.8 %bitcast_convert_fusion.3 = (bf16[2,256,12,64]{1,3,2,0:T(8,128)(2,1)S(1)}, f32[2,12,64,256]{3,2,1,0:T(8,128)}) fusion(bf16[2,512,12,64]{1,3,2,0:T(8,128)(2,1)} %bitcast.187, f32[2,12,256,512]{3,2,1,0:T(8,128)} %copy-done.7, f32[2,12,256]{2,1,0:T(8,128)S(1)} %log_add_fusion, pred[2,512]{1,0:T(4,128)(4,1)S(1)} %iota_compare_fusion), kind=kOutput, calls=%fused_computation.43 | convolution fusion | flops 415629312 | bytes 16540672 | tf_op jit(solution)/shard_map/phqk,pkhd->pqhd/dot_general | solution.py:697
  137.5 0.9 fusion.45
  138.8 19.8 %multiply_convert_fusion.1 = (bf16[512,3072]{1,0:T(8,128)(2,1)S(1)}, f32[512,3072]{1,0:T(8,128)}, f32[512,3072]{1,0:T(8,128)}) fusion(f32[3072]{0:T(1024)S(1)} %reshape.308, bf16[768,3072]{0,1:T(8,128)(2,1)S(1)} %bitcast.178, f32[512,768]{1,0:T(8,128)S(1)} %get-tuple-element.82, f32[768]{0:T(1024)S(1)} %reshape.307, f32[768]{0:T(1024)S(1)} %reshape.306, ...), kind=kOutput, calls=%fused_computation.10 | convolution fusion | flops 2521694208 | bytes 22042624 | tf_op jit(solution)/shard_map/dot_general | solution.py:557
  158.7 2.8 fusion.46
  162.6 1.6 fusion.42
  164.4 9.6 %convert_reduce_fusion = (f32[3072]{0:T(1024)S(1)}, bf16[512,3072]{1,0:T(8,128)(2,1)}) fusion(f32[512,3072]{1,0:T(8,128)} %get-tuple-element.63, f32[512,3072]{1,0:T(8,128)} %get-tuple-element.83, f32[3072]{0:T(1024)S(1)} %reshape.308, bf16[512,768]{1,0:T(8,128)(2,1)S(1)} %get-tuple-element.55, bf16[3072,768]{1,0:T(8,128)(2,1)S(1)} %bitcast.211), kind=kOutput, calls=%fused_computation.8 | convolution fusion | flops 2442654720 | bytes 21258240 | tf_op jit(solution)/shard_map/dot_general | solution.py:557
  174.0 4.9 %multiply_reduce_fusion = (f32[768]{0:T(1024)S(1)}, f32[512]{0:T(512)S(1)}, f32[768]{0:T(1024)S(1)}, f32[512,768]{1,0:T(8,128)S(1)}) fusion(f32[512,768]{1,0:T(8,128)S(1)} %get-tuple-element.82, f32[512]{0:T(512)S(1)} %fusion.32, f32[512]{0:T(512)S(1)} %broadcast_multiply_fusion.1, f32[768]{0:T(1024)S(1)} %reshape.306, ...), kind=kOutput, calls=%fused_computation.46 | convolution fusion | flops 2419849216 | bytes 12600320 | tf_op jit(solution)/shard_map/dot_general | solution.py:557
  180.8 1.7 convolution_convert_fusion.5
  182.4 2.3 copy.51
  184.7 2.9 reshape_reshape.7
  187.7 1.9 fusion.12
  189.5 7.9 %multiply_convert_fusion = bf16[2,12,256,512]{3,2,1,0:T(8,128)(2,1)S(1)} fusion(f32[2,12,256,512]{3,2,1,0:T(8,128)} %copy-done.7, f32[2,12,256]{2,1,0:T(8,128)S(1)} %bitcast.207, f32[2,12,256]{2,1,0:T(8,128)S(1)} %log_add_fusion, pred[2,512]{1,0:T(4,128)(4,1)S(1)} %iota_compare_fusion, bf16[2,512,12,64]{1,3,2,0:T(8,128)(2,1)} %bitcast.188, ...), kind=kOutput, calls=%fused_computation | convolution fusion | flops 421527552 | bytes 21283840 | tf_op jit(solution)/shard_map/pqhd,pkhd->phqk/dot_general | solution.py:755
  197.5 2.7 multiply_convert_fusion.2
  200.5 2.6 copy.56
  203.2 8.6 %convolution_convert_fusion.2 = bf16[2,12,64,512]{3,2,1,0:T(8,128)(2,1)} fusion(bf16[2,256,12,64]{1,0,3,2:T(2,128)(2,1)} %reshape_reshape.7, f32[2,12,256,512]{3,2,1,0:T(8,128)} %copy-done.7, f32[2,12,256]{2,1,0:T(8,128)S(1)} %log_add_fusion, pred[2,512]{1,0:T(4,128)(4,1)S(1)} %iota_compare_fusion), kind=kOutput, calls=%fused_computation.34 | convolution fusion | flops 416022528 | bytes 14967808 | tf_op jit(solution)/shard_map/phqk,pqhd->pkhd/dot_general | solution.py:765
  211.9 2.8 copy.58
  214.7 1.3 convert_reduce_fusion.1
  216.0 5.0 %convert_reduce_fusion.5 = (f32[12,64]{1,0:T(8,128)S(1)}, bf16[2,12,64,256]{3,2,1,0:T(8,128)(2,1)S(1)}) fusion(bf16[2,512,12,64]{1,3,2,0:T(8,128)(2,1)S(1)} %bitcast.172, bf16[2,12,256,512]{3,2,1,0:T(8,128)(2,1)} %copy-done.8), kind=kOutput, calls=%fused_computation.49 | convolution fusion | flops 404225280 | bytes 8653824 | tf_op jit(solution)/shard_map/phqk,pkhd->pqhd/dot_general | solution.py:759
  221.9 1.1 copy.70
  222.9 3.4 convolution_convert_fusion.1
  226.3 2.4 copy.83
  228.9 3.1 convolution_convert_fusion.3
  232.0 3.2 bitcast_convert_fusion.2
  235.2 2.0 fusion.47
  237.2 4.4 %convolution_convert_fusion = bf16[3072,768]{1,0:T(8,128)(2,1)} fusion(bf16[512,3072]{1,0:T(8,128)(2,1)S(1)} %copy-done.45, bf16[512,768]{1,0:T(8,128)(2,1)S(1)} %copy-done.30), kind=kOutput, calls=%fused_computation.24 | convolution fusion | flops 2418278400 | bytes 8650752 | tf_op jit(solution)/shard_map/dot_general | solution.py:557
  241.6 3.1 fusion.48
  244.7 1.4 convert_reduce_fusion.4
  246.7 2.3 bitcast_convert_fusion
  249.1 2.0 bitcast_convert_fusion.1
  251.1 2.5 pad_maximum_fusion.p_attn
  253.6 83.4 %reduce_grads.1 = (f32[24,768]{1,0:T(8,128)}, f32[24,768]{1,0:T(8,128)}, f32[24,768]{1,0:T(8,128)}, f32[24,768]{1,0:T(8,128)}, f32[24,3072]{1,0:T(8,128)}, /*index=5*/f32[96,768]{1,0:T(8,128)}, f32[16,768]{1,0:T(8,128)}) custom-call(bf16[4,16,2,24,768]{4,3,2,1,0:T(8,128)(2,1)} %pad_maximum_fusion.p_attn, bf16[4,16,2,24,768]{4,3,2,1,0:T(8,128)(2,1)} %bitcast.170, ...), custom_call_target="tpu_custom_call" | custom-call | tf_op jit(solution)/shard_map/reduce_grads/pallas_call | solution.py:520
  337.8 1.6 dynamic-slice_bitcast_fusion
  340.0 1.3 dynamic_slice.32
  341.3 3.7 %add_convert_fusion.1 = bf16[512,768]{1,0:T(8,128)(2,1)} fusion(f32[512,768]{1,0:T(8,128)} %fusion.48, f32[512,768]{1,0:T(8,128)} %fusion.47, bf16[512,768]{1,0:T(8,128)(2,1)S(1)} %bitcast.186, bf16[768,768]{1,0:T(8,128)(2,1)S(1)} %bitcast.175, f32[512,768]{1,0:T(8,128)S(1)} %get-tuple-element.59, f32[512]{0:T(512)S(1)} %negate_multiply_fusion.1), kind=kOutput, calls=%fused_computation.50 | convolution fusion | flops 605945856 | bytes 7473152 | tf_op jit(solution)/shard_map/dot_general | solution.py:557
  (170 shorter events, 22.4 us)
Async XLA Ops:
  7.2 108.2 %all-gather.5.cloned.1.call-start = ((), (), s32[]{:S(2)}) async-start(), calls=%async_computation.3 | async-start | bytes 2359296 | tf_op jit(solution)/shard_map/all_gather | solution.py:690
  10.7 0.9 copy-start.1
  97.9 2.5 copy-start
  97.9 3.5 copy-start.39
  100.4 1.0 copy-start.19
  100.4 6.0 %copy-start.14 = (bf16[1,32,24,768]{3,2,1,0:T(8,128)(2,1)}, bf16[1,32,24,768]{3,2,1,0:T(8,128)(2,1)S(1)}, u32[]{:S(2)}) copy-start(bf16[1,32,24,768]{3,2,1,0:T(8,128)(2,1)S(1)} %get-tuple-element.67) | copy-start | bytes 3538948
  100.4 13.6 %copy-start.21 = (bf16[1,32,24,768]{3,2,1,0:T(8,128)(2,1)}, bf16[1,32,24,768]{3,2,1,0:T(8,128)(2,1)S(1)}, u32[]{:S(2)}) copy-start(bf16[1,32,24,768]{3,2,1,0:T(8,128)(2,1)S(1)} %get-tuple-element.66) | copy-start | bytes 3538948
  103.1 22.5 %all-gather.3.cloned.1.call-start = ((), (), s32[]{:S(2)}) async-start(), calls=%async_computation.2 | async-start | bytes 2359296 | tf_op jit(solution)/shard_map/all_gather | solution.py:691
  106.4 135.2 %reduce-scatter.3.cloned.1.call-start = ((), (), s32[]{:S(2)}) async-start(), calls=%async_computation.4 | async-start | bytes 2359296 | tf_op jit(solution)/shard_map/reduce_scatter | solution.py:785
  106.9 6.9 %copy-start.38 = (s32[2]{0:T(128)S(1)}, s32[2]{0:T(128)}, u32[]{:S(2)}) copy-start(s32[2]{0:T(128)} %param.19) | copy-start | bytes 28
  106.9 7.1 %copy-start.40 = (bf16[2,256,768]{2,1,0:T(8,128)(2,1)S(1)}, bf16[2,256,768]{2,1,0:T(8,128)(2,1)}, u32[]{:S(2)}) copy-start(bf16[2,256,768]{2,1,0:T(8,128)(2,1)} %param.18) | copy-start | bytes 2359300
  115.0 4.4 %copy-start.9 = (bf16[2,256,12,64]{1,0,3,2:T(2,128)(2,1)}, bf16[2,256,12,64]{1,0,3,2:T(2,128)(2,1)S(1)}, u32[]{:S(2)}) copy-start(bf16[2,256,12,64]{1,0,3,2:T(2,128)(2,1)S(1)} %reshape_reshape.6) | copy-start | bytes 2359300
  119.4 5.0 %copy-start.7 = (f32[2,12,256,512]{3,2,1,0:T(8,128)}, f32[2,12,256,512]{3,2,1,0:T(8,128)S(1)}, u32[]{:S(2)}) copy-start(f32[2,12,256,512]{3,2,1,0:T(8,128)S(1)} %get-tuple-element.78) | copy-start | bytes 37748740
  125.6 13.2 %slice-start = ((s8[4718592]{0:T(1024)(128)(4,1)}), s8[524288]{0:T(1024)(128)(4,1)S(1)}, s32[]{:S(2)}) async-start(s8[4718592]{0:T(1024)(128)(4,1)} %bitcast.176), calls=%async_computation.6 | async-start | bytes 1048576
  128.2 10.6 %slice-start.1 = ((s8[4718592]{0:T(1024)(128)(4,1)}), s8[4194304]{0:T(1024)(128)(4,1)S(1)}, s32[]{:S(2)}) async-start(s8[4718592]{0:T(1024)(128)(4,1)} %bitcast.176), calls=%async_computation.7 | async-start | bytes 8388608
  136.0 1.3 copy-start.23
  136.0 1.5 copy-start.41
  137.0 1.8 copy-start.26
  137.5 21.1 %slice-start.2 = ((s8[4718592]{0:T(1024)(128)(4,1)}), s8[4194304]{0:T(1024)(128)(4,1)S(1)}, s32[]{:S(2)}) async-start(s8[4718592]{0:T(1024)(128)(4,1)} %bitcast.208), calls=%async_computation.8 | async-start | bytes 8388608
  138.4 40.6 %copy-start.12 = (f32[512,768]{1,0:T(8,128)}, f32[512,768]{1,0:T(8,128)S(1)}, u32[]{:S(2)}) copy-start(f32[512,768]{1,0:T(8,128)S(1)} %get-tuple-element.82) | copy-start | bytes 4718596
  138.8 19.8 %slice-start.3 = ((s8[4718592]{0:T(1024)(128)(4,1)}), s8[524288]{0:T(1024)(128)(4,1)S(1)}, s32[]{:S(2)}) async-start(s8[4718592]{0:T(1024)(128)(4,1)} %bitcast.208), calls=%async_computation.9 | async-start | bytes 1048576
  158.6 2.8 copy-start.44
  158.7 3.1 copy-start.11
  164.4 9.6 %copy-start.29 = (bf16[512,768]{1,0:T(8,128)(2,1)}, bf16[512,768]{1,0:T(8,128)(2,1)S(1)}, u32[]{:S(2)}) copy-start(bf16[512,768]{1,0:T(8,128)(2,1)S(1)} %get-tuple-element.55) | copy-start | bytes 2359300
  189.5 7.9 %copy-start.10 = (bf16[2,256,12,64]{1,0,3,2:T(2,128)(2,1)S(1)}, bf16[2,256,12,64]{1,0,3,2:T(2,128)(2,1)}, u32[]{:S(2)}) copy-start(bf16[2,256,12,64]{1,0,3,2:T(2,128)(2,1)} %copy-done.9) | copy-start | bytes 2359300
  197.5 3.1 copy-start.8
  203.2 41.5 %reduce-scatter.5.cloned.1.call-start = ((), (), s32[]{:S(2)}) async-start(), calls=%async_computation.5 | async-start | bytes 2359296 | tf_op jit(solution)/shard_map/reduce_scatter | solution.py:788
  216.0 6.9 %copy-start.43 = (bf16[512,3072]{1,0:T(8,128)(2,1)S(1)}, bf16[512,3072]{1,0:T(8,128)(2,1)}, u32[]{:S(2)}) copy-start(bf16[512,3072]{1,0:T(8,128)(2,1)} %get-tuple-element.53) | copy-start | bytes 9437188
  221.0 5.3 %copy-start.16 = (bf16[2,12,64,256]{3,2,1,0:T(8,128)(2,1)}, bf16[2,12,64,256]{3,2,1,0:T(8,128)(2,1)S(1)}, u32[]{:S(2)}) copy-start(bf16[2,12,64,256]{3,2,1,0:T(8,128)(2,1)S(1)} %get-tuple-element.88) | copy-start | bytes 2359300
  221.0 1.9 copy-start.13
  226.3 2.6 copy-start.27
  228.8 3.2 copy-start.17
  228.9 6.3 %copy-start.22 = (bf16[1,32,24,768]{3,2,1,0:T(8,128)(2,1)S(1)}, bf16[1,32,24,768]{3,2,1,0:T(8,128)(2,1)}, u32[]{:S(2)}) copy-start(bf16[1,32,24,768]{3,2,1,0:T(8,128)(2,1)} %copy-done.21) | copy-start | bytes 3538948
  228.9 6.3 %copy-start.28 = (bf16[96,8,2,256]{3,1,2,0:T(8,128)(2,1)S(1)}, bf16[96,8,2,256]{3,1,2,0:T(8,128)(2,1)}, u32[]{:S(2)}) copy-start(bf16[96,8,2,256]{3,1,2,0:T(8,128)(2,1)} %copy.70) | copy-start | bytes 2359300
  232.0 5.2 %copy-start.30 = (bf16[512,768]{1,0:T(8,128)(2,1)S(1)}, bf16[512,768]{1,0:T(8,128)(2,1)}, u32[]{:S(2)}) copy-start(bf16[512,768]{1,0:T(8,128)(2,1)} %copy-done.29) | copy-start | bytes 2359300
  232.0 5.2 %copy-start.45 = (bf16[512,3072]{1,0:T(8,128)(2,1)S(1)}, bf16[512,3072]{1,0:T(8,128)(2,1)}, u32[]{:S(2)}) copy-start(bf16[512,3072]{1,0:T(8,128)(2,1)} %copy-done.44) | copy-start | bytes 9437188
  237.2 4.4 %copy-start.20 = (bf16[1,32,24,768]{3,2,1,0:T(8,128)(2,1)S(1)}, bf16[1,32,24,768]{3,2,1,0:T(8,128)(2,1)}, u32[]{:S(2)}) copy-start(bf16[1,32,24,768]{3,2,1,0:T(8,128)(2,1)} %copy-done.19) | copy-start | bytes 3538948
  244.7 4.4 %copy-start.42 = (bf16[2,256,768]{2,1,0:T(8,128)(2,1)S(1)}, bf16[2,256,768]{2,1,0:T(8,128)(2,1)}, u32[]{:S(2)}) copy-start(bf16[2,256,768]{2,1,0:T(8,128)(2,1)} %param.18) | copy-start | bytes 2359300
  246.7 4.3 %copy-start.24 = (bf16[768,768]{1,0:T(8,128)(2,1)S(1)}, bf16[768,768]{1,0:T(8,128)(2,1)}, u32[]{:S(2)}) copy-start(bf16[768,768]{1,0:T(8,128)(2,1)} %convolution_convert_fusion.3) | copy-start | bytes 3538948
  246.7 4.3 %copy-start.25 = (bf16[768,768]{0,1:T(8,128)(2,1)S(1)}, bf16[768,768]{0,1:T(8,128)(2,1)}, u32[]{:S(2)}) copy-start(bf16[768,768]{0,1:T(8,128)(2,1)} %bitcast_convert_fusion.2) | copy-start | bytes 3538948
  253.6 87.6 %copy-start.15 = (bf16[1,32,24,768]{3,2,1,0:T(8,128)(2,1)S(1)}, bf16[1,32,24,768]{3,2,1,0:T(8,128)(2,1)}, u32[]{:S(2)}) copy-start(bf16[1,32,24,768]{3,2,1,0:T(8,128)(2,1)} %copy-done.14) | copy-start | bytes 3538948
  253.6 87.6 %copy-start.18 = (bf16[2,256,768]{2,1,0:T(8,128)(2,1)S(1)}, bf16[2,256,768]{2,1,0:T(8,128)(2,1)}, u32[]{:S(2)}) copy-start(bf16[2,256,768]{2,1,0:T(8,128)(2,1)} %reduce-scatter.5.cloned.1.call-done) | copy-start | bytes 2359300
  341.2 3.7 %copy-start.37 = (f32[24,768]{1,0:T(8,128)S(1)}, f32[24,768]{1,0:T(8,128)}, u32[]{:S(2)}) copy-start(f32[24,768]{1,0:T(8,128)} %get-tuple-element.116) | copy-start | bytes 221188
  341.2 4.3 %copy-start.36 = (f32[24,768]{1,0:T(8,128)S(1)}, f32[24,768]{1,0:T(8,128)}, u32[]{:S(2)}) copy-start(f32[24,768]{1,0:T(8,128)} %get-tuple-element.117) | copy-start | bytes 221188
  341.3 5.0 %copy-start.35 = (f32[24,768]{1,0:T(8,128)S(1)}, f32[24,768]{1,0:T(8,128)}, u32[]{:S(2)}) copy-start(f32[24,768]{1,0:T(8,128)} %get-tuple-element.118) | copy-start | bytes 221188
  341.3 5.6 %copy-start.34 = (f32[24,768]{1,0:T(8,128)S(1)}, f32[24,768]{1,0:T(8,128)}, u32[]{:S(2)}) copy-start(f32[24,768]{1,0:T(8,128)} %get-tuple-element.119) | copy-start | bytes 221188
  341.3 6.2 %copy-start.33 = (f32[24,3072]{1,0:T(8,128)S(1)}, f32[24,3072]{1,0:T(8,128)}, u32[]{:S(2)}) copy-start(f32[24,3072]{1,0:T(8,128)} %get-tuple-element.125) | copy-start | bytes 884740
  341.3 6.9 %copy-start.32 = (f32[96,768]{1,0:T(8,128)S(1)}, f32[96,768]{1,0:T(8,128)}, u32[]{:S(2)}) copy-start(f32[96,768]{1,0:T(8,128)} %get-tuple-element.127) | copy-start | bytes 884740
  (6 other events, 4.9 us)
Sparse Core Ops, SparseCore 0:
  103.2 9.2 all-gather.4
  114.6 10.9 all-gather.2
  203.3 10.2 reduce-scatter.2
  215.8 10.2 reduce-scatter.4

commit v2 on v1

--- a/solution.py
+++ b/solution.py
@@ -1,4 +1,5 @@
 import functools
+import types
 import jax
 import jax.numpy as jnp
 from jax import lax
@@ -12,6 +13,8 @@
 DMA = pltpu.SemaphoreType.DMA
 BF = jnp.bfloat16
 F32 = jnp.float32
+AXES = PAGE, SEQ = ("page", "seq")
+SMALL, PANELS, ROWS = range(3)
 
 
 def page_grid(pages):
@@ -24,8 +27,8 @@
 class Place:
     def __init__(self, pages):
         self.nz, self.ny, self.nx = page_grid(pages)
-        self.p = lax.axis_index("page")
-        self.c = lax.axis_index("seq")
+        self.p = lax.axis_index(PAGE)
+        self.c = lax.axis_index(SEQ)
         self.x = lax.rem(self.p, self.nx)
         self.y = lax.rem(self.p // self.nx, self.ny)
         self.z = self.p // (self.nx * self.ny)
@@ -70,10 +73,10 @@
 
     def view(self, block, part):
         ref = self.ref
-        if part == "all" or self.kind == "small":
+        if part == "all" or self.kind == SMALL:
             return ref.at[:, block]
         half = 0 if part == "a" else 1
-        if self.kind == "panels":
+        if self.kind == PANELS:
             n = ref.shape[0] // 2
             return ref.at[half * n:(half + 1) * n, block]
         n = ref.shape[2] // 2
@@ -127,10 +130,9 @@
             self.y_copy(d, dz, True).start()
         self.core_copy(dz, 0, 0, True).start()
 
-    def begin(self):
+    def begin_z(self):
         for d in range(1, self.pl.nz):
             self.z_copy(d, True).start()
-        self.spread(0)
 
     def column(self, dz):
         self.z_copy(dz, False).wait_recv()
@@ -145,7 +147,7 @@
             self.core_copy(dz, dy, 0, True).start()
         for dx in range(1, p.nx):
             self.x_copy(dx, dz, False).wait_recv()
-            if self.kind != "small":
+            if self.kind != SMALL:
                 for dy in range(1, p.ny):
                     self.yb_copy(dx, dy, dz, True).start()
             self.core_copy(dz, 0, dx, True).start()
@@ -155,7 +157,7 @@
         for dy in range(1, p.ny):
             for dx in range(1, p.nx):
                 self.xa_copy(dx, dy, dz, False).wait_recv()
-                if self.kind != "small":
+                if self.kind != SMALL:
                     self.yb_copy(dx, dy, dz, False).wait_recv()
                 self.core_copy(dz, dy, dx, True).start()
 
@@ -177,68 +179,11 @@
                 self.y_copy(dy, dz, True).wait_send()
                 for dx in range(1, p.nx):
                     self.xa_copy(dx, dy, dz, True).wait_send()
-                    if self.kind != "small":
+                    if self.kind != SMALL:
                         self.yb_copy(dx, dy, dz, True).wait_send()
             for dy in range(p.ny):
                 for dx in range(p.nx):
                     self.core_copy(dz, dy, dx, True).wait_send()
-
-
-def gather_kernel(pages, wq, wk, wv, wo, wi, wout, small, g_attn, g_inner, g_outer, g_small, *sems):
-    place = Place(pages)
-    mine = 2 * place.p + place.c
-    for j, ref in enumerate((wq, wk, wv, wo)):
-        g_attn[j, mine] = ref[...]
-    width = g_inner.shape[3]
-    for j in range(g_inner.shape[0]):
-        g_inner[j, mine] = wi[:, j * width:(j + 1) * width]
-    g_outer[0, mine] = wout[...]
-    g_small[0, mine] = small[...]
-    place.greet()
-    segs = [
-        Gather(place, ref, sems[2 * i], sems[2 * i + 1], kind)
-        for i, (ref, kind) in enumerate(
-            ((g_small, "small"), (g_attn, "panels"), (g_inner, "panels"), (g_outer, "rows")))
-    ]
-    groups = [segs[:2], segs[2:3], segs[3:]]
-    for group in groups:
-        for seg in group:
-            seg.begin()
-        for dz in range(1, place.nz):
-            for seg in group:
-                seg.column(dz)
-        for dz in range(place.nz):
-            for seg in group:
-                seg.plane(dz)
-        for dz in range(place.nz):
-            for seg in group:
-                seg.corner(dz)
-    for seg in segs:
-        seg.finish_core()
-    for seg in segs:
-        seg.drain()
-
-
-def gather_weights(pages, wq, wk, wv, wo, wi, wout, small):
-    rows, width = wq.shape
-    devices = 2 * pages
-    panels = wi.shape[1] // width
-    _, slots = gather_slots(pages)
-    v = pl.BlockSpec(memory_space=VMEM)
-    return pl.pallas_call(
-        functools.partial(gather_kernel, pages),
-        name="gather_weights",
-        out_shape=(
-            jax.ShapeDtypeStruct((4, devices, rows, width), BF),
-            jax.ShapeDtypeStruct((panels, devices, rows, width), BF),
-            jax.ShapeDtypeStruct((1, devices, wout.shape[0], width), BF),
-            jax.ShapeDtypeStruct((1, devices) + small.shape, BF),
-        ),
-        in_specs=[v] * 7,
-        out_specs=(v,) * 4,
-        scratch_shapes=[DMA((slots,))] * 8,
-        compiler_params=pltpu.CompilerParams(collective_id=0, has_side_effects=True, vmem_limit_bytes=40 << 20),
-    )(wq, wk, wv, wo, wi, wout, small)
 
 
 def reduce_slots(pages):
@@ -256,7 +201,7 @@
 def reduce_scratch(pages, panels, rows, width, kind):
     nz, ny, nx = page_grid(pages)
     fx, fy = nx - 1, ny - 1
-    half = (panels // 2, rows) if kind == "panels" else (panels, rows // 2)
+    half = (panels // 2, rows) if kind == PANELS else (panels, rows // 2)
     _, slots = reduce_slots(pages)
     return [
         VMEM((panels, nz * ny * nx, rows, width), BF),
@@ -283,7 +228,7 @@
             device_id=target, device_id_type=MESH)
 
     def half(self, page, which):
-        if self.kind == "panels":
+        if self.kind == PANELS:
             n = self.total.shape[0] // 2
             return self.total.at[which * n:(which + 1) * n, page]
         n = self.total.shape[2] // 2
@@ -292,7 +237,7 @@
     def core_copy(self, dz, dy, dx):
         p = self.pl
         page = p.page(dz, dy, dx)
-        return self.remote("core", (dz * p.ny + dy) * p.nx + dx, self.part.at[:, page, 1 - p.c], self.total.at[:, page], (p.p, 1 - p.c))
+        return self.remote("core", (dz * p.ny + dy) * p.nx + dx, self.part.at[:, 2 * page + 1 - p.c], self.total.at[:, page], (p.p, 1 - p.c))
 
     def diag(self, dz, dy, dx):
         p = self.pl
@@ -320,19 +265,18 @@
         p = self.pl
         return self.remote("z", dz - 1, self.total.at[:, p.page(dz, 0, 0)], self.rz.at[dz - 1], (p.page(dz=dz), p.c))
 
-    def begin(self):
+    def begin(self, dz):
         p = self.pl
         order = [(dy, dx) for dy in range(1, p.ny) for dx in range(1, p.nx)]
         order += [(0, dx) for dx in range(1, p.nx)] + [(dy, 0) for dy in range(1, p.ny)] + [(0, 0)]
         for dy, dx in order:
-            for dz in range(p.nz):
-                self.core_copy(dz, dy, dx).start()
+            self.core_copy(dz, dy, dx).start()
 
     def pair(self, dz, dy, dx):
         p = self.pl
         self.core_copy(dz, dy, dx).wait_recv()
         page = p.page(dz, dy, dx)
-        return self.part[:, page, p.c].astype(F32) + self.total[:, page].astype(F32)
+        return self.part[:, 2 * page + p.c].astype(F32) + self.total[:, page].astype(F32)
 
     def corner(self, dz):
         p = self.pl
@@ -351,7 +295,7 @@
             for dy in range(1, p.ny):
                 self.yb_copy(dz, dy, dx).wait_recv()
                 add = self.db[self.diag(dz, dy, dx)].astype(F32)
-                if self.kind == "panels":
+                if self.kind == PANELS:
                     n = panels // 2
                     total = jnp.concatenate([total[:n], total[n:] + add], axis=0)
                 else:
@@ -365,7 +309,7 @@
             for dx in range(1, p.nx):
                 self.xa_copy(dz, dy, dx).wait_recv()
                 add = self.da[self.diag(dz, dy, dx)].astype(F32)
-                if self.kind == "panels":
+                if self.kind == PANELS:
                     n = panels // 2
                     total = jnp.concatenate([total[:n] + add, total[n:]], axis=0)
                 else:
@@ -467,18 +411,442 @@
                 copy.wait_send()
 
 
-def reduce_kernel(pages, p_attn, p_inner, p_outer, vec, o_q, o_k, o_v, o_o, o_inner, o_outer, o_vec, *scratch):
+HEADS = 12
+
+
+masked_value = -1e30
+norm_eps = 1e-06
+
+
+def layer_norm(values, norm_gain, norm_shift):
+    centre = jnp.mean(values, axis=-1, keepdims=True)
+    centered = values - centre
+    spread = jnp.mean(centered * centered, axis=-1, keepdims=True)
+    return centered * lax.rsqrt(spread + norm_eps) * norm_gain + norm_shift
+
+
+def gelu_exact(values):
+    return jax.nn.gelu(values, approximate=False)
+
+
+def matmul(left_side, right_side):
+    return jnp.dot(left_side, right_side, preferred_element_type=jnp.float32)
+
+
+def column_sum(values):
+    return jnp.sum(values.astype(jnp.float32), axis=0)
+
+
+def usable_keys(page_lengths, seg_len):
+    places = lax.broadcasted_iota(jnp.int32, (page_lengths.shape[0], seg_len), 1)
+    return places < page_lengths[:, None]
+
+
+def head_split(values, head_count):
+    return values.reshape(
+        values.shape[0], values.shape[1], head_count, values.shape[2] // head_count
+    )
+
+
+def page_scores(query_heads, key_piece, usable, score_scale):
+    key_heads = head_split(key_piece, query_heads.shape[2])
+    scores = (
+        jnp.einsum("pqhd,pkhd->phqk", query_heads, key_heads, preferred_element_type=jnp.float32)
+        * score_scale
+    )
+    return jnp.where(usable[:, None, None, :], scores, masked_value)
+
+
+VECTORS = 8
+
+
+def pack_vectors(vectors, inner):
+    lanes = 128
+    rows = [jnp.pad(v, (0, lanes - v.shape[0])) for v in (*vectors, inner)]
+    rows += [jnp.zeros((lanes,), BF)] * (16 - len(rows))
+    return jnp.stack(rows)
+
+
+LOG2E = 1.4426950408889634
+LANES = 128
+VEC_ROWS = 16
+NT = ((1,), (1,))
+TN = ((0,), (0,))
+
+
+def steps_loop(count, body, steps):
+    def one(i, _):
+        body(i)
+        for at, todo in steps.items():
+            def run(todo=todo):
+                for step in todo:
+                    step()
+            pl.when(i == at)(run)
+        return 0
+
+    lax.fori_loop(0, count, one, 0)
+
+
+def dot(left, right, dims=((1,), (0,))):
+    return lax.dot_general(left, right, (dims, ((), ())), preferred_element_type=F32)
+
+
+def standardize(values):
+    centered = values - jnp.mean(values, axis=-1, keepdims=True)
+    r = lax.rsqrt(jnp.mean(centered * centered, axis=-1, keepdims=True) + norm_eps)
+    return centered * r, r
+
+
+def norm_back(grad, xhat, r, gain):
+    e = grad * gain
+    return r * (e - jnp.mean(e, axis=-1, keepdims=True) - xhat * jnp.mean(e * xhat, axis=-1, keepdims=True))
+
+
+def add_row(ref, row, values):
+    ref[row:row + 1, :] += jnp.sum(values, axis=0, keepdims=True)
+
+
+def spread_lanes(small, n, width, first):
+    devices, vectors, lanes = small.shape
+    column = (first + lax.broadcasted_iota(jnp.int32, (lanes, width), 1)).astype(F32)
+    owner = jnp.floor((column + 0.5) * (1.0 / n))
+    lane = lax.broadcasted_iota(jnp.int32, (lanes, width), 0).astype(F32)
+    pick = jnp.where(column - owner * n == lane, 1.0, 0.0).astype(BF)
+    values = dot(small.reshape(devices * vectors, lanes), pick).reshape(devices, vectors, width)
+    device = lax.broadcasted_iota(jnp.int32, (devices, vectors, width), 0).astype(F32)
+    return jnp.sum(jnp.where(owner[:1][None] == device, values, 0.0), axis=0)
+
+
+def layer_scratch(pages, rows, width, panels, tokens, local_pages):
+    devices = 2 * pages
+    _, gs = gather_slots(pages)
+    seg = tokens // local_pages
+    own = dict(
+        g_attn=VMEM((4, devices, rows, width), BF),
+        g_inner=VMEM((panels, devices, rows, width), BF),
+        g_outer=VMEM((1, devices, panels * rows, width), BF),
+        g_small=VMEM((1, devices, VEC_ROWS, LANES), BF),
+        p_one=VMEM((2, devices, rows, width), BF),
+        p_two=VMEM((2, devices, rows, width), BF),
+        xs=VMEM((tokens, width), BF),
+        q=VMEM((tokens, width), BF),
+        k=VMEM((local_pages, 2 * seg, width), BF),
+        v=VMEM((local_pages, 2 * seg, width), BF),
+        ctx=VMEM((tokens, width), BF),
+        xhat=VMEM((tokens, width), F32),
+        r_one=VMEM((tokens, 1), F32),
+        low=VMEM((tokens, width), BF),
+        post=VMEM((panels, tokens, width), BF),
+        slope=VMEM((panels, tokens, width), BF),
+        res=VMEM((tokens, width), F32),
+        d_low=VMEM((tokens, width), BF),
+        vec=VMEM((VEC_ROWS, width), F32),
+        par=VMEM((VEC_ROWS, width), F32),
+        rk=VMEM((local_pages, seg, width), BF),
+        rv=VMEM((local_pages, seg, width), BF),
+        x_sem=DMA((2,)),
+        kv_sem=DMA((4, local_pages)),
+    )
+    gather = [DMA((gs,))] * 8
+    reduce = []
+    for count, size, kind in ((1, panels * rows, ROWS), (panels, rows, PANELS), (2, rows, PANELS), (2, rows, PANELS)):
+        reduce += reduce_scratch(pages, count, size, width, kind)
+    return own, gather + reduce + vector_scratch(pages, VEC_ROWS, width)
+
+
+def layer_kernel(pages, heads, names, lengths, x, cot, wq, wk, wv, wo, wi, wout, small,
+                 layer_out, hidden_grad, o_q, o_k, o_v, o_o, o_inner, o_outer, o_vec, *scratch):
+    s = types.SimpleNamespace(**dict(zip(names, scratch)))
+    s.d_ctx = s.xs
+    rest = scratch[len(names):]
     place = Place(pages)
-    outer = Reduce(place, p_outer, scratch[0:8], "rows")
-    inner = Reduce(place, p_inner, scratch[8:16], "panels")
-    attn = Reduce(place, p_attn, scratch[16:24], "panels")
-    vectors = VectorSum(place, scratch[24:28])
+    c, nz = place.c, place.nz
+    mine = 2 * place.p + c
+    sibling = (place.p, 1 - c)
+    tokens, width = x.shape
+    panels, devices, rows = s.g_inner.shape[:3]
+    local_pages, page_len = s.k.shape[:2]
+    seg = tokens // local_pages
+    full = (width, width)
+    scale = (width // heads) ** -0.5
+    q, k, v, ctx, res, par, vec = s.q, s.k, s.v, s.ctx, s.res, s.par, s.vec
+
+    for j, ref in enumerate((wq, wk, wv, wo)):
+        s.g_attn[j, mine] = ref[...]
+    for j in range(panels):
+        s.g_inner[j, mine] = wi[:, j * width:(j + 1) * width]
+    s.g_outer[0, mine] = wout[...]
+    s.g_small[0, mine] = small[...]
     place.greet()
-    nz = place.nz
-    segs = (outer, inner, attn)
+    x_copy = pltpu.make_async_remote_copy(
+        src_ref=x, dst_ref=s.xs, send_sem=s.x_sem.at[0], recv_sem=s.x_sem.at[1],
+        device_id=sibling, device_id_type=MESH)
+    x_copy.start()
+    tiny, attn, inner, outer = (
+        Gather(place, ref, rest[2 * i], rest[2 * i + 1], kind)
+        for i, (ref, kind) in enumerate(((s.g_small, SMALL), (s.g_attn, PANELS), (s.g_inner, PANELS), (s.g_outer, ROWS))))
+    first = (tiny, attn)
+    for one in (tiny, attn, inner, outer):
+        one.begin_z()
+    for one in first:
+        one.spread(0)
+    for dz in range(1, nz):
+        for one in first:
+            one.column(dz)
+    for dz in range(nz):
+        for one in first:
+            one.plane(dz)
+    inner.spread(0)
+    for dz in range(1, nz):
+        inner.column(dz)
+    for dz in range(nz):
+        for one in first:
+            one.corner(dz)
+    for one in first:
+        one.finish_core()
+    x_copy.wait()
+
+    def weight(ref, j):
+        return ref[j].reshape(full)
+
+    def outer_weight(j):
+        n = devices // panels
+        return s.g_outer[0, pl.ds(j * n, n)].reshape(full)
+
+    gathered = s.g_small[0]
+    par[...] = spread_lanes(gathered, rows, width, 0)
+    for j in range(panels):
+        par[VECTORS + j:VECTORS + j + 1, :] = spread_lanes(gathered, panels * rows, width, j * width)[VECTORS:VECTORS + 1]
+    vec[...] = jnp.zeros_like(vec)
+
+    def vector(j):
+        return par[j:j + 1, :]
+
+    q[...] = (dot(x[...], weight(s.g_attn, 0)) + vector(0)).astype(BF)
+    inner.plane(0)
+
+    def project(i, _):
+        ref, half = (x, c) if i == 0 else (s.xs, 1 - c)
+        rows_of = pl.ds(pl.multiple_of(half * seg, seg), seg)
+        k[:, rows_of, :] = dot(ref[...], weight(s.g_attn, 1)).astype(BF).reshape(local_pages, seg, width)
+        v[:, rows_of, :] = (dot(ref[...], weight(s.g_attn, 2)) + vector(1)).astype(BF).reshape(local_pages, seg, width)
+
+    project(0, 0)
+    inner.plane(1)
+    project(1, 0)
+    inner.plane(2)
+
+    pairs = heads // 2
+    head_dim = width // heads
+
+    def place_of(i):
+        page, pair = i // pairs, lax.rem(i, pairs)
+        return page, pl.ds(pl.multiple_of(page * seg, seg), seg), pl.ds(pl.multiple_of(pair * LANES, LANES), LANES)
+
+    low_half = lax.broadcasted_iota(jnp.int32, (1, LANES), 1) < head_dim
+    key_at = lax.broadcasted_iota(jnp.int32, (1, page_len), 1)
+
+    def one_head(values, head):
+        return jnp.where(low_half if head == 0 else jnp.logical_not(low_half), values, jnp.zeros_like(values))
+
+    def probabilities(q2, k2, head, usable):
+        t = jnp.where(usable, dot(q2, one_head(k2, head), NT) * (scale * LOG2E), masked_value)
+        e = jnp.exp2(t - jnp.max(t, axis=-1, keepdims=True))
+        return e * (1.0 / jnp.sum(e, axis=-1, keepdims=True))
+
+    def attend(i):
+        page, rows_of, cols = place_of(i)
+        q2, k2, v2 = q[rows_of, cols], k[page, :, cols], v[page, :, cols]
+        usable = key_at < lengths[page]
+        parts = [dot(probabilities(q2, k2, head, usable).astype(BF), v2) for head in range(2)]
+        ctx[rows_of, cols] = jnp.where(low_half, *parts).astype(BF)
+
+    steps_loop(local_pages * pairs, attend, {
+        0: [lambda: inner.plane(3), lambda: outer.spread(0)],
+        1: [lambda: outer.column(1)],
+        2: [lambda: outer.column(2)],
+        3: [lambda: outer.column(3)],
+        4: [lambda: inner.corner(0)],
+        5: [lambda: inner.corner(1)],
+        6: [lambda: inner.corner(2)],
+        7: [lambda: inner.corner(3)],
+        8: [lambda: outer.plane(0)],
+        9: [lambda: outer.plane(1)],
+        10: [lambda: outer.plane(2)],
+        11: [lambda: outer.plane(3)],
+    })
+
+    res[...] = dot(ctx[...], weight(s.g_attn, 3))
+    chunk = 128
+
+    def chunks(body):
+        def one(i, _):
+            body(pl.ds(pl.multiple_of(i * chunk, chunk), chunk))
+            return 0
+        lax.fori_loop(0, tokens // chunk, one, 0)
+
+    def norm_one(at):
+        xhat, r = standardize(x[at, :].astype(F32) + res[at, :] + vector(2))
+        s.xhat[at, :] = xhat
+        s.r_one[at, :] = r
+        normed = xhat * vector(3) + vector(4)
+        s.low[at, :] = normed.astype(BF)
+        res[at, :] = normed + vector(5)
+
+    chunks(norm_one)
+
+    inner.finish_core()
+    root_half = 0.7071067811865476
+
+    def expand(j):
+        pre = dot(s.low[...], weight(s.g_inner, j)) + par[pl.ds(VECTORS + j, 1), :]
+        half_one = 0.5 * (1.0 + lax.erf(pre * root_half))
+        bell = jnp.exp2(pre * pre * (-0.5 * LOG2E)) * 0.3989422804014327
+        s.post[j] = (pre * half_one).astype(BF)
+        s.slope[j] = (half_one + pre * bell).astype(BF)
+
+    steps_loop(panels, expand, {j: [lambda j=j: outer.corner(j)] for j in range(nz)})
+    outer.finish_core()
+
+    def contract(j, _):
+        res[...] += dot(s.post[j], outer_weight(j))
+        return 0
+
+    lax.fori_loop(0, panels, contract, 0)
+
+    def norm_two(at):
+        xhat, r = standardize(res[at, :])
+        layer_out[at, :] = (xhat * vector(6) + vector(7)).astype(BF)
+        grad = cot[at, :].astype(F32)
+        add_row(vec, 6, grad * xhat)
+        add_row(vec, 7, grad)
+        d_res = norm_back(grad, xhat, r, vector(6))
+        res[at, :] = d_res
+        d_low = d_res.astype(BF)
+        s.d_low[at, :] = d_low
+        add_row(vec, 5, d_low.astype(F32))
+
+    chunks(norm_two)
+
+    reducers = [
+        Reduce(place, part, rest[8 + 8 * i:16 + 8 * i], kind)
+        for i, (part, kind) in enumerate(((s.g_outer, ROWS), (s.g_inner, PANELS), (s.p_one, PANELS), (s.p_two, PANELS)))]
+    r_outer, r_inner, r_first, r_second = reducers
+    outer.drain()
+
+    def outer_back(dz):
+        j = lax.rem(place.z + dz, nz)
+        d_low = s.d_low[...]
+        d_pre = (dot(d_low, outer_weight(j), NT) * s.slope[j].astype(F32)).astype(BF)
+        n = devices // panels
+        s.g_outer[0, pl.ds(j * n, n)] = dot(s.post[j], d_low, TN).reshape(n, panels * rows, width).astype(BF)
+        r_outer.begin(dz)
+        s.slope[j] = d_pre
+        vec[pl.ds(VECTORS + j, 1), :] = jnp.sum(d_pre.astype(F32), axis=0, keepdims=True)
+
+    steps_loop(nz, outer_back, {
+        1: [lambda: r_outer.corner(0)],
+        2: [lambda: r_outer.corner(1)],
+        3: [lambda: r_outer.corner(2)],
+    })
+    inner.drain()
+
+    def inner_back(j):
+        d_pre = s.slope[j]
+        res[...] += dot(d_pre, weight(s.g_inner, j), NT)
+        s.g_inner[j] = dot(s.low[...], d_pre, TN).reshape(devices, rows, width).astype(BF)
+
+    steps_loop(panels, inner_back, {
+        0: [lambda: r_outer.corner(3), lambda: r_outer.plane(0)],
+        1: [lambda: r_outer.plane(1)],
+        2: [lambda: r_outer.plane(2)],
+        3: [lambda: r_outer.plane(3)],
+    })
+    for dz in range(nz):
+        r_inner.begin(dz)
+
+    def norm_one_back(at):
+        grad, xhat = res[at, :], s.xhat[at, :]
+        add_row(vec, 3, grad * xhat)
+        add_row(vec, 4, grad)
+        d_res = norm_back(grad, xhat, s.r_one[at, :], vector(3))
+        res[at, :] = d_res
+        d_low = d_res.astype(BF)
+        s.d_low[at, :] = d_low
+        add_row(vec, 2, d_low.astype(F32))
+
+    chunks(norm_one_back)
+    s.d_ctx[...] = dot(s.d_low[...], weight(s.g_attn, 3), NT).astype(BF)
+    s.p_one[0] = dot(ctx[...], s.d_low[...], TN).reshape(devices, rows, width).astype(BF)
+    r_inner.corner(0)
+    r_inner.corner(1)
+
+    d_q, d_k, d_v = s.post.at[0], s.post.at[1:1 + local_pages], s.slope.at[0:local_pages]
+
+    def kv_copies(page):
+        theirs = pl.ds(pl.multiple_of((1 - c) * seg, seg), seg)
+        return [
+            pltpu.make_async_remote_copy(
+                src_ref=grad.at[page, theirs], dst_ref=got.at[page], send_sem=s.kv_sem.at[2 * n, page],
+                recv_sem=s.kv_sem.at[2 * n + 1, page], device_id=sibling, device_id_type=MESH)
+            for n, (grad, got) in enumerate(((d_k, s.rk), (d_v, s.rv)))]
+
+    def attend_back(i):
+        page, rows_of, cols = place_of(i)
+        q2, k2, v2 = q[rows_of, cols], k[page, :, cols], v[page, :, cols]
+        c2 = s.d_ctx[rows_of, cols]
+        usable = key_at < lengths[page]
+        parts = []
+        for head in range(2):
+            p = probabilities(q2, k2, head, usable)
+            d_p = dot(c2, one_head(v2, head), NT)
+            d_s = (p * (d_p - jnp.sum(p * d_p, axis=-1, keepdims=True))).astype(BF)
+            parts.append((dot(d_s, k2), dot(d_s, q2, TN), dot(p.astype(BF), c2, TN)))
+        both = [jnp.where(low_half, one, two) for one, two in zip(*parts)]
+        d_q[rows_of, cols] = (both[0] * scale).astype(BF)
+        d_k[page, :, cols] = (both[1] * scale).astype(BF)
+        d_v[page, :, cols] = both[2].astype(BF)
+
+    def send_kv(page):
+        for copy in kv_copies(page):
+            copy.start()
+
+    def finish_outer():
+        o_outer[...] = r_outer.finish()[0]
+
+    steps_loop(local_pages * pairs, attend_back, {
+        0: [lambda: r_inner.corner(2)],
+        1: [lambda: r_inner.corner(3)],
+        2: [lambda: r_outer.column(1)],
+        3: [lambda: r_outer.column(2)],
+        4: [lambda: r_outer.column(3)],
+        5: [lambda: r_inner.plane(0)],
+        6: [lambda: r_inner.plane(1)],
+        7: [lambda: r_inner.plane(2)],
+        8: [lambda: r_inner.plane(3)],
+        9: [finish_outer],
+    })
+    for page in range(local_pages):
+        send_kv(page)
+    s.p_one[1] = dot(x[...], d_q[...], TN).reshape(devices, rows, width).astype(BF)
+    for dz in range(nz):
+        r_first.begin(dz)
+    add_row(vec, 0, d_q[...].astype(F32))
+    for page in range(local_pages):
+        for copy in kv_copies(page):
+            copy.wait()
+    ours = pl.ds(pl.multiple_of(c * seg, seg), seg)
+    for j, (grad, got) in enumerate(((d_k, s.rk), (d_v, s.rv))):
+        total = (grad[:, ours, :].astype(F32) + got[...].astype(F32)).astype(BF)
+        got[...] = total
+        total = total.reshape(tokens, width)
+        if j == 1:
+            add_row(vec, 1, total.astype(F32))
+        s.p_two[j] = dot(x[...], total, TN).reshape(devices, rows, width).astype(BF)
+    vectors = VectorSum(place, rest[40:44])
     vectors.put(0, vec[...])
-    for seg in segs:
-        seg.begin()
+    for dz in range(nz):
+        r_second.begin(dz)
 
     def loop(start, body):
         def one(dz, _):
@@ -486,151 +854,59 @@
             return 0
         lax.fori_loop(start, nz, one, 0)
 
-    loop(0, outer.corner)
+    loop(0, r_first.corner)
+    loop(1, r_inner.column)
     vectors.put(1, vectors.take(0))
-    loop(0, inner.corner)
-    loop(0, outer.plane)
+    loop(0, r_second.corner)
     vectors.put(2, vectors.take(1))
-    loop(0, attn.corner)
-    loop(0, inner.plane)
+    loop(0, r_first.plane)
     vectors.put(3, vectors.take(2))
-    loop(1, outer.column)
-    loop(0, attn.plane)
-    loop(1, inner.column)
-    o_outer[...] = outer.finish()[0]
+    loop(0, r_second.plane)
+    d_keys, d_values = s.rk[...].reshape(tokens, width), s.rv[...].reshape(tokens, width)
+    res[...] += dot(d_q[...], weight(s.g_attn, 0), NT)
+    res[...] += dot(d_keys, weight(s.g_attn, 1), NT)
+    hidden_grad[...] = (res[...] + dot(d_values, weight(s.g_attn, 2), NT)).astype(BF)
+    total = r_inner.finish()
+    for j in range(panels):
+        o_inner[:, j * width:(j + 1) * width] = total[j]
+    loop(1, r_first.column)
+    loop(1, r_second.column)
     o_vec[...] = vectors.take(3)
-    loop(1, attn.column)
-    total = inner.finish()
-    width = total.shape[2]
-    for j in range(total.shape[0]):
-        o_inner[:, j * width:(j + 1) * width] = total[j]
-    total = attn.finish()
-    for j, ref in enumerate((o_q, o_k, o_v, o_o)):
-        ref[...] = total[j]
-    for seg in segs:
-        seg.drain()
+    total = r_first.finish()
+    o_o[...] = total[0]
+    o_q[...] = total[1]
+    total = r_second.finish()
+    o_k[...] = total[0]
+    o_v[...] = total[1]
+    tiny.drain()
+    attn.drain()
+    for one in reducers:
+        one.drain()
     vectors.drain()
 
 
-def reduce_grads(pages, p_attn, p_inner, p_outer, vec):
-    panels, width = p_inner.shape[0], p_inner.shape[4]
-    rows, rows_outer = p_inner.shape[3], p_outer.shape[3]
-    v = pl.BlockSpec(memory_space=VMEM)
+def whole_layer(pages, heads, lengths, x, cot, wq, wk, wv, wo, wi, wout, small, local_pages):
+    tokens, width = x.shape
+    rows, panels = wq.shape[0], wi.shape[1] // width
+    own, scratch = layer_scratch(pages, rows, width, panels, tokens, local_pages)
+    vm = pl.BlockSpec(memory_space=VMEM)
+    row_shape = jax.ShapeDtypeStruct((tokens, width), BF)
     square = jax.ShapeDtypeStruct((rows, width), F32)
     return pl.pallas_call(
-        functools.partial(reduce_kernel, pages),
-        name="reduce_grads",
-        out_shape=(square,) * 4 + (
-            jax.ShapeDtypeStruct((rows, panels * width), F32),
-            jax.ShapeDtypeStruct((rows_outer, width), F32),
-            jax.ShapeDtypeStruct(vec.shape, F32),
-        ),
-        in_specs=[v] * 4,
-        out_specs=(v,) * 7,
-        scratch_shapes=reduce_scratch(pages, 1, rows_outer, width, "rows")
-        + reduce_scratch(pages, panels, rows, width, "panels")
-        + reduce_scratch(pages, 4, rows, width, "panels")
-        + vector_scratch(pages, *vec.shape),
-        compiler_params=pltpu.CompilerParams(collective_id=1, has_side_effects=True, vmem_limit_bytes=56 << 20),
-    )(p_attn, p_inner, p_outer, vec)
-
-
-HEADS = 12
-
-
-masked_value = -1e30
-norm_eps = 1e-06
-
-
-def layer_norm(values, norm_gain, norm_shift):
-    centre = jnp.mean(values, axis=-1, keepdims=True)
-    centered = values - centre
-    spread = jnp.mean(centered * centered, axis=-1, keepdims=True)
-    return centered * lax.rsqrt(spread + norm_eps) * norm_gain + norm_shift
-
-
-def gelu_exact(values):
-    return jax.nn.gelu(values, approximate=False)
-
-
-def matmul(left_side, right_side):
-    return jnp.dot(left_side, right_side, preferred_element_type=jnp.float32)
-
-
-def column_sum(values):
-    return jnp.sum(values.astype(jnp.float32), axis=0)
-
-
-def usable_keys(page_lengths, seg_len):
-    places = lax.broadcasted_iota(jnp.int32, (page_lengths.shape[0], seg_len), 1)
-    return places < page_lengths[:, None]
-
-
-def head_split(values, head_count):
-    return values.reshape(
-        values.shape[0], values.shape[1], head_count, values.shape[2] // head_count
-    )
-
-
-def page_scores(query_heads, key_piece, usable, score_scale):
-    key_heads = head_split(key_piece, query_heads.shape[2])
-    scores = (
-        jnp.einsum("pqhd,pkhd->phqk", query_heads, key_heads, preferred_element_type=jnp.float32)
-        * score_scale
-    )
-    return jnp.where(usable[:, None, None, :], scores, masked_value)
-
-
-AXES = ("page", "seq")
-VECTORS = 8
-
-
-def pack_vectors(vectors, inner):
-    lanes = 128
-    rows = [jnp.pad(v, (0, lanes - v.shape[0])) for v in (*vectors, inner)]
-    rows += [jnp.zeros((lanes,), BF)] * (16 - len(rows))
-    return jnp.stack(rows)
-
-
-def unpack_vectors(small, rows):
-    vectors = [small[:, j, :rows].reshape(-1) for j in range(VECTORS)]
-    return vectors + [small[:, VECTORS, : 4 * rows].reshape(-1)]
-
-
-def gather_all(pages, wq, wk, wv, wo, wi, wout, vectors, b_inner):
-    rows, width = wq.shape
-    panels = wi.shape[1] // width
-    if rows % 8 == 0:
-        small = pack_vectors(vectors, b_inner)
-        ga, gi, go, gs = gather_weights(pages, wq, wk, wv, wo, wi, wout, small)
-        full = width, width
-        return ga.reshape(4, *full), gi.reshape(panels, *full), go.reshape(-1, width), unpack_vectors(gs[0], rows)
-    spread = lambda w: lax.all_gather(w, AXES, axis=0, tiled=True)
-    ga = lax.all_gather(jnp.stack((wq, wk, wv, wo)), AXES, axis=1, tiled=True)
-    gi = lax.all_gather(wi.reshape(rows, panels, width).transpose(1, 0, 2), AXES, axis=1, tiled=True)
-    return ga, gi, spread(wout), [spread(v) for v in (*vectors, b_inner)]
-
-
-def reduce_all(pages, pa, pi, po, vec):
-    panels, width = pi.shape[0], pi.shape[2]
-    rows = width // (2 * pages)
-    at = lax.axis_index("page") * 2 + lax.axis_index("seq")
-    if rows % 8 == 0:
-        split = lambda p: p.reshape(p.shape[0], pages, 2, -1, width)
-        *squares, o_inner, o_outer, total = reduce_grads(pages, split(pa), split(pi), split(po[None]), vec)
-    else:
-        scatter = lambda g, d: lax.psum_scatter(g.astype(F32), AXES, scatter_dimension=d, tiled=True)
-        squares = list(scatter(pa, 1))
-        o_inner = scatter(pi, 1).transpose(1, 0, 2).reshape(rows, -1)
-        o_outer = scatter(po, 0)
-        total = lax.psum(vec, AXES)
-    vectors = [lax.dynamic_slice(total, (j, rows * at), (1, rows))[0] for j in range(VECTORS)]
-    flat = total[VECTORS : VECTORS + panels].reshape(-1)
-    return squares, o_inner, o_outer, vectors, lax.dynamic_slice(flat, (panels * rows * at,), (panels * rows,))
-
-
-def per_device(
-    page_count,
+        functools.partial(layer_kernel, pages, heads, tuple(own)),
+        name="whole_layer",
+        out_shape=(row_shape, row_shape, square, square, square, square,
+                   jax.ShapeDtypeStruct((rows, panels * width), F32),
+                   jax.ShapeDtypeStruct((panels * rows, width), F32),
+                   jax.ShapeDtypeStruct((VEC_ROWS, width), F32)),
+        in_specs=[pl.BlockSpec(memory_space=pltpu.SMEM)] + [vm] * 9,
+        out_specs=(vm,) * 9,
+        scratch_shapes=[*own.values(), *scratch],
+        compiler_params=pltpu.CompilerParams(collective_id=0, has_side_effects=True, vmem_limit_bytes=61 << 20),
+    )(lengths, x, cot, wq, wk, wv, wo, wi, wout, small)
+
+
+def plain_layer(
     hidden,
     lengths,
     w_query,
@@ -658,14 +934,27 @@
     work_hidden, work_cot = (hidden, cotangent)
     local_pages, local_tokens = (work_hidden.shape[0], work_hidden.shape[1])
     row_count = local_pages * local_tokens
-    pages = page_count
-    ga, gi, go, vectors = gather_all(
-        pages, w_query, w_key, w_value, w_output, w_inner, w_outer,
-        (b_query, b_value, b_output, attn_gain, attn_shift, b_outer, ffn_gain, ffn_shift), b_inner)
-    query_full, key_full, value_full, output_full = ga[0], ga[1], ga[2], ga[3]
-    query_bias, value_bias, output_bias, gain_one, shift_one, outer_bias, gain_two, shift_two, inner_bias = vectors
-    outer_full = go
-    panels = gi.shape[0]
+    (
+        query_full,
+        key_full,
+        value_full,
+        output_full,
+        query_bias,
+        value_bias,
+        output_bias,
+        gain_one,
+        shift_one,
+    ) = (
+        lax.all_gather(w_query, AXES, axis=0, tiled=True),
+        lax.all_gather(w_key, AXES, axis=0, tiled=True),
+        lax.all_gather(w_value, AXES, axis=0, tiled=True),
+        lax.all_gather(w_output, AXES, axis=0, tiled=True),
+        lax.all_gather(b_query, AXES, axis=0, tiled=True),
+        lax.all_gather(b_value, AXES, axis=0, tiled=True),
+        lax.all_gather(b_output, AXES, axis=0, tiled=True),
+        lax.all_gather(attn_gain, AXES, axis=0, tiled=True),
+        lax.all_gather(attn_shift, AXES, axis=0, tiled=True),
+    )
     flat_rows = work_hidden.reshape(row_count, model_width)
     queries = (matmul(flat_rows, query_full) + query_bias.astype(f32)).astype(bf16)
     key_rows = matmul(flat_rows, key_full).astype(bf16)
@@ -675,7 +964,7 @@
     value_pages = value_rows.reshape(local_pages, local_tokens, model_width)
     stat_shape = (local_pages, head_count, local_tokens)
     stat_start = (jnp.full(stat_shape, masked_value, f32), jnp.zeros(stat_shape, f32))
-    key_piece = lax.all_gather(key_pages, "seq", axis=1, tiled=True)
+    key_piece = lax.all_gather(key_pages, SEQ, axis=1, tiled=True)
     usable = usable_keys(lengths, key_piece.shape[1])
 
     def merged():
@@ -687,8 +976,8 @@
 
     run_peak, run_total = merged()
     log_norm = run_peak + jnp.log(run_total)
-    add_key_piece = lax.all_gather(key_pages, "seq", axis=1, tiled=True)
-    value_piece = lax.all_gather(value_pages, "seq", axis=1, tiled=True)
+    add_key_piece = lax.all_gather(key_pages, SEQ, axis=1, tiled=True)
+    value_piece = lax.all_gather(value_pages, SEQ, axis=1, tiled=True)
     add_usable = usable_keys(lengths, add_key_piece.shape[1])
 
     def merged():
@@ -710,8 +999,15 @@
     normed_one, pull_one = jax.vjp(
         layer_norm, residual_one, gain_one.astype(f32), shift_one.astype(f32)
     )
+    inner_full, outer_full, inner_bias, outer_bias, gain_two, shift_two = (
+        lax.all_gather(w_inner, AXES, axis=0, tiled=True),
+        lax.all_gather(w_outer, AXES, axis=0, tiled=True),
+        lax.all_gather(b_inner, AXES, axis=0, tiled=True),
+        lax.all_gather(b_outer, AXES, axis=0, tiled=True),
+        lax.all_gather(ffn_gain, AXES, axis=0, tiled=True),
+        lax.all_gather(ffn_shift, AXES, axis=0, tiled=True),
+    )
     normed_low = normed_one.astype(bf16)
-    inner_full = gi.transpose(1, 0, 2).reshape(model_width, -1)
     pre_gelu = matmul(normed_low, inner_full) + inner_bias.astype(f32)
     post_gelu, pull_gelu = jax.vjp(gelu_exact, pre_gelu)
     post_low = post_gelu.astype(bf16)
@@ -730,6 +1026,14 @@
     inner_b_grad = column_sum(d_pre)
     d_normed = d_res_two + matmul(d_pre, inner_full.T)
     d_res_one, gain_one_grad, shift_one_grad = pull_one(d_normed)
+    ffn_owned = (
+        lax.psum_scatter(inner_w_grad, AXES, scatter_dimension=0, tiled=True),
+        lax.psum_scatter(outer_w_grad, AXES, scatter_dimension=0, tiled=True),
+        lax.psum_scatter(inner_b_grad, AXES, scatter_dimension=0, tiled=True),
+        lax.psum_scatter(outer_b_grad, AXES, scatter_dimension=0, tiled=True),
+        lax.psum_scatter(gain_two_grad, AXES, scatter_dimension=0, tiled=True),
+        lax.psum_scatter(shift_two_grad, AXES, scatter_dimension=0, tiled=True),
+    )
     d_attn = d_res_one.astype(bf16)
     output_w_grad = matmul(context_low.T, d_attn)
     output_b_grad = column_sum(d_attn)
@@ -777,16 +1081,16 @@
 
     query_grad, key_grads, value_grads = add_grads(
         (
-            lax.all_gather(key_pages, "seq", axis=1, tiled=True),
-            lax.all_gather(value_pages, "seq", axis=1, tiled=True),
+            lax.all_gather(key_pages, SEQ, axis=1, tiled=True),
+            lax.all_gather(value_pages, SEQ, axis=1, tiled=True),
         )
     )
     key_owned, value_owned = (
         lax.psum_scatter(
-            key_grads.astype(jnp.bfloat16), "seq", scatter_dimension=1, tiled=True
+            key_grads.astype(jnp.bfloat16), SEQ, scatter_dimension=1, tiled=True
         ).astype(jnp.float32),
         lax.psum_scatter(
-            value_grads.astype(jnp.bfloat16), "seq", scatter_dimension=1, tiled=True
+            value_grads.astype(jnp.bfloat16), SEQ, scatter_dimension=1, tiled=True
         ).astype(jnp.float32),
     )
     d_queries = query_grad.astype(bf16).reshape(row_count, model_width)
@@ -803,60 +1107,100 @@
         + matmul(d_keys, key_full.T)
         + matmul(d_values, value_full.T)
     ).astype(bf16)
-    pa = jnp.stack([g.astype(bf16) for g in (query_w_grad, key_w_grad, value_w_grad, output_w_grad)])
-    pi = inner_w_grad.astype(bf16).reshape(model_width, panels, model_width).transpose(1, 0, 2)
-    po = outer_w_grad.astype(bf16)
-    singles = (query_b_grad, value_b_grad, output_b_grad, gain_one_grad, shift_one_grad, outer_b_grad, gain_two_grad, shift_two_grad)
-    vec = jnp.concatenate([jnp.stack(singles), inner_b_grad.reshape(panels, model_width)])
-    vec = jnp.pad(vec, ((0, 16 - vec.shape[0]), (0, 0)))
-    squares, o_inner, o_outer, owned, o_inner_bias = reduce_all(pages, pa, pi, po, vec)
+    attn_owned = (
+        lax.psum_scatter(query_w_grad, AXES, scatter_dimension=0, tiled=True),
+        lax.psum_scatter(key_w_grad, AXES, scatter_dimension=0, tiled=True),
+        lax.psum_scatter(value_w_grad, AXES, scatter_dimension=0, tiled=True),
+        lax.psum_scatter(output_w_grad, AXES, scatter_dimension=0, tiled=True),
+        lax.psum_scatter(query_b_grad, AXES, scatter_dimension=0, tiled=True),
+        lax.psum_scatter(value_b_grad, AXES, scatter_dimension=0, tiled=True),
+        lax.psum_scatter(output_b_grad, AXES, scatter_dimension=0, tiled=True),
+        lax.psum_scatter(gain_one_grad, AXES, scatter_dimension=0, tiled=True),
+        lax.psum_scatter(shift_one_grad, AXES, scatter_dimension=0, tiled=True),
+    )
     out_pages = layer_out.astype(bf16).reshape(local_pages, local_tokens, model_width)
     grad_pages = hidden_grad.reshape(local_pages, local_tokens, model_width)
     return (
-        out_pages, grad_pages, *squares, owned[0], owned[1], owned[2], owned[3], owned[4],
-        o_inner, o_inner_bias, o_outer, owned[5], owned[6], owned[7])
+        out_pages,
+        grad_pages,
+        attn_owned[0],
+        attn_owned[1],
+        attn_owned[2],
+        attn_owned[3],
+        attn_owned[4],
+        attn_owned[5],
+        attn_owned[6],
+        attn_owned[7],
+        attn_owned[8],
+        ffn_owned[0],
+        ffn_owned[2],
+        ffn_owned[1],
+        ffn_owned[3],
+        ffn_owned[4],
+        ffn_owned[5],
+    )
+
+
+def per_device(pages, hidden, lengths, w_query, w_key, w_value, w_output, b_query, b_value, b_output, attn_gain, attn_shift,
+               w_inner, b_inner, w_outer, b_outer, ffn_gain, ffn_shift, cotangent):
+    local_pages, seg, width = hidden.shape
+    rows, panels = w_query.shape[0], w_inner.shape[1] // width
+    nz, _, _ = page_grid(pages)
+    if rows % 8 or nz != panels or local_pages * seg != 2 * seg or 4 * rows > 128:
+        return plain_layer(hidden, lengths, w_query, w_key, w_value, w_output, b_query, b_value, b_output, attn_gain, attn_shift,
+                           w_inner, b_inner, w_outer, b_outer, ffn_gain, ffn_shift, cotangent)
+    small = pack_vectors((b_query, b_value, b_output, attn_gain, attn_shift, b_outer, ffn_gain, ffn_shift), b_inner)
+    flat = local_pages * seg, width
+    out, grad, g_q, g_k, g_v, g_o, g_inner, g_outer, total = whole_layer(
+        pages, HEADS, lengths, hidden.reshape(flat), cotangent.reshape(flat), w_query, w_key, w_value, w_output, w_inner, w_outer,
+        small, local_pages)
+    at = lax.axis_index(PAGE) * 2 + lax.axis_index(SEQ)
+    own = [lax.dynamic_slice(total, (j, rows * at), (1, rows))[0] for j in range(VECTORS)]
+    wide = lax.dynamic_slice(total[VECTORS:VECTORS + panels].reshape(-1), (panels * rows * at,), (panels * rows,))
+    return (out.reshape(hidden.shape), grad.reshape(hidden.shape), g_q, g_k, g_v, g_o, own[0], own[1], own[2], own[3], own[4],
+            g_inner, wide, g_outer, own[5], own[6], own[7])
 
 
 def solution(mesh):
     in_specs = (
-        P("page", "seq", None),
-        P("page"),
-        P(("page", "seq"), None),
-        P(("page", "seq"), None),
-        P(("page", "seq"), None),
-        P(("page", "seq"), None),
-        P(("page", "seq")),
-        P(("page", "seq")),
-        P(("page", "seq")),
-        P(("page", "seq")),
-        P(("page", "seq")),
-        P(("page", "seq"), None),
-        P(("page", "seq")),
-        P(("page", "seq"), None),
-        P(("page", "seq")),
-        P(("page", "seq")),
-        P(("page", "seq")),
-        P("page", "seq", None),
+        P(PAGE, SEQ, None),
+        P(PAGE),
+        P(AXES, None),
+        P(AXES, None),
+        P(AXES, None),
+        P(AXES, None),
+        P(AXES),
+        P(AXES),
+        P(AXES),
+        P(AXES),
+        P(AXES),
+        P(AXES, None),
+        P(AXES),
+        P(AXES, None),
+        P(AXES),
+        P(AXES),
+        P(AXES),
+        P(PAGE, SEQ, None),
     )
     out_specs = (
-        P("page", "seq", None),
-        P("page", "seq", None),
-        P(("page", "seq"), None),
-        P(("page", "seq"), None),
-        P(("page", "seq"), None),
-        P(("page", "seq"), None),
-        P(("page", "seq")),
-        P(("page", "seq")),
-        P(("page", "seq")),
-        P(("page", "seq")),
-        P(("page", "seq")),
-        P(("page", "seq"), None),
-        P(("page", "seq")),
-        P(("page", "seq"), None),
-        P(("page", "seq")),
-        P(("page", "seq")),
-        P(("page", "seq")),
+        P(PAGE, SEQ, None),
+        P(PAGE, SEQ, None),
+        P(AXES, None),
+        P(AXES, None),
+        P(AXES, None),
+        P(AXES, None),
+        P(AXES),
+        P(AXES),
+        P(AXES),
+        P(AXES),
+        P(AXES),
+        P(AXES, None),
+        P(AXES),
+        P(AXES, None),
+        P(AXES),
+        P(AXES),
+        P(AXES),
     )
     return jax.shard_map(
-        functools.partial(per_device, mesh.shape["page"]), mesh=mesh, in_specs=in_specs, out_specs=out_specs, check_vma=False
-    )
+        functools.partial(per_device, mesh.shape[PAGE]), mesh=mesh, in_specs=in_specs, out_specs=out_specs, check_vma=False
+    )

time: 360 us -> 180 us (0.50); the launches traced: 356 us -> 180 us
  matrix products: 106 us -> 0 us
  local copies, waits for them, and re-layouts: 52.3 us -> 15.2 us
  other arithmetic: 14.9 us -> 0 us
  between operations: 14.6 us -> 0.72 us
    dot_general x24 -> x0, matrix products: 106 us -> none  [the longest x18 72.1 us: matmul(): return jnp.dot(left_side, right_side, preferred_element_type=jnp.float32)]
    reduce_sum x11 -> x0, other arithmetic: 11.8 us -> none  [the longest x1 3.26 us: merged(): summed = jnp.sum(jnp.exp(scores - new_peak[..., None]), axis=-1)]
    convert_element_type x14 -> x0, local copies, waits for them, and re-layouts: 10 us -> none  [the longest x1 2.82 us: per_device(): value_grads.astype(jnp.bfloat16)]
    reshape x8 -> x1, local copies, waits for them, and re-layouts: 9.89 us -> 0.01 us  [per_device(): total[VECTORS:VECTORS + panels].reshape(-1)]
    unnamed x108 -> x36, local copies, waits for them, and re-layouts: 15.7 us -> 10.3 us
    all_gather x2 -> x0, local copies, waits for them, and re-layouts: 4.37 us -> none  [the longest x1 2.65 us: per_device(): value_piece = lax.all_gather(value_pages, 'seq', axis=1, tiled=True)]
    pallas_call x2 -> x1, Pallas kernels: 166 us -> 164 us  [whole_layer(): pl.pallas_call(functools.partial(layer_kernel, pages, heads, tuple(own)),...]
  transfers between devices with their start and end apart: 4 -> 0, of which waited for: 1 -> 0; matrix products, arithmetic and copies ran while one was open for 17% -> 0% of each run, Pallas kernels for 0% -> 0%
where the time goes in v2:
time: 180 us
  Pallas kernels  164 us (91%)
  local copies, waits for them, and re-layouts  15.2 us (8%)
    pallas_call x1, Pallas kernels, whole_layer(): pl.pallas_call(functools.partial(layer_kernel, pages, heads, tuple(own)),...  164 us
    unnamed x36, local copies, waits for them, and re-layouts  10.3 us

profile of v2, /device:TPU:0, one launch (start us, length us, event | category | flops | bytes accessed | tf_op | source)
XLA Modules:
  0.0 179.7 jit_solution(10060133996106345825)
XLA Ops:
  0.7 0.7 pad_bitcast_fusion
  1.3 0.0 copy-start.7
  1.3 0.0 copy-start.8
  1.3 0.6 copy-done.7
  2.0 0.0 copy-done.8
  2.0 0.0 copy-start.9
  2.0 0.0 copy-start.10
  2.0 0.6 copy-done.9
  2.7 0.0 copy-done.10
  2.7 0.0 copy-start.11
  2.7 0.0 copy-start.12
  2.7 0.6 copy-done.11
  3.3 0.0 copy-done.12
  3.4 0.0 copy-start.13
  3.4 0.7 copy-done.13
  4.0 1.2 stack.47.small
  5.3 163.8 %whole_layer.1 = (bf16[512,768]{1,0:T(8,128)(2,1)}, bf16[512,768]{1,0:T(8,128)(2,1)}, f32[24,768]{1,0:T(8,128)}, f32[24,768]{1,0:T(8,128)}, f32[24,768]{1,0:T(8,...) custom-call(s32[2]{0:T(128)} %lengths.1, bf16[512,768]{1,0:T(8,128)(2,1)} %bitcast.38, ...), custom_call_target="tpu_custom_call" | custom-call | tf_op jit(solution)/shard_map/whole_layer/pallas_call | solution.py:895
  169.1 1.6 dynamic-slice_bitcast_fusion
  170.7 0.7 slice.3
  171.4 0.6 dynamic_slice.32
  172.0 0.0 copy-start
  172.0 2.1 %copy.43 = bf16[2,256,768]{2,1,0:T(8,128)(2,1)} copy(bf16[2,256,768]{2,1,0:T(8,128)(2,1)} %bitcast.41) | data formatting | bytes 1572864
  174.2 0.0 copy-done
  174.2 0.0 copy-start.6
  174.2 0.0 copy-start.5
  174.2 0.0 copy-start.4
  174.2 0.9 copy.44
  175.1 0.0 copy-done.6
  175.1 0.0 copy-start.2
  175.1 0.6 copy.45
  175.7 0.0 copy-done.5
  175.7 0.6 copy.46
  176.4 0.0 copy-done.4
  176.4 0.0 copy-start.3
  176.4 0.6 copy.47
  177.0 0.3 copy-done.3
  177.3 0.6 copy.48
  177.9 0.0 copy-done.2
  177.9 0.0 copy-start.1
  177.9 0.7 copy.49
  178.6 0.4 copy-done.1
  179.0 0.7 copy.50
  (8 shorter events, 0.0 us)
Async XLA Ops:
  1.3 0.7 copy-start.7
  1.3 0.7 copy-start.8
  2.0 0.7 copy-start.9
  2.0 0.7 copy-start.10
  2.7 0.7 copy-start.11
  2.7 0.7 copy-start.12
  3.4 0.7 copy-start.13
  172.0 2.1 %copy-start = (bf16[512,768]{1,0:T(8,128)(2,1)S(1)}, bf16[512,768]{1,0:T(8,128)(2,1)}, u32[]{:S(2)}) copy-start(bf16[512,768]{1,0:T(8,128)(2,1)} %get-tuple-element.27) | copy-start | bytes 2359300
  174.2 0.9 copy-start.6
  174.2 1.5 copy-start.5
  174.2 2.2 %copy-start.4 = (f32[24,768]{1,0:T(8,128)S(1)}, f32[24,768]{1,0:T(8,128)}, u32[]{:S(2)}) copy-start(f32[24,768]{1,0:T(8,128)} %get-tuple-element.72) | copy-start | bytes 221188
  175.1 2.8 %copy-start.2 = (f32[24,3072]{1,0:T(8,128)S(1)}, f32[24,3072]{1,0:T(8,128)}, u32[]{:S(2)}) copy-start(f32[24,3072]{1,0:T(8,128)} %get-tuple-element.79) | copy-start | bytes 884740
  176.4 0.9 copy-start.3
  177.9 1.1 copy-start.1

commit v3 on v2

--- a/solution.py
+++ b/solution.py
@@ -13,8 +13,11 @@
 DMA = pltpu.SemaphoreType.DMA
 BF = jnp.bfloat16
 F32 = jnp.float32
+LANES = 128
 AXES = PAGE, SEQ = ("page", "seq")
 SMALL, PANELS, ROWS = range(3)
+SPREAD_RELAY = 128
+RELAY = 0
 
 
 def page_grid(pages):
@@ -27,11 +30,14 @@
 class Place:
     def __init__(self, pages):
         self.nz, self.ny, self.nx = page_grid(pages)
+        self.plane = self.ny * self.nx
         self.p = lax.axis_index(PAGE)
         self.c = lax.axis_index(SEQ)
         self.x = lax.rem(self.p, self.nx)
         self.y = lax.rem(self.p // self.nx, self.ny)
-        self.z = self.p // (self.nx * self.ny)
+        self.z = self.p // self.plane
+        self.sibling = (self.p, 1 - self.c)
+        self.others = [(dy, dx) for dy in range(self.ny) for dx in range(self.nx) if dy or dx]
 
     def page(self, dz=0, dy=0, dx=0):
         z = lax.rem(self.z + dz + self.nz, self.nz)
@@ -39,88 +45,105 @@
         x = lax.rem(self.x + dx + self.nx, self.nx)
         return (z * self.ny + y) * self.nx + x
 
-    def partners(self):
-        out = [(self.page(dz=d), self.c) for d in range(1, self.nz)]
-        out += [(self.page(dy=d), self.c) for d in range(1, self.ny)]
-        out += [(self.page(dx=d), self.c) for d in range(1, self.nx)]
-        return out + [(self.p, 1 - self.c)]
-
-    def greet(self):
+    def level(self, dz):
+        return lax.rem(self.z + dz + self.nz, self.nz) * self.plane
+
+    def there(self, dz=0, dy=0, dx=0):
+        return self.page(dz, dy, dx), self.c
+
+    def signal(self):
         barrier = pltpu.get_barrier_semaphore()
-        partners = self.partners()
+        partners = [self.there(dz=d) for d in range(1, self.nz)] + [self.there(0, *d) for d in self.others] + [self.sibling]
         for partner in partners:
             pl.semaphore_signal(barrier, inc=1, device_id=partner, device_id_type=MESH)
-        pl.semaphore_wait(barrier, len(partners))
+        return lambda: pl.semaphore_wait(barrier, len(partners))
+
+
+def slots(sizes):
+    base, at = [], 0
+    for size in sizes:
+        base.append(at)
+        at += size
+    return base, at
 
 
 def gather_slots(pages):
     nz, ny, nx = page_grid(pages)
-    fx, fy = nx - 1, ny - 1
-    base, at = {}, 0
-    for name, size in (
-        ("z", nz - 1), ("x", nz * fx), ("y", nz * fy), ("xa", nz * fx * fy),
-        ("yb", nz * fx * fy), ("core", nz * ny * nx),
-    ):
-        base[name] = at
-        at += size
-    return base, at
+    return slots((1, 1, 1, nz, nz)), slots((nz - 1, nz * (nx - 1), nz * (ny - 1), nz * (nx - 1) * (ny - 1), 1, nz, 1))
 
 
 class Gather:
     def __init__(self, place, ref, send, recv, kind):
         self.pl, self.ref, self.send, self.recv, self.kind = place, ref, send, recv, kind
-        self.base, _ = gather_slots(place.nz * place.ny * place.nx)
-
-    def view(self, block, part):
-        ref = self.ref
-        if part == "all" or self.kind == SMALL:
-            return ref.at[:, block]
-        half = 0 if part == "a" else 1
+        (self.sbase, _), (self.rbase, _) = gather_slots(place.nz * place.plane)
+        self.low = 0 if kind == SMALL else SPREAD_RELAY
+
+    def view(self, page, part, core=None, count=None):
+        ref, low = self.ref, self.low
+        core = self.pl.c if core is None else core
+        pages = page if count is None else pl.ds(page, count)
+        if part == 3:
+            return ref.at[:, pages, core, :, 0:low]
+        if part == 4:
+            return ref.at[:, pages, core]
+        if part == 0 or self.kind == SMALL:
+            return ref.at[:, pages, core, :, low:]
         if self.kind == PANELS:
             n = ref.shape[0] // 2
-            return ref.at[half * n:(half + 1) * n, block]
-        n = ref.shape[2] // 2
-        return ref.at[:, block, half * n:(half + 1) * n]
-
-    def copy(self, name, slot, block, part, target):
-        where = self.base[name] + slot
-        view = self.view(block, part)
+            return ref.at[(part - 1) * n:part * n, pages, core, :, low:]
+        n = ref.shape[3] // 2
+        return ref.at[:, pages, core, (part - 1) * n:part * n, low:]
+
+    def copy(self, view, send, recv, target):
         return pltpu.make_async_remote_copy(
-            src_ref=view, dst_ref=view, send_sem=self.send.at[where], recv_sem=self.recv.at[where],
+            src_ref=view, dst_ref=view, send_sem=self.send.at[send], recv_sem=self.recv.at[recv],
             device_id=target, device_id_type=MESH)
 
-    def block(self, dz=0, dy=0, dx=0):
-        return 2 * self.pl.page(dz, dy, dx) + self.pl.c
+    def plain(self, group, slot, page, part, target):
+        return self.copy(self.view(page, part), self.sbase[0], self.rbase[group] + slot, target)
+
+    def corner_slot(self, dx, dy, dz):
+        return (dz * (self.pl.ny - 1) + dy - 1) * (self.pl.nx - 1) + dx - 1
 
     def z_copy(self, dz, mine):
         p = self.pl
-        return self.copy("z", dz - 1, self.block(0 if mine else -dz), "all", (p.page(dz=dz), p.c))
+        return self.plain(0, dz - 1, p.page(0 if mine else -dz), 0, p.there(dz=dz))
 
     def x_copy(self, dx, dz, mine):
         p = self.pl
-        return self.copy("x", dz * (p.nx - 1) + dx - 1, self.block(-dz, 0, 0 if mine else -dx), "all", (p.page(dx=dx), p.c))
+        return self.plain(1, dz * (p.nx - 1) + dx - 1, p.page(-dz, 0, 0 if mine else -dx), 0, p.there(dx=dx))
 
     def y_copy(self, dy, dz, mine):
         p = self.pl
-        return self.copy("y", dz * (p.ny - 1) + dy - 1, self.block(-dz, 0 if mine else -dy, 0), "all", (p.page(dy=dy), p.c))
-
-    def diag_slot(self, dx, dy, dz):
-        p = self.pl
-        return (dz * (p.ny - 1) + dy - 1) * (p.nx - 1) + dx - 1
-
-    def xa_copy(self, dx, dy, dz, mine):
-        p = self.pl
-        return self.copy("xa", self.diag_slot(dx, dy, dz), self.block(-dz, -dy, 0 if mine else -dx), "a", (p.page(dx=dx), p.c))
-
-    def yb_copy(self, dx, dy, dz, mine):
-        p = self.pl
-        return self.copy("yb", self.diag_slot(dx, dy, dz), self.block(-dz, 0 if mine else -dy, -dx), "b", (p.page(dy=dy), p.c))
-
-    def core_copy(self, dz, dy, dx, mine):
-        p = self.pl
-        slot = (dz * p.ny + dy) * p.nx + dx
-        block = 2 * p.page(-dz, -dy, -dx) + (p.c if mine else 1 - p.c)
-        return self.copy("core", slot, block, "all", (p.p, 1 - p.c))
+        return self.plain(2, dz * (p.ny - 1) + dy - 1, p.page(-dz, 0 if mine else -dy, 0), 0, p.there(dy=dy))
+
+    def xa_copy(self, dx, dy, dz):
+        p = self.pl
+        return self.plain(3, self.corner_slot(dx, dy, dz), p.page(-dz, -dy, 0), 1, p.there(dx=dx))
+
+    def yb_copy(self, dx, dy, dz):
+        p = self.pl
+        return self.plain(3, self.corner_slot(dx, dy, dz), p.page(-dz, 0, -dx), 2, p.there(dy=dy))
+
+    def core_copy(self, page, part, count=None):
+        return self.copy(self.view(page, part, None, count), self.sbase[1], self.rbase[6], self.pl.sibling)
+
+    def relay_copy(self, level, up):
+        p = self.pl
+        group = level // p.plane
+        target = p.there(dz=1 if up else p.nz - 1)
+        return self.copy(self.view(level, 3, None, p.plane), self.sbase[3 if up else 4] + group, self.rbase[5] + group, target)
+
+    def wait(self, view, sem):
+        pltpu.make_async_copy(view, view, sem).wait()
+
+    def begin(self):
+        p = self.pl
+        if self.low:
+            for dy, dx in p.others:
+                self.copy(self.view(p.page(), 3), self.sbase[2], self.rbase[4], p.there(0, dy, dx)).start()
+        for d in range(1, p.nz):
+            self.z_copy(d, True).start()
 
     def spread(self, dz):
         p = self.pl
@@ -128,199 +151,270 @@
             self.x_copy(d, dz, True).start()
         for d in range(1, p.ny):
             self.y_copy(d, dz, True).start()
-        self.core_copy(dz, 0, 0, True).start()
-
-    def begin_z(self):
-        for d in range(1, self.pl.nz):
-            self.z_copy(d, True).start()
+        self.core_copy(p.page(-dz), 0).start()
 
     def column(self, dz):
         self.z_copy(dz, False).wait_recv()
         self.spread(dz)
 
+    def rise(self):
+        p = self.pl
+        if not self.low:
+            return
+        level = p.level(0)
+        self.wait(self.view(level, 3, None, p.plane - 1), self.recv.at[self.rbase[4]])
+        pl.when(p.z < p.nz - 1)(lambda: self.relay_copy(level, True).start())
+        pl.when(p.z > 0)(lambda: self.relay_copy(level, False).start())
+        self.core_copy(level, 3, p.plane).start()
+
+    def relay(self, d):
+        p = self.pl
+        if not self.low:
+            return
+
+        def step(up):
+            level = (p.z - d if up else p.z + d) * p.plane
+            self.relay_copy(level, up).wait_recv()
+            pl.when(p.z < p.nz - 1 if up else p.z > 0)(lambda: self.relay_copy(level, up).start())
+            self.core_copy(level, 3, p.plane).start()
+
+        pl.when(p.z >= d)(lambda: step(True))
+        pl.when(p.z + d < p.nz)(lambda: step(False))
+
     def plane(self, dz):
         p = self.pl
         for dy in range(1, p.ny):
             self.y_copy(dy, dz, False).wait_recv()
             for dx in range(1, p.nx):
-                self.xa_copy(dx, dy, dz, True).start()
-            self.core_copy(dz, dy, 0, True).start()
+                self.xa_copy(dx, dy, dz).start()
+            self.core_copy(p.page(-dz, -dy), 0).start()
         for dx in range(1, p.nx):
             self.x_copy(dx, dz, False).wait_recv()
             if self.kind != SMALL:
                 for dy in range(1, p.ny):
-                    self.yb_copy(dx, dy, dz, True).start()
-            self.core_copy(dz, 0, dx, True).start()
+                    self.yb_copy(dx, dy, dz).start()
+            self.core_copy(p.page(-dz, 0, -dx), 0).start()
 
     def corner(self, dz):
         p = self.pl
         for dy in range(1, p.ny):
             for dx in range(1, p.nx):
-                self.xa_copy(dx, dy, dz, False).wait_recv()
-                if self.kind != SMALL:
-                    self.yb_copy(dx, dy, dz, False).wait_recv()
-                self.core_copy(dz, dy, dx, True).start()
+                page = p.page(-dz, -dy, -dx)
+                self.wait(self.view(page, 0), self.recv.at[self.rbase[3] + self.corner_slot(dx, dy, dz)])
+                self.core_copy(page, 0).start()
 
     def finish_core(self):
-        p = self.pl
-        for dz in range(p.nz):
-            for dy in range(p.ny):
-                for dx in range(p.nx):
-                    self.core_copy(dz, dy, dx, False).wait_recv()
+        self.wait(self.view(0, 4, 1 - self.pl.c, self.pl.nz * self.pl.plane), self.recv.at[self.rbase[6]])
 
     def drain(self):
         p = self.pl
-        for d in range(1, p.nz):
-            self.z_copy(d, True).wait_send()
-        for dz in range(p.nz):
-            for dx in range(1, p.nx):
-                self.x_copy(dx, dz, True).wait_send()
-            for dy in range(1, p.ny):
-                self.y_copy(dy, dz, True).wait_send()
-                for dx in range(1, p.nx):
-                    self.xa_copy(dx, dy, dz, True).wait_send()
-                    if self.kind != SMALL:
-                        self.yb_copy(dx, dy, dz, True).wait_send()
-            for dy in range(p.ny):
-                for dx in range(p.nx):
-                    self.core_copy(dz, dy, dx, True).wait_send()
+        pages = p.nz * p.plane
+        self.wait(self.view(0, 4, None, pages), self.send.at[self.sbase[1]])
+        corners = p.nz * (p.ny - 1) * (p.nx - 1)
+        blocks = p.nz - 1 + p.nz * (p.nx - 1) + p.nz * (p.ny - 1) + corners
+        if self.low:
+            self.wait(self.view(0, 3, None, p.plane - 1), self.send.at[self.sbase[2]])
+        self.wait(self.view(0, 0, None, blocks), self.send.at[self.sbase[0]])
+        if self.low:
+            def group(g):
+                pl.when(jnp.logical_and(p.z < p.nz - 1, g <= p.z))(lambda: self.relay_copy(g * p.plane, True).wait_send())
+                pl.when(jnp.logical_and(p.z > 0, g >= p.z))(lambda: self.relay_copy(g * p.plane, False).wait_send())
+            for g in range(p.nz):
+                group(g)
 
 
 def reduce_slots(pages):
     nz, ny, nx = page_grid(pages)
-    fx, fy = nx - 1, ny - 1
-    base, at = {}, 0
-    for name, size in (
-        ("core", nz * ny * nx), ("xa", nz * fx * fy), ("yb", nz * fx * fy), ("x", nz * fx), ("y", nz * fy), ("z", nz - 1),
-    ):
-        base[name] = at
-        at += size
-    return base, at
+    corners = nz * (nx - 1) * (ny - 1)
+    return slots((1, 1, 1, nz, nz)), slots((nz, corners, corners, nz * (nx - 1), nz * (ny - 1), nz - 1, 1, nz, nz))
 
 
 def reduce_scratch(pages, panels, rows, width, kind):
     nz, ny, nx = page_grid(pages)
     fx, fy = nx - 1, ny - 1
     half = (panels // 2, rows) if kind == PANELS else (panels, rows // 2)
-    _, slots = reduce_slots(pages)
+    rest = width - RELAY
+    (_, sends), (_, recvs) = reduce_slots(pages)
     return [
         VMEM((panels, nz * ny * nx, rows, width), BF),
-        VMEM((nz * fx * fy,) + half + (width,), BF),
-        VMEM((nz * fx * fy,) + half + (width,), BF),
-        VMEM((nz * fx, panels, rows, width), BF),
-        VMEM((nz * fy, panels, rows, width), BF),
-        VMEM((nz - 1, panels, rows, width), BF),
-        DMA((slots,)),
-        DMA((slots,)),
+        VMEM((nz * fx * fy,) + half + (rest,), BF),
+        VMEM((nz * fx * fy,) + half + (rest,), BF),
+        VMEM((nz * fx, panels, rows, rest), BF),
+        VMEM((nz * fy, panels, rows, rest), BF),
+        VMEM((nz - 1, panels, rows, rest), BF),
+        VMEM((ny * nx - 1, panels, rows, RELAY) if RELAY else (8, LANES), BF),
+        VMEM((2, nz, panels, ny * nx, rows, RELAY) if RELAY else (8, LANES), BF),
+        DMA((sends,)),
+        DMA((recvs,)),
     ]
+
+
+REDUCE_REFS = 10
 
 
 class Reduce:
     def __init__(self, place, part, scratch, kind):
         self.pl, self.part, self.kind = place, part, kind
-        self.total, self.da, self.db, self.rx, self.ry, self.rz, self.send, self.recv = scratch
-        self.base, _ = reduce_slots(place.nz * place.ny * place.nx)
-
-    def remote(self, name, slot, src, dst, target):
-        where = self.base[name] + slot
+        self.total, self.da, self.db, self.rx, self.ry, self.rz, self.rp, self.rr, self.send, self.recv = scratch
+        (self.sbase, _), (self.rbase, _) = reduce_slots(place.nz * place.plane)
+
+    def remote(self, send, recv, src, dst, target):
         return pltpu.make_async_remote_copy(
-            src_ref=src, dst_ref=dst, send_sem=self.send.at[where], recv_sem=self.recv.at[where],
+            src_ref=src, dst_ref=dst, send_sem=self.send.at[send], recv_sem=self.recv.at[recv],
             device_id=target, device_id_type=MESH)
+
+    def plain(self, group, slot, src, dst, target):
+        return self.remote(self.sbase[0], self.rbase[group] + slot, src, dst, target)
+
+    def wait(self, view, sem):
+        pltpu.make_async_copy(view, view, sem).wait()
 
     def half(self, page, which):
         if self.kind == PANELS:
             n = self.total.shape[0] // 2
-            return self.total.at[which * n:(which + 1) * n, page]
+            return self.total.at[which * n:(which + 1) * n, page, :, RELAY:]
         n = self.total.shape[2] // 2
-        return self.total.at[:, page, which * n:(which + 1) * n]
-
-    def core_copy(self, dz, dy, dx):
-        p = self.pl
-        page = p.page(dz, dy, dx)
-        return self.remote("core", (dz * p.ny + dy) * p.nx + dx, self.part.at[:, 2 * page + 1 - p.c], self.total.at[:, page], (p.p, 1 - p.c))
-
-    def diag(self, dz, dy, dx):
-        p = self.pl
-        return (dz * (p.ny - 1) + dy - 1) * (p.nx - 1) + dx - 1
+        return self.total.at[:, page, which * n:(which + 1) * n, RELAY:]
+
+    def corner_slot(self, dz, dy, dx):
+        return (dz * (self.pl.ny - 1) + dy - 1) * (self.pl.nx - 1) + dx - 1
+
+    def core_copy(self, dz):
+        p = self.pl
+        pages = pl.ds(p.level(dz), p.plane)
+        return self.remote(
+            self.sbase[1], self.rbase[0] + dz, self.part.at[:, pages, 1 - p.c], self.total.at[:, pages], p.sibling)
 
     def xa_copy(self, dz, dy, dx):
-        p, slot = self.pl, self.diag(dz, dy, dx)
-        return self.remote("xa", slot, self.half(p.page(dz, dy, dx), 0), self.da.at[slot], (p.page(dx=dx), p.c))
+        p, slot = self.pl, self.corner_slot(dz, dy, dx)
+        return self.plain(1, slot, self.half(p.page(dz, dy, dx), 0), self.da.at[slot], p.there(dx=dx))
 
     def yb_copy(self, dz, dy, dx):
-        p, slot = self.pl, self.diag(dz, dy, dx)
-        return self.remote("yb", slot, self.half(p.page(dz, dy, dx), 1), self.db.at[slot], (p.page(dy=dy), p.c))
+        p, slot = self.pl, self.corner_slot(dz, dy, dx)
+        return self.plain(2, slot, self.half(p.page(dz, dy, dx), 1), self.db.at[slot], p.there(dy=dy))
 
     def x_copy(self, dz, dx):
         p = self.pl
         slot = dz * (p.nx - 1) + dx - 1
-        return self.remote("x", slot, self.total.at[:, p.page(dz, 0, dx)], self.rx.at[slot], (p.page(dx=dx), p.c))
+        return self.plain(3, slot, self.total.at[:, p.page(dz, 0, dx), :, RELAY:], self.rx.at[slot], p.there(dx=dx))
 
     def y_copy(self, dz, dy):
         p = self.pl
         slot = dz * (p.ny - 1) + dy - 1
-        return self.remote("y", slot, self.total.at[:, p.page(dz, dy, 0)], self.ry.at[slot], (p.page(dy=dy), p.c))
+        return self.plain(4, slot, self.total.at[:, p.page(dz, dy, 0), :, RELAY:], self.ry.at[slot], p.there(dy=dy))
 
     def z_copy(self, dz):
         p = self.pl
-        return self.remote("z", dz - 1, self.total.at[:, p.page(dz, 0, 0)], self.rz.at[dz - 1], (p.page(dz=dz), p.c))
+        return self.plain(5, dz - 1, self.total.at[:, p.page(dz), :, RELAY:], self.rz.at[dz - 1], p.there(dz=dz))
+
+    def relay_copy(self, level, up):
+        p = self.pl
+        group, way = level // p.plane, 0 if up else 1
+        return self.remote(
+            self.sbase[3 + way] + group, self.rbase[7 + way] + group,
+            self.total.at[:, pl.ds(level, p.plane), :, 0:RELAY], self.rr.at[way, group], p.there(dz=1 if up else p.nz - 1))
+
+    def plane_copy(self, k, dy, dx):
+        p = self.pl
+        return self.remote(
+            self.sbase[2], self.rbase[6], self.total.at[:, p.page(0, dy, dx), :, 0:RELAY], self.rp.at[k], p.there(0, dy, dx))
 
     def begin(self, dz):
-        p = self.pl
-        order = [(dy, dx) for dy in range(1, p.ny) for dx in range(1, p.nx)]
-        order += [(0, dx) for dx in range(1, p.nx)] + [(dy, 0) for dy in range(1, p.ny)] + [(0, 0)]
-        for dy, dx in order:
-            self.core_copy(dz, dy, dx).start()
-
-    def pair(self, dz, dy, dx):
-        p = self.pl
-        self.core_copy(dz, dy, dx).wait_recv()
-        page = p.page(dz, dy, dx)
-        return self.part[:, 2 * page + p.c].astype(F32) + self.total[:, page].astype(F32)
+        self.core_copy(dz).start()
+
+    def arrive(self, dz):
+        self.core_copy(dz).wait_recv()
+
+    def pair(self, page):
+        return self.part[:, page, self.pl.c, :, RELAY:].astype(F32) + self.total[:, page, :, RELAY:].astype(F32)
 
     def corner(self, dz):
         p = self.pl
         for dy in range(1, p.ny):
             for dx in range(1, p.nx):
-                self.total[:, p.page(dz, dy, dx)] = self.pair(dz, dy, dx).astype(BF)
+                page = p.page(dz, dy, dx)
+                self.total[:, page, :, RELAY:] = self.pair(page).astype(BF)
                 self.xa_copy(dz, dy, dx).start()
                 self.yb_copy(dz, dy, dx).start()
 
+    def level_sum(self, level):
+        p = self.pl
+        pages, group = pl.ds(level, p.plane), level // p.plane
+        total = self.part[:, pages, p.c, :, 0:RELAY].astype(F32) + self.total[:, pages, :, 0:RELAY].astype(F32)
+        return total, pages, group
+
+    def relay(self, d):
+        p = self.pl
+        if not RELAY:
+            return
+
+        def step(up):
+            total, pages, group = self.level_sum((p.z + d if up else p.z - d) * p.plane)
+            self.total[:, pages, :, 0:RELAY] = total.astype(BF)
+
+            def add():
+                self.relay_copy(group * p.plane, up).wait_recv()
+                got = self.rr[0 if up else 1, group].astype(F32)
+                self.total[:, pages, :, 0:RELAY] = (total + got).astype(BF)
+
+            pl.when(p.z > 0 if up else p.z < p.nz - 1)(add)
+            self.relay_copy(group * p.plane, up).start()
+
+        pl.when(p.z + d < p.nz)(lambda: step(True))
+        pl.when(p.z >= d)(lambda: step(False))
+
+    def settle(self):
+        p = self.pl
+        if not RELAY:
+            return
+        total, pages, group = self.level_sum(p.level(0))
+        self.total[:, pages, :, 0:RELAY] = total.astype(BF)
+        for way in range(2):
+            def add(way=way):
+                self.relay_copy(group * p.plane, way == 0).wait_recv()
+                self.total[:, pages, :, 0:RELAY] = (
+                    self.total[:, pages, :, 0:RELAY].astype(F32) + self.rr[way, group].astype(F32)).astype(BF)
+            pl.when(p.z > 0 if way == 0 else p.z < p.nz - 1)(add)
+        for k, (dy, dx) in enumerate(p.others):
+            self.plane_copy(k, dy, dx).start()
+
+    def owned(self):
+        p = self.pl
+        self.wait(self.rp, self.recv.at[self.rbase[6]])
+        total = self.total[:, p.page(), :, 0:RELAY].astype(F32)
+        for k in range(len(p.others)):
+            total += self.rp[k].astype(F32)
+        return total
+
     def plane(self, dz):
         p = self.pl
         panels, rows = self.total.shape[0], self.total.shape[2]
+
+        def with_half(total, add, which):
+            axis, n = (0, panels // 2) if self.kind == PANELS else (1, rows // 2)
+            first, second = (total[:n], total[n:]) if axis == 0 else (total[:, :n], total[:, n:])
+            return jnp.concatenate([first + add, second] if which == 0 else [first, second + add], axis=axis)
+
         for dx in range(1, p.nx):
-            total = self.pair(dz, 0, dx)
             page = p.page(dz, 0, dx)
+            total = self.pair(page)
             for dy in range(1, p.ny):
                 self.yb_copy(dz, dy, dx).wait_recv()
-                add = self.db[self.diag(dz, dy, dx)].astype(F32)
-                if self.kind == PANELS:
-                    n = panels // 2
-                    total = jnp.concatenate([total[:n], total[n:] + add], axis=0)
-                else:
-                    n = rows // 2
-                    total = jnp.concatenate([total[:, :n], total[:, n:] + add], axis=1)
-            self.total[:, page] = total.astype(BF)
+                total = with_half(total, self.db[self.corner_slot(dz, dy, dx)].astype(F32), 1)
+            self.total[:, page, :, RELAY:] = total.astype(BF)
             self.x_copy(dz, dx).start()
         for dy in range(1, p.ny):
-            total = self.pair(dz, dy, 0)
             page = p.page(dz, dy, 0)
+            total = self.pair(page)
             for dx in range(1, p.nx):
                 self.xa_copy(dz, dy, dx).wait_recv()
-                add = self.da[self.diag(dz, dy, dx)].astype(F32)
-                if self.kind == PANELS:
-                    n = panels // 2
-                    total = jnp.concatenate([total[:n] + add, total[n:]], axis=0)
-                else:
-                    n = rows // 2
-                    total = jnp.concatenate([total[:, :n] + add, total[:, n:]], axis=1)
-            self.total[:, page] = total.astype(BF)
+                total = with_half(total, self.da[self.corner_slot(dz, dy, dx)].astype(F32), 0)
+            self.total[:, page, :, RELAY:] = total.astype(BF)
             self.y_copy(dz, dy).start()
 
     def column_sum(self, dz):
         p = self.pl
-        total = self.pair(dz, 0, 0)
+        total = self.pair(p.page(dz))
         for dx in range(1, p.nx):
             self.x_copy(dz, dx).wait_recv()
             total += self.rx[dz * (p.nx - 1) + dx - 1].astype(F32)
@@ -330,7 +424,7 @@
         return total
 
     def column(self, dz):
-        self.total[:, self.pl.page(dz, 0, 0)] = self.column_sum(dz).astype(BF)
+        self.total[:, self.pl.page(dz), :, RELAY:] = self.column_sum(dz).astype(BF)
         self.z_copy(dz).start()
 
     def finish(self):
@@ -338,28 +432,23 @@
         for dz in range(1, self.pl.nz):
             self.z_copy(dz).wait_recv()
             total += self.rz[dz - 1].astype(F32)
-        return total
+        return jnp.concatenate([self.owned(), total], axis=2) if RELAY else total
 
     def drain(self):
         p = self.pl
-
-        def one(dz, _):
-            for dy in range(p.ny):
-                for dx in range(p.nx):
-                    self.core_copy(dz, dy, dx).wait_send()
-            for dy in range(1, p.ny):
-                for dx in range(1, p.nx):
-                    self.xa_copy(dz, dy, dx).wait_send()
-                    self.yb_copy(dz, dy, dx).wait_send()
-            for dx in range(1, p.nx):
-                self.x_copy(dz, dx).wait_send()
-            for dy in range(1, p.ny):
-                self.y_copy(dz, dy).wait_send()
-            return 0
-
-        lax.fori_loop(0, p.nz, one, 0)
-        for dz in range(1, p.nz):
-            self.z_copy(dz).wait_send()
+        pages = p.nz * p.plane
+        self.wait(self.part.at[:, :, 0], self.send.at[self.sbase[1]])
+        self.wait(self.total.at[:, 0:pages - 1, :, RELAY:], self.send.at[self.sbase[0]])
+        if not RELAY:
+            return
+        self.wait(self.rp, self.send.at[self.sbase[2]])
+
+        def group(g):
+            pl.when(g > p.z)(lambda: self.relay_copy(g * p.plane, True).wait_send())
+            pl.when(g < p.z)(lambda: self.relay_copy(g * p.plane, False).wait_send())
+
+        for g in range(p.nz):
+            group(g)
 
 
 def vector_scratch(pages, rows, width):
@@ -376,10 +465,10 @@
     def legs(self):
         p = self.pl
         return [
-            [(p.p, 1 - p.c)],
-            [(p.page(dx=d), p.c) for d in range(1, p.nx)],
-            [(p.page(dy=d), p.c) for d in range(1, p.ny)],
-            [(p.page(dz=d), p.c) for d in range(1, p.nz)],
+            [p.sibling],
+            [p.there(dx=d) for d in range(1, p.nx)],
+            [p.there(dy=d) for d in range(1, p.ny)],
+            [p.there(dz=d) for d in range(1, p.nz)],
         ]
 
     def copies(self, leg):
@@ -461,14 +550,11 @@
 
 
 def pack_vectors(vectors, inner):
-    lanes = 128
-    rows = [jnp.pad(v, (0, lanes - v.shape[0])) for v in (*vectors, inner)]
-    rows += [jnp.zeros((lanes,), BF)] * (16 - len(rows))
-    return jnp.stack(rows)
+    rows = [jnp.pad(v[None], ((j, 15 - j), (0, 128 - v.shape[0]))) for j, v in enumerate((*vectors, inner))]
+    return functools.reduce(jnp.add, rows)
 
 
 LOG2E = 1.4426950408889634
-LANES = 128
 VEC_ROWS = 16
 NT = ((1,), (1,))
 TN = ((0,), (0,))
@@ -518,16 +604,15 @@
 
 
 def layer_scratch(pages, rows, width, panels, tokens, local_pages):
-    devices = 2 * pages
-    _, gs = gather_slots(pages)
+    (_, gather_sends), (_, gather_recvs) = gather_slots(pages)
     seg = tokens // local_pages
     own = dict(
-        g_attn=VMEM((4, devices, rows, width), BF),
-        g_inner=VMEM((panels, devices, rows, width), BF),
-        g_outer=VMEM((1, devices, panels * rows, width), BF),
-        g_small=VMEM((1, devices, VEC_ROWS, LANES), BF),
-        p_one=VMEM((2, devices, rows, width), BF),
-        p_two=VMEM((2, devices, rows, width), BF),
+        g_attn=VMEM((4, pages, 2, rows, width), BF),
+        g_inner=VMEM((panels, pages, 2, rows, width), BF),
+        g_outer=VMEM((1, pages, 2, panels * rows, width), BF),
+        g_small=VMEM((1, pages, 2, VEC_ROWS, LANES), BF),
+        p_one=VMEM((2, pages, 2, rows, width), BF),
+        p_two=VMEM((2, pages, 2, rows, width), BF),
         xs=VMEM((tokens, width), BF),
         q=VMEM((tokens, width), BF),
         k=VMEM((local_pages, 2 * seg, width), BF),
@@ -544,40 +629,63 @@
         par=VMEM((VEC_ROWS, width), F32),
         rk=VMEM((local_pages, seg, width), BF),
         rv=VMEM((local_pages, seg, width), BF),
+        x=VMEM((tokens, width), BF),
+        cot=VMEM((tokens, width), BF),
+        out=VMEM((tokens, width), BF),
+        squares=VMEM((4, rows, width), F32),
+        wide=VMEM((rows, panels * width), F32),
+        tall=VMEM((panels * rows, width), F32),
+        total=VMEM((VEC_ROWS, width), F32),
+        in_sem=DMA((8 + panels,)),
+        out_sem=DMA((9,)),
         x_sem=DMA((2,)),
         kv_sem=DMA((4, local_pages)),
     )
-    gather = [DMA((gs,))] * 8
+    gather = [DMA((gather_sends,)), DMA((gather_recvs,))] * 4
     reduce = []
     for count, size, kind in ((1, panels * rows, ROWS), (panels, rows, PANELS), (2, rows, PANELS), (2, rows, PANELS)):
         reduce += reduce_scratch(pages, count, size, width, kind)
     return own, gather + reduce + vector_scratch(pages, VEC_ROWS, width)
 
 
-def layer_kernel(pages, heads, names, lengths, x, cot, wq, wk, wv, wo, wi, wout, small,
+def layer_kernel(pages, heads, names, lengths, x_in, cot_in, wq, wk, wv, wo, wi, wout, small,
                  layer_out, hidden_grad, o_q, o_k, o_v, o_o, o_inner, o_outer, o_vec, *scratch):
     s = types.SimpleNamespace(**dict(zip(names, scratch)))
-    s.d_ctx = s.xs
+    s.d_ctx, s.grad = s.xs, s.cot
     rest = scratch[len(names):]
     place = Place(pages)
     c, nz = place.c, place.nz
-    mine = 2 * place.p + c
-    sibling = (place.p, 1 - c)
+    mine = place.p, c
+    sibling = place.sibling
+    x, cot = s.x, s.cot
     tokens, width = x.shape
-    panels, devices, rows = s.g_inner.shape[:3]
+    panels, _, _, rows = s.g_inner.shape[:4]
+    blocks = (pages, 2, rows, width)
     local_pages, page_len = s.k.shape[:2]
     seg = tokens // local_pages
     full = (width, width)
     scale = (width // heads) ** -0.5
     q, k, v, ctx, res, par, vec = s.q, s.k, s.v, s.ctx, s.res, s.par, s.vec
 
-    for j, ref in enumerate((wq, wk, wv, wo)):
-        s.g_attn[j, mine] = ref[...]
-    for j in range(panels):
-        s.g_inner[j, mine] = wi[:, j * width:(j + 1) * width]
-    s.g_outer[0, mine] = wout[...]
-    s.g_small[0, mine] = small[...]
-    place.greet()
+    arrived = place.signal()
+    moves = [(x_in, x), (small, s.g_small.at[0, *mine])]
+    moves += [(ref, s.g_attn.at[j, *mine]) for j, ref in enumerate((wq, wk, wv, wo))]
+    moves += [(wi.at[:, j * width:(j + 1) * width], s.g_inner.at[j, *mine]) for j in range(panels)]
+    moves += [(wout, s.g_outer.at[0, *mine]), (cot_in, cot)]
+    moves = [pltpu.make_async_copy(src, dst, s.in_sem.at[i]) for i, (src, dst) in enumerate(moves)]
+    for move in moves:
+        move.start()
+    for move in moves[:-1]:
+        move.wait()
+    arrived()
+
+    def emit(i, src, dst):
+        return pltpu.make_async_copy(src, dst, s.out_sem.at[i])
+
+    results = [
+        emit(i, src, dst) for i, (src, dst) in enumerate((
+            (s.out, layer_out), (s.grad, hidden_grad), (s.squares.at[0], o_q), (s.squares.at[1], o_k), (s.squares.at[2], o_v),
+            (s.squares.at[3], o_o), (s.wide, o_inner), (s.tall, o_outer), (s.total, o_vec)))]
     x_copy = pltpu.make_async_remote_copy(
         src_ref=x, dst_ref=s.xs, send_sem=s.x_sem.at[0], recv_sem=s.x_sem.at[1],
         device_id=sibling, device_id_type=MESH)
@@ -585,23 +693,30 @@
     tiny, attn, inner, outer = (
         Gather(place, ref, rest[2 * i], rest[2 * i + 1], kind)
         for i, (ref, kind) in enumerate(((s.g_small, SMALL), (s.g_attn, PANELS), (s.g_inner, PANELS), (s.g_outer, ROWS))))
-    first = (tiny, attn)
-    for one in (tiny, attn, inner, outer):
-        one.begin_z()
+    first = (attn, tiny)
+    for one in first:
+        one.begin()
     for one in first:
         one.spread(0)
     for dz in range(1, nz):
         for one in first:
             one.column(dz)
+    attn.rise()
+    inner.begin()
     for dz in range(nz):
         for one in first:
             one.plane(dz)
+    attn.relay(1)
     inner.spread(0)
+    attn.relay(2)
     for dz in range(1, nz):
         inner.column(dz)
+    attn.relay(3)
+    inner.rise()
     for dz in range(nz):
         for one in first:
             one.corner(dz)
+    outer.begin()
     for one in first:
         one.finish_core()
     x_copy.wait()
@@ -610,10 +725,10 @@
         return ref[j].reshape(full)
 
     def outer_weight(j):
-        n = devices // panels
+        n = pages // panels
         return s.g_outer[0, pl.ds(j * n, n)].reshape(full)
 
-    gathered = s.g_small[0]
+    gathered = s.g_small[0].reshape(2 * pages, VEC_ROWS, LANES)
     par[...] = spread_lanes(gathered, rows, width, 0)
     for j in range(panels):
         par[VECTORS + j:VECTORS + j + 1, :] = spread_lanes(gathered, panels * rows, width, j * width)[VECTORS:VECTORS + 1]
@@ -662,17 +777,17 @@
         ctx[rows_of, cols] = jnp.where(low_half, *parts).astype(BF)
 
     steps_loop(local_pages * pairs, attend, {
-        0: [lambda: inner.plane(3), lambda: outer.spread(0)],
-        1: [lambda: outer.column(1)],
-        2: [lambda: outer.column(2)],
-        3: [lambda: outer.column(3)],
+        0: [lambda: inner.plane(3), lambda: inner.relay(1), lambda: outer.spread(0)],
+        1: [lambda: outer.column(1), lambda: inner.relay(2)],
+        2: [lambda: outer.column(2), outer.rise],
+        3: [lambda: outer.column(3), lambda: inner.relay(3)],
         4: [lambda: inner.corner(0)],
         5: [lambda: inner.corner(1)],
-        6: [lambda: inner.corner(2)],
+        6: [lambda: inner.corner(2), lambda: outer.relay(1)],
         7: [lambda: inner.corner(3)],
-        8: [lambda: outer.plane(0)],
+        8: [lambda: outer.plane(0), lambda: outer.relay(2)],
         9: [lambda: outer.plane(1)],
-        10: [lambda: outer.plane(2)],
+        10: [lambda: outer.plane(2), lambda: outer.relay(3)],
         11: [lambda: outer.plane(3)],
     })
 
@@ -716,7 +831,7 @@
 
     def norm_two(at):
         xhat, r = standardize(res[at, :])
-        layer_out[at, :] = (xhat * vector(6) + vector(7)).astype(BF)
+        s.out[at, :] = (xhat * vector(6) + vector(7)).astype(BF)
         grad = cot[at, :].astype(F32)
         add_row(vec, 6, grad * xhat)
         add_row(vec, 7, grad)
@@ -726,10 +841,12 @@
         s.d_low[at, :] = d_low
         add_row(vec, 5, d_low.astype(F32))
 
+    moves[-1].wait()
     chunks(norm_two)
+    results[0].start()
 
     reducers = [
-        Reduce(place, part, rest[8 + 8 * i:16 + 8 * i], kind)
+        Reduce(place, part, rest[8 + REDUCE_REFS * i:8 + REDUCE_REFS * (i + 1)], kind)
         for i, (part, kind) in enumerate(((s.g_outer, ROWS), (s.g_inner, PANELS), (s.p_one, PANELS), (s.p_two, PANELS)))]
     r_outer, r_inner, r_first, r_second = reducers
     outer.drain()
@@ -738,29 +855,29 @@
         j = lax.rem(place.z + dz, nz)
         d_low = s.d_low[...]
         d_pre = (dot(d_low, outer_weight(j), NT) * s.slope[j].astype(F32)).astype(BF)
-        n = devices // panels
-        s.g_outer[0, pl.ds(j * n, n)] = dot(s.post[j], d_low, TN).reshape(n, panels * rows, width).astype(BF)
+        n = pages // panels
+        s.g_outer[0, pl.ds(j * n, n)] = dot(s.post[j], d_low, TN).reshape(n, 2, panels * rows, width).astype(BF)
         r_outer.begin(dz)
         s.slope[j] = d_pre
         vec[pl.ds(VECTORS + j, 1), :] = jnp.sum(d_pre.astype(F32), axis=0, keepdims=True)
 
     steps_loop(nz, outer_back, {
-        1: [lambda: r_outer.corner(0)],
-        2: [lambda: r_outer.corner(1)],
-        3: [lambda: r_outer.corner(2)],
+        1: [lambda: r_outer.arrive(0), lambda: r_outer.corner(0)],
+        2: [lambda: r_outer.arrive(1), lambda: r_outer.corner(1)],
+        3: [lambda: r_outer.arrive(2), lambda: r_outer.corner(2)],
     })
     inner.drain()
 
     def inner_back(j):
         d_pre = s.slope[j]
         res[...] += dot(d_pre, weight(s.g_inner, j), NT)
-        s.g_inner[j] = dot(s.low[...], d_pre, TN).reshape(devices, rows, width).astype(BF)
+        s.g_inner[j] = dot(s.low[...], d_pre, TN).reshape(blocks).astype(BF)
 
     steps_loop(panels, inner_back, {
-        0: [lambda: r_outer.corner(3), lambda: r_outer.plane(0)],
-        1: [lambda: r_outer.plane(1)],
-        2: [lambda: r_outer.plane(2)],
-        3: [lambda: r_outer.plane(3)],
+        0: [lambda: r_outer.arrive(3), lambda: r_outer.corner(3), lambda: r_outer.relay(3), lambda: r_outer.plane(0)],
+        1: [lambda: r_outer.plane(1), lambda: r_outer.relay(2)],
+        2: [lambda: r_outer.plane(2), lambda: r_outer.relay(1)],
+        3: [lambda: r_outer.plane(3), r_outer.settle],
     })
     for dz in range(nz):
         r_inner.begin(dz)
@@ -777,7 +894,9 @@
 
     chunks(norm_one_back)
     s.d_ctx[...] = dot(s.d_low[...], weight(s.g_attn, 3), NT).astype(BF)
-    s.p_one[0] = dot(ctx[...], s.d_low[...], TN).reshape(devices, rows, width).astype(BF)
+    s.p_one[0] = dot(ctx[...], s.d_low[...], TN).reshape(blocks).astype(BF)
+    for dz in range(nz):
+        r_inner.arrive(dz)
     r_inner.corner(0)
     r_inner.corner(1)
 
@@ -812,23 +931,24 @@
             copy.start()
 
     def finish_outer():
-        o_outer[...] = r_outer.finish()[0]
+        s.tall[...] = r_outer.finish()[0]
+        results[7].start()
 
     steps_loop(local_pages * pairs, attend_back, {
         0: [lambda: r_inner.corner(2)],
         1: [lambda: r_inner.corner(3)],
-        2: [lambda: r_outer.column(1)],
+        2: [lambda: r_outer.column(1), lambda: r_inner.relay(3)],
         3: [lambda: r_outer.column(2)],
         4: [lambda: r_outer.column(3)],
-        5: [lambda: r_inner.plane(0)],
+        5: [lambda: r_inner.plane(0), lambda: r_inner.relay(2)],
         6: [lambda: r_inner.plane(1)],
-        7: [lambda: r_inner.plane(2)],
+        7: [lambda: r_inner.plane(2), lambda: r_inner.relay(1)],
         8: [lambda: r_inner.plane(3)],
-        9: [finish_outer],
+        9: [finish_outer, r_inner.settle],
     })
     for page in range(local_pages):
         send_kv(page)
-    s.p_one[1] = dot(x[...], d_q[...], TN).reshape(devices, rows, width).astype(BF)
+    s.p_one[1] = dot(x[...], d_q[...], TN).reshape(blocks).astype(BF)
     for dz in range(nz):
         r_first.begin(dz)
     add_row(vec, 0, d_q[...].astype(F32))
@@ -842,8 +962,8 @@
         total = total.reshape(tokens, width)
         if j == 1:
             add_row(vec, 1, total.astype(F32))
-        s.p_two[j] = dot(x[...], total, TN).reshape(devices, rows, width).astype(BF)
-    vectors = VectorSum(place, rest[40:44])
+        s.p_two[j] = dot(x[...], total, TN).reshape(blocks).astype(BF)
+    vectors = VectorSum(place, rest[8 + 4 * REDUCE_REFS:])
     vectors.put(0, vec[...])
     for dz in range(nz):
         r_second.begin(dz)
@@ -854,42 +974,97 @@
             return 0
         lax.fori_loop(start, nz, one, 0)
 
+    loop(0, r_first.arrive)
     loop(0, r_first.corner)
+    r_first.relay(3)
     loop(1, r_inner.column)
     vectors.put(1, vectors.take(0))
+    loop(0, r_second.arrive)
     loop(0, r_second.corner)
+    r_first.relay(2)
+    r_second.relay(3)
     vectors.put(2, vectors.take(1))
     loop(0, r_first.plane)
+    r_first.relay(1)
+    r_second.relay(2)
     vectors.put(3, vectors.take(2))
     loop(0, r_second.plane)
+    r_second.relay(1)
+    r_first.settle()
     d_keys, d_values = s.rk[...].reshape(tokens, width), s.rv[...].reshape(tokens, width)
     res[...] += dot(d_q[...], weight(s.g_attn, 0), NT)
     res[...] += dot(d_keys, weight(s.g_attn, 1), NT)
-    hidden_grad[...] = (res[...] + dot(d_values, weight(s.g_attn, 2), NT)).astype(BF)
+    s.grad[...] = (res[...] + dot(d_values, weight(s.g_attn, 2), NT)).astype(BF)
+    r_second.settle()
     total = r_inner.finish()
     for j in range(panels):
-        o_inner[:, j * width:(j + 1) * width] = total[j]
+        s.wide[:, j * width:(j + 1) * width] = total[j]
+    results[1].start()
+    results[6].start()
     loop(1, r_first.column)
     loop(1, r_second.column)
-    o_vec[...] = vectors.take(3)
+    s.total[...] = vectors.take(3)
+    results[8].start()
     total = r_first.finish()
-    o_o[...] = total[0]
-    o_q[...] = total[1]
+    s.squares[3] = total[0]
+    s.squares[0] = total[1]
+    results[2].start()
+    results[5].start()
     total = r_second.finish()
-    o_k[...] = total[0]
-    o_v[...] = total[1]
+    s.squares[1] = total[0]
+    s.squares[2] = total[1]
+    results[3].start()
+    results[4].start()
     tiny.drain()
     attn.drain()
     for one in reducers:
         one.drain()
     vectors.drain()
+    for result in results:
+        result.wait()
+
+
+def finish_kernel(rows, panels, out, grad, g_q, g_k, g_v, g_o, g_inner, g_outer, total, *refs):
+    outs, owned, held, sems = refs[:8], refs[8:8 + VECTORS + 1], refs[8 + VECTORS + 1:-1], refs[-1]
+    copies = [
+        (pltpu.make_async_copy(src, way, sems.at[i, 0]), pltpu.make_async_copy(way, dst, sems.at[i, 1]))
+        for i, (src, way, dst) in enumerate(zip((out, grad, g_q, g_k, g_v, g_o, g_inner, g_outer), held, outs))]
+    for copy, _ in copies:
+        copy.start()
+    for copy, onward in copies:
+        copy.wait()
+        onward.start()
+    at = lax.axis_index(PAGE) * 2 + lax.axis_index(SEQ)
+    width = total.shape[1]
+    mine = pltpu.roll(total[0:VECTORS, :], width - rows * at, 1)
+    for j, ref in enumerate(owned[:VECTORS]):
+        ref[...] = mine[j, :rows]
+    per_row = width // (panels * rows)
+    row = total[pl.ds(VECTORS + at // per_row, 1), :]
+    mine = pltpu.roll(row, width - panels * rows * lax.rem(at, per_row), 1)
+    owned[VECTORS][...] = mine[0, :panels * rows]
+    for _, onward in copies:
+        onward.wait()
+
+
+def finish(rows, panels, arrays):
+    hbm, vm = pl.BlockSpec(memory_space=pl.ANY), pl.BlockSpec(memory_space=VMEM)
+    return pl.pallas_call(
+        functools.partial(finish_kernel, rows, panels),
+        name="finish",
+        out_shape=tuple(jax.ShapeDtypeStruct(a.shape, a.dtype) for a in arrays[:8])
+        + (jax.ShapeDtypeStruct((rows,), F32),) * VECTORS + (jax.ShapeDtypeStruct((panels * rows,), F32),),
+        in_specs=[hbm] * 8 + [vm],
+        out_specs=(hbm,) * 8 + (vm,) * (VECTORS + 1),
+        scratch_shapes=[VMEM(a.shape, a.dtype) for a in arrays[:8]] + [DMA((8, 2))],
+    )(*arrays)
 
 
 def whole_layer(pages, heads, lengths, x, cot, wq, wk, wv, wo, wi, wout, small, local_pages):
     tokens, width = x.shape
     rows, panels = wq.shape[0], wi.shape[1] // width
     own, scratch = layer_scratch(pages, rows, width, panels, tokens, local_pages)
-    vm = pl.BlockSpec(memory_space=VMEM)
+    hbm = pl.BlockSpec(memory_space=pl.ANY)
     row_shape = jax.ShapeDtypeStruct((tokens, width), BF)
     square = jax.ShapeDtypeStruct((rows, width), F32)
     return pl.pallas_call(
@@ -899,8 +1074,8 @@
                    jax.ShapeDtypeStruct((rows, panels * width), F32),
                    jax.ShapeDtypeStruct((panels * rows, width), F32),
                    jax.ShapeDtypeStruct((VEC_ROWS, width), F32)),
-        in_specs=[pl.BlockSpec(memory_space=pltpu.SMEM)] + [vm] * 9,
-        out_specs=(vm,) * 9,
+        in_specs=[pl.BlockSpec(memory_space=pltpu.SMEM)] + [hbm] * 9,
+        out_specs=(hbm,) * 9,
         scratch_shapes=[*own.values(), *scratch],
         compiler_params=pltpu.CompilerParams(collective_id=0, has_side_effects=True, vmem_limit_bytes=61 << 20),
     )(lengths, x, cot, wq, wk, wv, wo, wi, wout, small)
@@ -1151,14 +1326,12 @@
                            w_inner, b_inner, w_outer, b_outer, ffn_gain, ffn_shift, cotangent)
     small = pack_vectors((b_query, b_value, b_output, attn_gain, attn_shift, b_outer, ffn_gain, ffn_shift), b_inner)
     flat = local_pages * seg, width
-    out, grad, g_q, g_k, g_v, g_o, g_inner, g_outer, total = whole_layer(
+    arrays = whole_layer(
         pages, HEADS, lengths, hidden.reshape(flat), cotangent.reshape(flat), w_query, w_key, w_value, w_output, w_inner, w_outer,
         small, local_pages)
-    at = lax.axis_index(PAGE) * 2 + lax.axis_index(SEQ)
-    own = [lax.dynamic_slice(total, (j, rows * at), (1, rows))[0] for j in range(VECTORS)]
-    wide = lax.dynamic_slice(total[VECTORS:VECTORS + panels].reshape(-1), (panels * rows * at,), (panels * rows,))
+    out, grad, g_q, g_k, g_v, g_o, g_inner, g_outer, *own = finish(rows, panels, arrays)
     return (out.reshape(hidden.shape), grad.reshape(hidden.shape), g_q, g_k, g_v, g_o, own[0], own[1], own[2], own[3], own[4],
-            g_inner, wide, g_outer, own[5], own[6], own[7])
+            g_inner, own[8], g_outer, own[5], own[6], own[7])
 
 
 def solution(mesh):

time: 180 us -> 161 us (0.89)
  local copies, waits for them, and re-layouts: 15.2 us -> 0.71 us
  Pallas kernels: 164 us -> 159 us
    unnamed x36 -> x18, local copies, waits for them, and re-layouts: 10.3 us -> 0.71 us
    pallas_call x1, Pallas kernels: 164 us -> 155 us  [whole_layer(): pl.pallas_call(functools.partial(layer_kernel, pages, heads, tuple(own)),...]
    pallas_call x0 -> x1, Pallas kernels: none -> 4.06 us  [finish(): pl.pallas_call(functools.partial(finish_kernel, rows, panels), name='fini...]
    another operation x9 -> x0, local copies, waits for them, and re-layouts: 1.92 us -> none  [pack_vectors(): return jnp.stack(rows)]
where the time goes in v3:
time: 161 us
  Pallas kernels  159 us (99%)
    pallas_call x1, Pallas kernels, whole_layer(): pl.pallas_call(functools.partial(layer_kernel, pages, heads, tuple(own)),...  155 us
    pallas_call x1, Pallas kernels, finish(): pl.pallas_call(functools.partial(finish_kernel, rows, panels), name='fini...  4.06 us

profile of v3, /device:TPU:0, one launch (start us, length us, event | category | flops | bytes accessed | tf_op | source)
XLA Modules:
  0.0 161.0 jit_solution(959892039709966117)
XLA Ops:
  0.7 0.0 copy-start.7
  0.7 0.0 copy-start.8
  0.7 0.0 copy-start.3
  0.7 0.0 copy-start.4
  0.7 0.0 copy-start.5
  0.7 0.0 copy-start.6
  0.7 0.0 copy-start
  0.7 0.0 copy-start.1
  0.7 0.0 copy-start.2
  0.7 0.6 copy-done.7
  1.3 0.0 copy-done.8
  1.3 0.0 copy-done.3
  1.3 0.0 copy-done.4
  1.4 0.0 copy-done.5
  1.4 0.0 copy-done.6
  1.4 0.0 copy-done
  1.4 0.0 copy-done.1
  1.4 0.0 copy-done.2
  1.4 0.6 pad_add_fusion.small
  2.1 154.7 %whole_layer.1 = (bf16[512,768]{1,0:T(8,128)(2,1)}, bf16[512,768]{1,0:T(8,128)(2,1)}, f32[24,768]{1,0:T(8,128)}, f32[24,768]{1,0:T(8,128)}, f32[24,768]{1,0:T(8,...) custom-call(s32[2]{0:T(128)} %lengths.1, bf16[512,768]{1,0:T(8,128)(2,1)} %bitcast.13, ...), custom_call_target="tpu_custom_call" | custom-call | tf_op jit(solution)/shard_map/whole_layer/pallas_call | solution.py:1070
  156.7 4.1 %finish.1 = (bf16[512,768]{1,0:T(8,128)(2,1)}, bf16[512,768]{1,0:T(8,128)(2,1)}, f32[24,768]{1,0:T(8,128)}, f32[24,768]{1,0:T(8,128)}, f32[24,768]{1,0:T(8,128)}...) custom-call(bf16[512,768]{1,0:T(8,128)(2,1)} %get-tuple-element.43.o, ...), custom_call_target="tpu_custom_call" | custom-call | tf_op jit(solution)/shard_map/finish/pallas_call | solution.py:1052
Async XLA Ops:
  0.7 0.7 copy-start.7
  0.7 0.7 copy-start.8
  0.7 0.7 copy-start.3
  0.7 0.7 copy-start.4
  0.7 0.7 copy-start.5
  0.7 0.7 copy-start.6
  0.7 0.7 copy-start
  0.7 0.7 copy-start.1
  0.7 0.7 copy-start.2

commit v4 on v3

--- a/solution.py
+++ b/solution.py
@@ -17,7 +17,7 @@
 AXES = PAGE, SEQ = ("page", "seq")
 SMALL, PANELS, ROWS = range(3)
 SPREAD_RELAY = 128
-RELAY = 0
+REDUCE_RELAY = 128
 
 
 def page_grid(pages):
@@ -223,18 +223,19 @@
                 group(g)
 
 
-def reduce_slots(pages):
+def reduce_slots(pages, low):
     nz, ny, nx = page_grid(pages)
     corners = nz * (nx - 1) * (ny - 1)
-    return slots((1, 1, 1, nz, nz)), slots((nz, corners, corners, nz * (nx - 1), nz * (ny - 1), nz - 1, 1, nz, nz))
-
-
-def reduce_scratch(pages, panels, rows, width, kind):
+    n = nz if low else 0
+    return slots((1, 1, 1, n, n)), slots((nz, corners, corners, nz * (nx - 1), nz * (ny - 1), nz - 1, 1, n, n))
+
+
+def reduce_scratch(pages, panels, rows, width, kind, low):
     nz, ny, nx = page_grid(pages)
     fx, fy = nx - 1, ny - 1
     half = (panels // 2, rows) if kind == PANELS else (panels, rows // 2)
-    rest = width - RELAY
-    (_, sends), (_, recvs) = reduce_slots(pages)
+    rest = width - low
+    (_, sends), (_, recvs) = reduce_slots(pages, low)
     return [
         VMEM((panels, nz * ny * nx, rows, width), BF),
         VMEM((nz * fx * fy,) + half + (rest,), BF),
@@ -242,8 +243,8 @@
         VMEM((nz * fx, panels, rows, rest), BF),
         VMEM((nz * fy, panels, rows, rest), BF),
         VMEM((nz - 1, panels, rows, rest), BF),
-        VMEM((ny * nx - 1, panels, rows, RELAY) if RELAY else (8, LANES), BF),
-        VMEM((2, nz, panels, ny * nx, rows, RELAY) if RELAY else (8, LANES), BF),
+        VMEM((ny * nx - 1, panels, rows, low) if low else (8, LANES), BF),
+        VMEM((2, nz, panels, ny * nx, rows, low) if low else (8, LANES), BF),
         DMA((sends,)),
         DMA((recvs,)),
     ]
@@ -253,10 +254,10 @@
 
 
 class Reduce:
-    def __init__(self, place, part, scratch, kind):
-        self.pl, self.part, self.kind = place, part, kind
+    def __init__(self, place, part, scratch, kind, low):
+        self.pl, self.part, self.kind, self.low = place, part, kind, low
         self.total, self.da, self.db, self.rx, self.ry, self.rz, self.rp, self.rr, self.send, self.recv = scratch
-        (self.sbase, _), (self.rbase, _) = reduce_slots(place.nz * place.plane)
+        (self.sbase, _), (self.rbase, _) = reduce_slots(place.nz * place.plane, low)
 
     def remote(self, send, recv, src, dst, target):
         return pltpu.make_async_remote_copy(
@@ -272,9 +273,9 @@
     def half(self, page, which):
         if self.kind == PANELS:
             n = self.total.shape[0] // 2
-            return self.total.at[which * n:(which + 1) * n, page, :, RELAY:]
+            return self.total.at[which * n:(which + 1) * n, page, :, self.low:]
         n = self.total.shape[2] // 2
-        return self.total.at[:, page, which * n:(which + 1) * n, RELAY:]
+        return self.total.at[:, page, which * n:(which + 1) * n, self.low:]
 
     def corner_slot(self, dz, dy, dx):
         return (dz * (self.pl.ny - 1) + dy - 1) * (self.pl.nx - 1) + dx - 1
@@ -296,28 +297,28 @@
     def x_copy(self, dz, dx):
         p = self.pl
         slot = dz * (p.nx - 1) + dx - 1
-        return self.plain(3, slot, self.total.at[:, p.page(dz, 0, dx), :, RELAY:], self.rx.at[slot], p.there(dx=dx))
+        return self.plain(3, slot, self.total.at[:, p.page(dz, 0, dx), :, self.low:], self.rx.at[slot], p.there(dx=dx))
 
     def y_copy(self, dz, dy):
         p = self.pl
         slot = dz * (p.ny - 1) + dy - 1
-        return self.plain(4, slot, self.total.at[:, p.page(dz, dy, 0), :, RELAY:], self.ry.at[slot], p.there(dy=dy))
+        return self.plain(4, slot, self.total.at[:, p.page(dz, dy, 0), :, self.low:], self.ry.at[slot], p.there(dy=dy))
 
     def z_copy(self, dz):
         p = self.pl
-        return self.plain(5, dz - 1, self.total.at[:, p.page(dz), :, RELAY:], self.rz.at[dz - 1], p.there(dz=dz))
+        return self.plain(5, dz - 1, self.total.at[:, p.page(dz), :, self.low:], self.rz.at[dz - 1], p.there(dz=dz))
 
     def relay_copy(self, level, up):
         p = self.pl
         group, way = level // p.plane, 0 if up else 1
         return self.remote(
             self.sbase[3 + way] + group, self.rbase[7 + way] + group,
-            self.total.at[:, pl.ds(level, p.plane), :, 0:RELAY], self.rr.at[way, group], p.there(dz=1 if up else p.nz - 1))
+            self.total.at[:, pl.ds(level, p.plane), :, 0:self.low], self.rr.at[way, group], p.there(dz=1 if up else p.nz - 1))
 
     def plane_copy(self, k, dy, dx):
         p = self.pl
         return self.remote(
-            self.sbase[2], self.rbase[6], self.total.at[:, p.page(0, dy, dx), :, 0:RELAY], self.rp.at[k], p.there(0, dy, dx))
+            self.sbase[2], self.rbase[6], self.total.at[:, p.page(0, dy, dx), :, 0:self.low], self.rp.at[k], p.there(0, dy, dx))
 
     def begin(self, dz):
         self.core_copy(dz).start()
@@ -326,36 +327,36 @@
         self.core_copy(dz).wait_recv()
 
     def pair(self, page):
-        return self.part[:, page, self.pl.c, :, RELAY:].astype(F32) + self.total[:, page, :, RELAY:].astype(F32)
+        return self.part[:, page, self.pl.c, :, self.low:].astype(F32) + self.total[:, page, :, self.low:].astype(F32)
 
     def corner(self, dz):
         p = self.pl
         for dy in range(1, p.ny):
             for dx in range(1, p.nx):
                 page = p.page(dz, dy, dx)
-                self.total[:, page, :, RELAY:] = self.pair(page).astype(BF)
+                self.total[:, page, :, self.low:] = self.pair(page).astype(BF)
                 self.xa_copy(dz, dy, dx).start()
                 self.yb_copy(dz, dy, dx).start()
 
     def level_sum(self, level):
         p = self.pl
         pages, group = pl.ds(level, p.plane), level // p.plane
-        total = self.part[:, pages, p.c, :, 0:RELAY].astype(F32) + self.total[:, pages, :, 0:RELAY].astype(F32)
+        total = self.part[:, pages, p.c, :, 0:self.low].astype(F32) + self.total[:, pages, :, 0:self.low].astype(F32)
         return total, pages, group
 
     def relay(self, d):
         p = self.pl
-        if not RELAY:
+        if not self.low:
             return
 
         def step(up):
             total, pages, group = self.level_sum((p.z + d if up else p.z - d) * p.plane)
-            self.total[:, pages, :, 0:RELAY] = total.astype(BF)
+            self.total[:, pages, :, 0:self.low] = total.astype(BF)
 
             def add():
                 self.relay_copy(group * p.plane, up).wait_recv()
                 got = self.rr[0 if up else 1, group].astype(F32)
-                self.total[:, pages, :, 0:RELAY] = (total + got).astype(BF)
+                self.total[:, pages, :, 0:self.low] = (total + got).astype(BF)
 
             pl.when(p.z > 0 if up else p.z < p.nz - 1)(add)
             self.relay_copy(group * p.plane, up).start()
@@ -365,15 +366,15 @@
 
     def settle(self):
         p = self.pl
-        if not RELAY:
+        if not self.low:
             return
         total, pages, group = self.level_sum(p.level(0))
-        self.total[:, pages, :, 0:RELAY] = total.astype(BF)
+        self.total[:, pages, :, 0:self.low] = total.astype(BF)
         for way in range(2):
             def add(way=way):
                 self.relay_copy(group * p.plane, way == 0).wait_recv()
-                self.total[:, pages, :, 0:RELAY] = (
-                    self.total[:, pages, :, 0:RELAY].astype(F32) + self.rr[way, group].astype(F32)).astype(BF)
+                self.total[:, pages, :, 0:self.low] = (
+                    self.total[:, pages, :, 0:self.low].astype(F32) + self.rr[way, group].astype(F32)).astype(BF)
             pl.when(p.z > 0 if way == 0 else p.z < p.nz - 1)(add)
         for k, (dy, dx) in enumerate(p.others):
             self.plane_copy(k, dy, dx).start()
@@ -381,7 +382,7 @@
     def owned(self):
         p = self.pl
         self.wait(self.rp, self.recv.at[self.rbase[6]])
-        total = self.total[:, p.page(), :, 0:RELAY].astype(F32)
+        total = self.total[:, p.page(), :, 0:self.low].astype(F32)
         for k in range(len(p.others)):
             total += self.rp[k].astype(F32)
         return total
@@ -401,7 +402,7 @@
             for dy in range(1, p.ny):
                 self.yb_copy(dz, dy, dx).wait_recv()
                 total = with_half(total, self.db[self.corner_slot(dz, dy, dx)].astype(F32), 1)
-            self.total[:, page, :, RELAY:] = total.astype(BF)
+            self.total[:, page, :, self.low:] = total.astype(BF)
             self.x_copy(dz, dx).start()
         for dy in range(1, p.ny):
             page = p.page(dz, dy, 0)
@@ -409,7 +410,7 @@
             for dx in range(1, p.nx):
                 self.xa_copy(dz, dy, dx).wait_recv()
                 total = with_half(total, self.da[self.corner_slot(dz, dy, dx)].astype(F32), 0)
-            self.total[:, page, :, RELAY:] = total.astype(BF)
+            self.total[:, page, :, self.low:] = total.astype(BF)
             self.y_copy(dz, dy).start()
 
     def column_sum(self, dz):
@@ -424,7 +425,7 @@
         return total
 
     def column(self, dz):
-        self.total[:, self.pl.page(dz), :, RELAY:] = self.column_sum(dz).astype(BF)
+        self.total[:, self.pl.page(dz), :, self.low:] = self.column_sum(dz).astype(BF)
         self.z_copy(dz).start()
 
     def finish(self):
@@ -432,14 +433,14 @@
         for dz in range(1, self.pl.nz):
             self.z_copy(dz).wait_recv()
             total += self.rz[dz - 1].astype(F32)
-        return jnp.concatenate([self.owned(), total], axis=2) if RELAY else total
+        return jnp.concatenate([self.owned(), total], axis=2) if self.low else total
 
     def drain(self):
         p = self.pl
         pages = p.nz * p.plane
         self.wait(self.part.at[:, :, 0], self.send.at[self.sbase[1]])
-        self.wait(self.total.at[:, 0:pages - 1, :, RELAY:], self.send.at[self.sbase[0]])
-        if not RELAY:
+        self.wait(self.total.at[:, 0:pages - 1, :, self.low:], self.send.at[self.sbase[0]])
+        if not self.low:
             return
         self.wait(self.rp, self.send.at[self.sbase[2]])
 
@@ -606,13 +607,14 @@
 def layer_scratch(pages, rows, width, panels, tokens, local_pages):
     (_, gather_sends), (_, gather_recvs) = gather_slots(pages)
     seg = tokens // local_pages
+    groups = width // (2 * LANES)
     own = dict(
         g_attn=VMEM((4, pages, 2, rows, width), BF),
         g_inner=VMEM((panels, pages, 2, rows, width), BF),
         g_outer=VMEM((1, pages, 2, panels * rows, width), BF),
         g_small=VMEM((1, pages, 2, VEC_ROWS, LANES), BF),
-        p_one=VMEM((2, pages, 2, rows, width), BF),
-        p_two=VMEM((2, pages, 2, rows, width), BF),
+        p_output=VMEM((2, pages, 2, rows, width // 2), BF),
+        p_groups=VMEM((groups, 6, pages, 2, rows, LANES), BF),
         xs=VMEM((tokens, width), BF),
         q=VMEM((tokens, width), BF),
         k=VMEM((local_pages, 2 * seg, width), BF),
@@ -639,12 +641,14 @@
         in_sem=DMA((8 + panels,)),
         out_sem=DMA((9,)),
         x_sem=DMA((2,)),
-        kv_sem=DMA((4, local_pages)),
+        kv_sem=DMA((4, groups)),
     )
     gather = [DMA((gather_sends,)), DMA((gather_recvs,))] * 4
     reduce = []
-    for count, size, kind in ((1, panels * rows, ROWS), (panels, rows, PANELS), (2, rows, PANELS), (2, rows, PANELS)):
-        reduce += reduce_scratch(pages, count, size, width, kind)
+    parts = [(1, panels * rows, width, ROWS, REDUCE_RELAY), (panels, rows, width, PANELS, REDUCE_RELAY)]
+    parts += [(2, rows, width // 2, PANELS, 0)] + [(6, rows, LANES, PANELS, 0)] * groups
+    for part in parts:
+        reduce += reduce_scratch(pages, *part)
     return own, gather + reduce + vector_scratch(pages, VEC_ROWS, width)
 
 
@@ -721,8 +725,22 @@
         one.finish_core()
     x_copy.wait()
 
+    def begin_all(one):
+        for dz in range(nz):
+            one.begin(dz)
+
+    def corners(one):
+        loop(0, one.arrive)
+        loop(0, one.corner)
+
     def weight(ref, j):
         return ref[j].reshape(full)
+
+    def loop(start, body):
+        def one(dz, _):
+            body(dz)
+            return 0
+        lax.fori_loop(start, nz, one, 0)
 
     def outer_weight(j):
         n = pages // panels
@@ -845,10 +863,12 @@
     chunks(norm_two)
     results[0].start()
 
+    parts = [(s.g_outer, ROWS, REDUCE_RELAY), (s.g_inner, PANELS, REDUCE_RELAY), (s.p_output, PANELS, 0)]
+    parts += [(s.p_groups.at[g], PANELS, 0) for g in range(s.p_groups.shape[0])]
     reducers = [
-        Reduce(place, part, rest[8 + REDUCE_REFS * i:8 + REDUCE_REFS * (i + 1)], kind)
-        for i, (part, kind) in enumerate(((s.g_outer, ROWS), (s.g_inner, PANELS), (s.p_one, PANELS), (s.p_two, PANELS)))]
-    r_outer, r_inner, r_first, r_second = reducers
+        Reduce(place, part, rest[8 + REDUCE_REFS * i:8 + REDUCE_REFS * (i + 1)], kind, low)
+        for i, (part, kind, low) in enumerate(parts)]
+    r_outer, r_inner, r_output, *r_groups = reducers
     outer.drain()
 
     def outer_back(dz):
@@ -874,13 +894,12 @@
         s.g_inner[j] = dot(s.low[...], d_pre, TN).reshape(blocks).astype(BF)
 
     steps_loop(panels, inner_back, {
-        0: [lambda: r_outer.arrive(3), lambda: r_outer.corner(3), lambda: r_outer.relay(3), lambda: r_outer.plane(0)],
-        1: [lambda: r_outer.plane(1), lambda: r_outer.relay(2)],
-        2: [lambda: r_outer.plane(2), lambda: r_outer.relay(1)],
-        3: [lambda: r_outer.plane(3), r_outer.settle],
+        0: [lambda: r_outer.arrive(3), lambda: r_outer.corner(3), lambda: r_outer.plane(0), lambda: r_outer.relay(3)],
+        1: [lambda: r_outer.plane(1)],
+        2: [lambda: r_outer.plane(2), lambda: r_outer.relay(2)],
+        3: [lambda: r_outer.plane(3)],
     })
-    for dz in range(nz):
-        r_inner.begin(dz)
+    begin_all(r_inner)
 
     def norm_one_back(at):
         grad, xhat = res[at, :], s.xhat[at, :]
@@ -894,132 +913,145 @@
 
     chunks(norm_one_back)
     s.d_ctx[...] = dot(s.d_low[...], weight(s.g_attn, 3), NT).astype(BF)
-    s.p_one[0] = dot(ctx[...], s.d_low[...], TN).reshape(blocks).astype(BF)
-    for dz in range(nz):
-        r_inner.arrive(dz)
+    grad = dot(ctx[...], s.d_low[...], TN).reshape(blocks)
+    half = width // 2
+    for j in range(2):
+        s.p_output[j] = grad[..., j * half:(j + 1) * half].astype(BF)
+    begin_all(r_output)
+    r_outer.relay(1)
+    r_inner.arrive(0)
     r_inner.corner(0)
+    r_inner.arrive(3)
+    r_inner.corner(3)
+    r_inner.arrive(1)
     r_inner.corner(1)
+    r_inner.arrive(2)
+    r_inner.corner(2)
+    r_inner.relay(3)
 
     d_q, d_k, d_v = s.post.at[0], s.post.at[1:1 + local_pages], s.slope.at[0:local_pages]
 
-    def kv_copies(page):
+    def kv_copies(g):
         theirs = pl.ds(pl.multiple_of((1 - c) * seg, seg), seg)
+        cols = slice(2 * LANES * g, 2 * LANES * (g + 1))
         return [
             pltpu.make_async_remote_copy(
-                src_ref=grad.at[page, theirs], dst_ref=got.at[page], send_sem=s.kv_sem.at[2 * n, page],
-                recv_sem=s.kv_sem.at[2 * n + 1, page], device_id=sibling, device_id_type=MESH)
+                src_ref=grad.at[:, theirs, cols], dst_ref=got.at[:, :, cols], send_sem=s.kv_sem.at[2 * n, g],
+                recv_sem=s.kv_sem.at[2 * n + 1, g], device_id=sibling, device_id_type=MESH)
             for n, (grad, got) in enumerate(((d_k, s.rk), (d_v, s.rv)))]
 
+    def exchange(g):
+        for copy in kv_copies(g):
+            copy.start()
+
+    def group_grads(g):
+        cols = slice(2 * LANES * g, 2 * LANES * (g + 1))
+        for copy in kv_copies(g):
+            copy.wait_recv()
+        ours = pl.ds(pl.multiple_of(c * seg, seg), seg)
+        for j in range(3):
+            if j == 0:
+                total = d_q[:, cols]
+            else:
+                mine_k, got = ((d_k, s.rk), (d_v, s.rv))[j - 1]
+                total = (mine_k[:, ours, cols].astype(F32) + got[:, :, cols].astype(F32)).astype(BF)
+                got[:, :, cols] = total
+                total = total.reshape(tokens, 2 * LANES)
+            if j != 1:
+                vec[j // 2:j // 2 + 1, cols] = jnp.sum(total.astype(F32), axis=0, keepdims=True)
+            grad = dot(x[...], total, TN).reshape(pages, 2, rows, 2 * LANES)
+            for n in range(2):
+                s.p_groups[g, 2 * j + n] = grad[..., n * LANES:(n + 1) * LANES].astype(BF)
+        for dz in range(nz):
+            r_groups[g].begin(dz)
+
     def attend_back(i):
-        page, rows_of, cols = place_of(i)
+        page, rows_of, cols = place_of(lax.rem(i, local_pages) * pairs + i // local_pages)
         q2, k2, v2 = q[rows_of, cols], k[page, :, cols], v[page, :, cols]
         c2 = s.d_ctx[rows_of, cols]
         usable = key_at < lengths[page]
-        parts = []
+        found = []
         for head in range(2):
             p = probabilities(q2, k2, head, usable)
             d_p = dot(c2, one_head(v2, head), NT)
             d_s = (p * (d_p - jnp.sum(p * d_p, axis=-1, keepdims=True))).astype(BF)
-            parts.append((dot(d_s, k2), dot(d_s, q2, TN), dot(p.astype(BF), c2, TN)))
-        both = [jnp.where(low_half, one, two) for one, two in zip(*parts)]
+            found.append((dot(d_s, k2), dot(d_s, q2, TN), dot(p.astype(BF), c2, TN)))
+        both = [jnp.where(low_half, one, two) for one, two in zip(*found)]
         d_q[rows_of, cols] = (both[0] * scale).astype(BF)
         d_k[page, :, cols] = (both[1] * scale).astype(BF)
         d_v[page, :, cols] = both[2].astype(BF)
 
-    def send_kv(page):
-        for copy in kv_copies(page):
-            copy.start()
-
     def finish_outer():
         s.tall[...] = r_outer.finish()[0]
         results[7].start()
 
+    def finish_inner():
+        total = r_inner.finish()
+        for j in range(panels):
+            s.wide[:, j * width:(j + 1) * width] = total[j]
+        results[6].start()
+
+    def finish_output():
+        total = r_output.finish()
+        for j in range(2):
+            s.squares[3, :, j * half:(j + 1) * half] = total[j]
+        results[5].start()
+
+    def finish_group(g):
+        total = r_groups[g].finish()
+        for j in range(3):
+            for n in range(2):
+                at = (2 * g + n) * LANES
+                s.squares[j, :, at:at + LANES] = total[2 * j + n]
+
+    vectors = VectorSum(place, rest[8 + len(reducers) * REDUCE_REFS:])
     steps_loop(local_pages * pairs, attend_back, {
-        0: [lambda: r_inner.corner(2)],
-        1: [lambda: r_inner.corner(3)],
-        2: [lambda: r_outer.column(1), lambda: r_inner.relay(3)],
-        3: [lambda: r_outer.column(2)],
-        4: [lambda: r_outer.column(3)],
-        5: [lambda: r_inner.plane(0), lambda: r_inner.relay(2)],
-        6: [lambda: r_inner.plane(1)],
-        7: [lambda: r_inner.plane(2), lambda: r_inner.relay(1)],
-        8: [lambda: r_inner.plane(3)],
-        9: [finish_outer, r_inner.settle],
+        0: [lambda: r_outer.column(1)],
+        1: [lambda: r_outer.column(2), lambda: r_outer.column(3), lambda: r_outer.settle()],
+        2: [lambda: corners(r_output)],
+        3: [lambda: r_inner.plane(0), lambda: exchange(0)],
+        4: [lambda: r_inner.relay(2), lambda: r_inner.plane(1)],
+        5: [lambda: finish_outer(), lambda: r_inner.plane(2), lambda: r_inner.plane(3), lambda: group_grads(0)],
+        6: [lambda: r_inner.relay(1), lambda: loop(0, r_output.plane)],
+        7: [lambda: exchange(1), lambda: corners(r_groups[0])],
+        8: [lambda: r_inner.column(1), lambda: r_inner.column(2), lambda: r_inner.column(3)],
+        9: [lambda: r_inner.settle(), lambda: group_grads(1)],
+        10: [lambda: loop(0, r_groups[0].plane)],
+        11: [lambda: exchange(2), lambda: corners(r_groups[1])],
     })
-    for page in range(local_pages):
-        send_kv(page)
-    s.p_one[1] = dot(x[...], d_q[...], TN).reshape(blocks).astype(BF)
-    for dz in range(nz):
-        r_first.begin(dz)
-    add_row(vec, 0, d_q[...].astype(F32))
-    for page in range(local_pages):
-        for copy in kv_copies(page):
-            copy.wait()
-    ours = pl.ds(pl.multiple_of(c * seg, seg), seg)
-    for j, (grad, got) in enumerate(((d_k, s.rk), (d_v, s.rv))):
-        total = (grad[:, ours, :].astype(F32) + got[...].astype(F32)).astype(BF)
-        got[...] = total
-        total = total.reshape(tokens, width)
-        if j == 1:
-            add_row(vec, 1, total.astype(F32))
-        s.p_two[j] = dot(x[...], total, TN).reshape(blocks).astype(BF)
-    vectors = VectorSum(place, rest[8 + 4 * REDUCE_REFS:])
+    loop(1, r_output.column)
+    res[...] += dot(d_q[...], weight(s.g_attn, 0), NT)
+    group_grads(2)
     vectors.put(0, vec[...])
-    for dz in range(nz):
-        r_second.begin(dz)
-
-    def loop(start, body):
-        def one(dz, _):
-            body(dz)
-            return 0
-        lax.fori_loop(start, nz, one, 0)
-
-    loop(0, r_first.arrive)
-    loop(0, r_first.corner)
-    r_first.relay(3)
-    loop(1, r_inner.column)
+    loop(0, r_groups[1].plane)
+    loop(1, r_groups[0].column)
+    corners(r_groups[2])
     vectors.put(1, vectors.take(0))
-    loop(0, r_second.arrive)
-    loop(0, r_second.corner)
-    r_first.relay(2)
-    r_second.relay(3)
+    res[...] += dot(s.rk[...].reshape(tokens, width), weight(s.g_attn, 1), NT)
     vectors.put(2, vectors.take(1))
-    loop(0, r_first.plane)
-    r_first.relay(1)
-    r_second.relay(2)
+    loop(0, r_groups[2].plane)
+    loop(1, r_groups[1].column)
+    s.grad[...] = (res[...] + dot(s.rv[...].reshape(tokens, width), weight(s.g_attn, 2), NT)).astype(BF)
+    results[1].start()
     vectors.put(3, vectors.take(2))
-    loop(0, r_second.plane)
-    r_second.relay(1)
-    r_first.settle()
-    d_keys, d_values = s.rk[...].reshape(tokens, width), s.rv[...].reshape(tokens, width)
-    res[...] += dot(d_q[...], weight(s.g_attn, 0), NT)
-    res[...] += dot(d_keys, weight(s.g_attn, 1), NT)
-    s.grad[...] = (res[...] + dot(d_values, weight(s.g_attn, 2), NT)).astype(BF)
-    r_second.settle()
-    total = r_inner.finish()
-    for j in range(panels):
-        s.wide[:, j * width:(j + 1) * width] = total[j]
-    results[1].start()
-    results[6].start()
-    loop(1, r_first.column)
-    loop(1, r_second.column)
+    finish_inner()
+    finish_output()
+    loop(1, r_groups[2].column)
+    finish_group(1)
+    finish_group(2)
+    finish_group(0)
     s.total[...] = vectors.take(3)
     results[8].start()
-    total = r_first.finish()
-    s.squares[3] = total[0]
-    s.squares[0] = total[1]
-    results[2].start()
-    results[5].start()
-    total = r_second.finish()
-    s.squares[1] = total[0]
-    s.squares[2] = total[1]
-    results[3].start()
-    results[4].start()
+    for i in (2, 3, 4):
+        results[i].start()
     tiny.drain()
     attn.drain()
     for one in reducers:
         one.drain()
     vectors.drain()
+    for g in range(len(r_groups)):
+        for copy in kv_copies(g):
+            copy.wait_send()
     for result in results:
         result.wait()
 

time: 161 us -> 155 us (0.963)
  Pallas kernels: 159 us -> 152 us
    pallas_call x1, Pallas kernels: 155 us -> 148 us  [whole_layer(): pl.pallas_call(functools.partial(layer_kernel, pages, heads, tuple(own)),...]
where the time goes in v4:
time: 155 us; the launch traced here: 154 us
  Pallas kernels  152 us (98%)
    pallas_call x1, Pallas kernels, whole_layer(): pl.pallas_call(functools.partial(layer_kernel, pages, heads, tuple(own)),...  148 us
    pallas_call x1, Pallas kernels, finish(): pl.pallas_call(functools.partial(finish_kernel, rows, panels), name='fini...  4.06 us

profile of v4, /device:TPU:0, one launch (start us, length us, event | category | flops | bytes accessed | tf_op | source)
XLA Modules:
  0.0 154.4 jit_solution(14534884149994777586)
XLA Ops:
  0.7 0.0 copy-start.7
  0.7 0.0 copy-start.8
  0.7 0.0 copy-start.3
  0.7 0.0 copy-start.4
  0.7 0.0 copy-start.5
  0.7 0.0 copy-start.6
  0.7 0.0 copy-start
  0.7 0.0 copy-start.1
  0.7 0.0 copy-start.2
  0.7 0.6 copy-done.7
  1.3 0.0 copy-done.8
  1.3 0.0 copy-done.3
  1.3 0.0 copy-done.4
  1.4 0.0 copy-done.5
  1.4 0.0 copy-done.6
  1.4 0.0 copy-done
  1.4 0.0 copy-done.1
  1.4 0.0 copy-done.2
  1.4 0.6 pad_add_fusion.small
  2.1 148.1 %whole_layer.1 = (bf16[512,768]{1,0:T(8,128)(2,1)}, bf16[512,768]{1,0:T(8,128)(2,1)}, f32[24,768]{1,0:T(8,128)}, f32[24,768]{1,0:T(8,128)}, f32[24,768]{1,0:T(8,...) custom-call(s32[2]{0:T(128)} %lengths.1, bf16[512,768]{1,0:T(8,128)(2,1)} %bitcast.13, ...), custom_call_target="tpu_custom_call" | custom-call | tf_op jit(solution)/shard_map/whole_layer/pallas_call | solution.py:1102
  150.1 4.1 %finish.1 = (bf16[512,768]{1,0:T(8,128)(2,1)}, bf16[512,768]{1,0:T(8,128)(2,1)}, f32[24,768]{1,0:T(8,128)}, f32[24,768]{1,0:T(8,128)}, f32[24,768]{1,0:T(8,128)}...) custom-call(bf16[512,768]{1,0:T(8,128)(2,1)} %get-tuple-element.43.o, ...), custom_call_target="tpu_custom_call" | custom-call | tf_op jit(solution)/shard_map/finish/pallas_call | solution.py:1084
Async XLA Ops:
  0.7 0.7 copy-start.7
  0.7 0.7 copy-start.8
  0.7 0.7 copy-start.3
  0.7 0.7 copy-start.4
  0.7 0.7 copy-start.5
  0.7 0.7 copy-start.6
  0.7 0.7 copy-start
  0.7 0.7 copy-start.1
  0.7 0.7 copy-start.2

commit v5 on v4

--- a/solution.py
+++ b/solution.py
@@ -37,16 +37,17 @@
         self.y = lax.rem(self.p // self.nx, self.ny)
         self.z = self.p // self.plane
         self.sibling = (self.p, 1 - self.c)
+        ys = [lax.rem(self.y + d, self.ny) * self.nx for d in range(self.ny)]
+        xs = [lax.rem(self.x + d, self.nx) for d in range(self.nx)]
+        self.levels = [lax.rem(self.z + d, self.nz) * self.plane for d in range(self.nz)]
+        self.pages = [[[level + y + x for x in xs] for y in ys] for level in self.levels]
         self.others = [(dy, dx) for dy in range(self.ny) for dx in range(self.nx) if dy or dx]
 
     def page(self, dz=0, dy=0, dx=0):
-        z = lax.rem(self.z + dz + self.nz, self.nz)
-        y = lax.rem(self.y + dy + self.ny, self.ny)
-        x = lax.rem(self.x + dx + self.nx, self.nx)
-        return (z * self.ny + y) * self.nx + x
+        return self.pages[dz % self.nz][dy % self.ny][dx % self.nx]
 
     def level(self, dz):
-        return lax.rem(self.z + dz + self.nz, self.nz) * self.plane
+        return self.levels[dz % self.nz]
 
     def there(self, dz=0, dy=0, dx=0):
         return self.page(dz, dy, dx), self.c
@@ -128,9 +129,9 @@
     def core_copy(self, page, part, count=None):
         return self.copy(self.view(page, part, None, count), self.sbase[1], self.rbase[6], self.pl.sibling)
 
-    def relay_copy(self, level, up):
-        p = self.pl
-        group = level // p.plane
+    def relay_copy(self, group, up):
+        p = self.pl
+        level = group * p.plane
         target = p.there(dz=1 if up else p.nz - 1)
         return self.copy(self.view(level, 3, None, p.plane), self.sbase[3 if up else 4] + group, self.rbase[5] + group, target)
 
@@ -163,8 +164,8 @@
             return
         level = p.level(0)
         self.wait(self.view(level, 3, None, p.plane - 1), self.recv.at[self.rbase[4]])
-        pl.when(p.z < p.nz - 1)(lambda: self.relay_copy(level, True).start())
-        pl.when(p.z > 0)(lambda: self.relay_copy(level, False).start())
+        pl.when(p.z < p.nz - 1)(lambda: self.relay_copy(p.z, True).start())
+        pl.when(p.z > 0)(lambda: self.relay_copy(p.z, False).start())
         self.core_copy(level, 3, p.plane).start()
 
     def relay(self, d):
@@ -173,10 +174,10 @@
             return
 
         def step(up):
-            level = (p.z - d if up else p.z + d) * p.plane
-            self.relay_copy(level, up).wait_recv()
-            pl.when(p.z < p.nz - 1 if up else p.z > 0)(lambda: self.relay_copy(level, up).start())
-            self.core_copy(level, 3, p.plane).start()
+            group = p.z - d if up else p.z + d
+            self.relay_copy(group, up).wait_recv()
+            pl.when(p.z < p.nz - 1 if up else p.z > 0)(lambda: self.relay_copy(group, up).start())
+            self.core_copy(group * p.plane, 3, p.plane).start()
 
         pl.when(p.z >= d)(lambda: step(True))
         pl.when(p.z + d < p.nz)(lambda: step(False))
@@ -217,8 +218,8 @@
         self.wait(self.view(0, 0, None, blocks), self.send.at[self.sbase[0]])
         if self.low:
             def group(g):
-                pl.when(jnp.logical_and(p.z < p.nz - 1, g <= p.z))(lambda: self.relay_copy(g * p.plane, True).wait_send())
-                pl.when(jnp.logical_and(p.z > 0, g >= p.z))(lambda: self.relay_copy(g * p.plane, False).wait_send())
+                pl.when(jnp.logical_and(p.z < p.nz - 1, g <= p.z))(lambda: self.relay_copy(g, True).wait_send())
+                pl.when(jnp.logical_and(p.z > 0, g >= p.z))(lambda: self.relay_copy(g, False).wait_send())
             for g in range(p.nz):
                 group(g)
 
@@ -280,9 +281,9 @@
     def corner_slot(self, dz, dy, dx):
         return (dz * (self.pl.ny - 1) + dy - 1) * (self.pl.nx - 1) + dx - 1
 
-    def core_copy(self, dz):
-        p = self.pl
-        pages = pl.ds(p.level(dz), p.plane)
+    def core_copy(self, dz, level=None):
+        p = self.pl
+        pages = pl.ds(p.level(dz) if level is None else level, p.plane)
         return self.remote(
             self.sbase[1], self.rbase[0] + dz, self.part.at[:, pages, 1 - p.c], self.total.at[:, pages], p.sibling)
 
@@ -308,9 +309,9 @@
         p = self.pl
         return self.plain(5, dz - 1, self.total.at[:, p.page(dz), :, self.low:], self.rz.at[dz - 1], p.there(dz=dz))
 
-    def relay_copy(self, level, up):
-        p = self.pl
-        group, way = level // p.plane, 0 if up else 1
+    def relay_copy(self, group, up):
+        p = self.pl
+        level, way = group * p.plane, 0 if up else 1
         return self.remote(
             self.sbase[3 + way] + group, self.rbase[7 + way] + group,
             self.total.at[:, pl.ds(level, p.plane), :, 0:self.low], self.rr.at[way, group], p.there(dz=1 if up else p.nz - 1))
@@ -320,8 +321,8 @@
         return self.remote(
             self.sbase[2], self.rbase[6], self.total.at[:, p.page(0, dy, dx), :, 0:self.low], self.rp.at[k], p.there(0, dy, dx))
 
-    def begin(self, dz):
-        self.core_copy(dz).start()
+    def begin(self, dz, level=None):
+        self.core_copy(dz, level).start()
 
     def arrive(self, dz):
         self.core_copy(dz).wait_recv()
@@ -338,11 +339,11 @@
                 self.xa_copy(dz, dy, dx).start()
                 self.yb_copy(dz, dy, dx).start()
 
-    def level_sum(self, level):
-        p = self.pl
-        pages, group = pl.ds(level, p.plane), level // p.plane
+    def level_sum(self, group):
+        p = self.pl
+        pages = pl.ds(group * p.plane, p.plane)
         total = self.part[:, pages, p.c, :, 0:self.low].astype(F32) + self.total[:, pages, :, 0:self.low].astype(F32)
-        return total, pages, group
+        return total, pages
 
     def relay(self, d):
         p = self.pl
@@ -350,16 +351,17 @@
             return
 
         def step(up):
-            total, pages, group = self.level_sum((p.z + d if up else p.z - d) * p.plane)
+            group = p.z + d if up else p.z - d
+            total, pages = self.level_sum(group)
             self.total[:, pages, :, 0:self.low] = total.astype(BF)
 
             def add():
-                self.relay_copy(group * p.plane, up).wait_recv()
+                self.relay_copy(group, up).wait_recv()
                 got = self.rr[0 if up else 1, group].astype(F32)
                 self.total[:, pages, :, 0:self.low] = (total + got).astype(BF)
 
             pl.when(p.z > 0 if up else p.z < p.nz - 1)(add)
-            self.relay_copy(group * p.plane, up).start()
+            self.relay_copy(group, up).start()
 
         pl.when(p.z + d < p.nz)(lambda: step(True))
         pl.when(p.z >= d)(lambda: step(False))
@@ -368,11 +370,12 @@
         p = self.pl
         if not self.low:
             return
-        total, pages, group = self.level_sum(p.level(0))
+        group = p.z
+        total, pages = self.level_sum(group)
         self.total[:, pages, :, 0:self.low] = total.astype(BF)
         for way in range(2):
             def add(way=way):
-                self.relay_copy(group * p.plane, way == 0).wait_recv()
+                self.relay_copy(group, way == 0).wait_recv()
                 self.total[:, pages, :, 0:self.low] = (
                     self.total[:, pages, :, 0:self.low].astype(F32) + self.rr[way, group].astype(F32)).astype(BF)
             pl.when(p.z > 0 if way == 0 else p.z < p.nz - 1)(add)
@@ -445,8 +448,8 @@
         self.wait(self.rp, self.send.at[self.sbase[2]])
 
         def group(g):
-            pl.when(g > p.z)(lambda: self.relay_copy(g * p.plane, True).wait_send())
-            pl.when(g < p.z)(lambda: self.relay_copy(g * p.plane, False).wait_send())
+            pl.when(g > p.z)(lambda: self.relay_copy(g, True).wait_send())
+            pl.when(g < p.z)(lambda: self.relay_copy(g, False).wait_send())
 
         for g in range(p.nz):
             group(g)
@@ -454,21 +457,20 @@
 
 def vector_scratch(pages, rows, width):
     nz, ny, nx = page_grid(pages)
-    n = 1 + nx - 1 + ny - 1 + nz - 1
-    return [VMEM((4, rows, width), F32), VMEM((n, rows, width), F32), DMA((n,)), DMA((n,))]
+    n = 1 + ny * nx - 1 + nz - 1
+    return [VMEM((3, rows, width), F32), VMEM((3, rows, width), BF), VMEM((n, rows, width), BF), DMA((n,)), DMA((n,))]
 
 
 class VectorSum:
     def __init__(self, place, scratch):
         self.pl = place
-        self.held, self.got, self.send, self.recv = scratch
+        self.own, self.held, self.got, self.send, self.recv = scratch
 
     def legs(self):
         p = self.pl
         return [
             [p.sibling],
-            [p.there(dx=d) for d in range(1, p.nx)],
-            [p.there(dy=d) for d in range(1, p.ny)],
+            [p.there(0, dy, dx) for dy, dx in p.others],
             [p.there(dz=d) for d in range(1, p.nz)],
         ]
 
@@ -483,20 +485,21 @@
         ], at
 
     def put(self, leg, value):
-        self.held[leg] = value
+        self.own[leg] = value
+        self.held[leg] = value.astype(BF)
         for copy in self.copies(leg)[0]:
             copy.start()
 
     def take(self, leg):
         copies, at = self.copies(leg)
-        value = self.held[leg]
+        value = self.own[leg]
         for i, copy in enumerate(copies):
             copy.wait_recv()
-            value += self.got[at + i]
+            value += self.got[at + i].astype(F32)
         return value
 
     def drain(self):
-        for leg in range(4):
+        for leg in range(3):
             for copy in self.copies(leg)[0]:
                 copy.wait_send()
 
@@ -710,17 +713,18 @@
     for dz in range(nz):
         for one in first:
             one.plane(dz)
+    inner.spread(0)
     attn.relay(1)
-    inner.spread(0)
     attn.relay(2)
     for dz in range(1, nz):
         inner.column(dz)
     attn.relay(3)
     inner.rise()
+    outer.begin()
+    outer.spread(0)
     for dz in range(nz):
         for one in first:
             one.corner(dz)
-    outer.begin()
     for one in first:
         one.finish_core()
     x_copy.wait()
@@ -737,10 +741,8 @@
         return ref[j].reshape(full)
 
     def loop(start, body):
-        def one(dz, _):
+        for dz in range(start, nz):
             body(dz)
-            return 0
-        lax.fori_loop(start, nz, one, 0)
 
     def outer_weight(j):
         n = pages // panels
@@ -795,7 +797,7 @@
         ctx[rows_of, cols] = jnp.where(low_half, *parts).astype(BF)
 
     steps_loop(local_pages * pairs, attend, {
-        0: [lambda: inner.plane(3), lambda: inner.relay(1), lambda: outer.spread(0)],
+        0: [lambda: inner.plane(3), lambda: inner.relay(1)],
         1: [lambda: outer.column(1), lambda: inner.relay(2)],
         2: [lambda: outer.column(2), outer.rise],
         3: [lambda: outer.column(3), lambda: inner.relay(3)],
@@ -877,7 +879,7 @@
         d_pre = (dot(d_low, outer_weight(j), NT) * s.slope[j].astype(F32)).astype(BF)
         n = pages // panels
         s.g_outer[0, pl.ds(j * n, n)] = dot(s.post[j], d_low, TN).reshape(n, 2, panels * rows, width).astype(BF)
-        r_outer.begin(dz)
+        r_outer.begin(dz, j * place.plane)
         s.slope[j] = d_pre
         vec[pl.ds(VECTORS + j, 1), :] = jnp.sum(d_pre.astype(F32), axis=0, keepdims=True)
 
@@ -919,6 +921,7 @@
         s.p_output[j] = grad[..., j * half:(j + 1) * half].astype(BF)
     begin_all(r_output)
     r_outer.relay(1)
+    r_outer.column(1)
     r_inner.arrive(0)
     r_inner.corner(0)
     r_inner.arrive(3)
@@ -1006,41 +1009,40 @@
 
     vectors = VectorSum(place, rest[8 + len(reducers) * REDUCE_REFS:])
     steps_loop(local_pages * pairs, attend_back, {
-        0: [lambda: r_outer.column(1)],
-        1: [lambda: r_outer.column(2), lambda: r_outer.column(3), lambda: r_outer.settle()],
+        0: [lambda: r_outer.column(2), lambda: r_outer.column(3)],
+        1: [lambda: r_outer.settle()],
         2: [lambda: corners(r_output)],
         3: [lambda: r_inner.plane(0), lambda: exchange(0)],
         4: [lambda: r_inner.relay(2), lambda: r_inner.plane(1)],
-        5: [lambda: finish_outer(), lambda: r_inner.plane(2), lambda: r_inner.plane(3), lambda: group_grads(0)],
+        5: [lambda: r_inner.plane(2), lambda: r_inner.plane(3), lambda: group_grads(0)],
         6: [lambda: r_inner.relay(1), lambda: loop(0, r_output.plane)],
-        7: [lambda: exchange(1), lambda: corners(r_groups[0])],
+        7: [lambda: exchange(1), lambda: corners(r_groups[0]), lambda: finish_outer()],
         8: [lambda: r_inner.column(1), lambda: r_inner.column(2), lambda: r_inner.column(3)],
         9: [lambda: r_inner.settle(), lambda: group_grads(1)],
         10: [lambda: loop(0, r_groups[0].plane)],
         11: [lambda: exchange(2), lambda: corners(r_groups[1])],
     })
     loop(1, r_output.column)
-    res[...] += dot(d_q[...], weight(s.g_attn, 0), NT)
     group_grads(2)
     vectors.put(0, vec[...])
     loop(0, r_groups[1].plane)
     loop(1, r_groups[0].column)
     corners(r_groups[2])
     vectors.put(1, vectors.take(0))
-    res[...] += dot(s.rk[...].reshape(tokens, width), weight(s.g_attn, 1), NT)
-    vectors.put(2, vectors.take(1))
+    res[...] += dot(d_q[...], weight(s.g_attn, 0), NT)
     loop(0, r_groups[2].plane)
     loop(1, r_groups[1].column)
+    vectors.put(2, vectors.take(1))
+    res[...] += dot(s.rk[...].reshape(tokens, width), weight(s.g_attn, 1), NT)
+    loop(1, r_groups[2].column)
     s.grad[...] = (res[...] + dot(s.rv[...].reshape(tokens, width), weight(s.g_attn, 2), NT)).astype(BF)
     results[1].start()
-    vectors.put(3, vectors.take(2))
     finish_inner()
     finish_output()
-    loop(1, r_groups[2].column)
     finish_group(1)
     finish_group(2)
     finish_group(0)
-    s.total[...] = vectors.take(3)
+    s.total[...] = vectors.take(2)
     results[8].start()
     for i in (2, 3, 4):
         results[i].start()

time: 155 us -> 151 us (0.974)
  Pallas kernels: 152 us -> 148 us
    pallas_call x1, Pallas kernels: 148 us -> 144 us  [whole_layer(): pl.pallas_call(functools.partial(layer_kernel, pages, heads, tuple(own)),...]
where the time goes in v5:
time: 151 us
  Pallas kernels  148 us (98%)
    pallas_call x1, Pallas kernels, whole_layer(): pl.pallas_call(functools.partial(layer_kernel, pages, heads, tuple(own)),...  144 us
    pallas_call x1, Pallas kernels, finish(): pl.pallas_call(functools.partial(finish_kernel, rows, panels), name='fini...  4.06 us

profile of v5, /device:TPU:0, one launch (start us, length us, event | category | flops | bytes accessed | tf_op | source)
XLA Modules:
  0.0 150.6 jit_solution(557084097660763839)
XLA Ops:
  0.7 0.0 copy-start.7
  0.7 0.0 copy-start.8
  0.7 0.0 copy-start.3
  0.7 0.0 copy-start.4
  0.7 0.0 copy-start.5
  0.7 0.0 copy-start.6
  0.7 0.0 copy-start
  0.7 0.0 copy-start.1
  0.7 0.0 copy-start.2
  0.7 0.6 copy-done.7
  1.3 0.0 copy-done.8
  1.3 0.0 copy-done.3
  1.3 0.0 copy-done.4
  1.4 0.0 copy-done.5
  1.4 0.0 copy-done.6
  1.4 0.0 copy-done
  1.4 0.0 copy-done.1
  1.4 0.0 copy-done.2
  1.4 0.6 pad_add_fusion.small
  2.1 144.4 %whole_layer.1 = (bf16[512,768]{1,0:T(8,128)(2,1)}, bf16[512,768]{1,0:T(8,128)(2,1)}, f32[24,768]{1,0:T(8,128)}, f32[24,768]{1,0:T(8,128)}, f32[24,768]{1,0:T(8,...) custom-call(s32[2]{0:T(128)} %lengths.1, bf16[512,768]{1,0:T(8,128)(2,1)} %bitcast.13, ...), custom_call_target="tpu_custom_call" | custom-call | tf_op jit(solution)/shard_map/whole_layer/pallas_call | solution.py:1104
  146.4 4.1 %finish.1 = (bf16[512,768]{1,0:T(8,128)(2,1)}, bf16[512,768]{1,0:T(8,128)(2,1)}, f32[24,768]{1,0:T(8,128)}, f32[24,768]{1,0:T(8,128)}, f32[24,768]{1,0:T(8,128)}...) custom-call(bf16[512,768]{1,0:T(8,128)(2,1)} %get-tuple-element.43.o, ...), custom_call_target="tpu_custom_call" | custom-call | tf_op jit(solution)/shard_map/finish/pallas_call | solution.py:1086
Async XLA Ops:
  0.7 0.7 copy-start.7
  0.7 0.7 copy-start.8
  0.7 0.7 copy-start.3
  0.7 0.7 copy-start.4
  0.7 0.7 copy-start.5
  0.7 0.7 copy-start.6
  0.7 0.7 copy-start
  0.7 0.7 copy-start.1
  0.7 0.7 copy-start.2
